TPU v7x, 32 devices: a whole 2x2x4 slice. The times are simulated.
32 devices in a mesh: dp: 8 (over y, x, core), mp: 4 (over z).
Axes of the slice: x: 2, y: 2, z: 4, core: 2. Of those that a mesh axis runs over, the one named last changes fastest.
Arguments:
- tokens: bfloat16 [12288, 1024], P(('dp', 'mp')), may hold values from -6 to 6
- seg_ids: int32 [8, 1536], P('dp'), may hold values from 0 to 1, as said below
- bucket_of: int32 [128], replicated, may hold values from 0 to 31, as said below
- ln1_gain: float32 [1024], replicated, may hold values from 0.5 to 1.5
- ln1_bias: float32 [1024], replicated, may hold values from -1.2 to 1.2
- w_qkv: bfloat16 [3, 1024, 1024], P(None, None, 'mp'), may hold values from -0.1875 to 0.1875
- rel_table: float32 [32, 16], P(None, 'mp'), may hold values from -4 to 4
- w_out: bfloat16 [1024, 1024], P('mp'), may hold values from -2 to 2
- ln2_gain: float32 [1024], replicated, may hold values from 0.5 to 1.5
- ln2_bias: float32 [1024], replicated, may hold values from -1.2 to 1.2
- w_up: bfloat16 [1024, 4096], P(None, 'mp'), may hold values from -0.1875 to 0.1875
- up_bias: float32 [4096], P('mp'), may hold values from -1.2 to 1.2
- w_down: bfloat16 [4096, 1024], P('mp'), may hold values from -0.09375 to 0.09375
- down_bias: float32 [1024], replicated, may hold values from -1.2 to 1.2
- out_grad: bfloat16 [12288, 1024], P(('dp', 'mp')), may hold values from -6 to 6
Outputs:
- layer_out: bfloat16 [12288, 1024], P(('dp', 'mp'))
- grad_tokens: bfloat16 [12288, 1024], P(('dp', 'mp'))
- grad_ln1_gain: float32 [1024], replicated
- grad_ln1_bias: float32 [1024], replicated
- grad_qkv: float32 [3, 1024, 1024], P(None, None, 'mp')
- grad_table: float32 [32, 16], P(None, 'mp')
- grad_wout: float32 [1024, 1024], P('mp')
- grad_ln2_gain: float32 [1024], replicated
- grad_ln2_bias: float32 [1024], replicated
- grad_up: float32 [1024, 4096], P(None, 'mp')
- grad_up_bias: float32 [4096], P('mp')
- grad_down: float32 [4096, 1024], P('mp')
- grad_down_bias: float32 [1024], replicated
Inputs may be any that keep to these rules, and one draw needn't show every extreme that they name: `seg_ids`: each row holds 2 sequences: ids 0 then 1, never falling; each sequence has 512 to 1024 tokens, and some row has one of exactly 1024 tokens. bucket_of[d] = d for d < 16; beyond, it never falls, rises by at most one from one distance to the next, and its last entry is 31.
All inputs are finite; a program needn't handle non-finite values.
Results may differ from a plain program's by a relative error of at most 0.02.
Values may be sent and summed in bfloat16 or wider, within the bound.
No kernel may reach another device: no remote copies, remote signals or barrier semaphores. Data moves between devices by JAX's collectives and lax.ppermute only.
A program may use at most 192 MiB of HBM per device.

v0:
```python
import jax
import jax.numpy as jnp
from jax import lax
from jax.sharding import PartitionSpec as P

BLOCK = 512


EPSILON = 1e-05
HIGHEST_PRECISION = lax.Precision.HIGHEST
MASKED_SCORE = -1e30


def layer_norm(inputs, norm_gain, norm_bias):
    center = inputs - jnp.mean(inputs, axis=-1, keepdims=True)
    spread = jnp.mean(center * center, axis=-1, keepdims=True)
    return center * lax.rsqrt(spread + EPSILON) * norm_gain + norm_bias


def gelu_exact(inputs):
    return jax.nn.gelu(inputs, approximate=False)


def bucket_tables(bucket_of, n_buckets, block_len):
    dist_limit = bucket_of.shape[0]
    query_pos = jnp.arange(block_len, dtype=jnp.int32)
    diag_index = jnp.clip(query_pos[:, None] - query_pos[None, :], 0, dist_limit - 1)
    prev_index = jnp.clip(query_pos[:, None] + block_len - query_pos[None, :], 0, dist_limit - 1)
    bucket_ids = jnp.arange(n_buckets, dtype=jnp.int32)
    diag_map = bucket_of[diag_index]
    prev_map = bucket_of[prev_index]
    diag_hot = (diag_map[None] == bucket_ids[:, None, None]).astype(jnp.float32)
    prev_hot = (prev_map[None] == bucket_ids[:, None, None]).astype(jnp.float32)
    far_hot = (bucket_of[dist_limit - 1] == bucket_ids).astype(jnp.float32)
    return (diag_hot, prev_hot, far_hot)


def bias_parts(table_part, hot_tables):
    diag_hot, prev_hot, far_hot = hot_tables
    diag_tile = jnp.einsum(
        "ngo,ns->sgo",
        diag_hot,
        table_part,
        precision=HIGHEST_PRECISION,
        preferred_element_type=jnp.float32,
    )
    prev_tile = jnp.einsum(
        "ngo,ns->sgo",
        prev_hot,
        table_part,
        precision=HIGHEST_PRECISION,
        preferred_element_type=jnp.float32,
    )
    far_value = jnp.dot(
        far_hot, table_part, precision=HIGHEST_PRECISION, preferred_element_type=jnp.float32
    )
    return (diag_tile, prev_tile, far_value)


def table_gradient(hot_tables, diag_sum, prev_sum, far_sum):
    diag_hot, prev_hot, far_hot = hot_tables
    from_diag = jnp.einsum(
        "fkm,pkm->fp",
        diag_hot,
        diag_sum,
        precision=HIGHEST_PRECISION,
        preferred_element_type=jnp.float32,
    )
    from_prev = jnp.einsum(
        "fkm,pkm->fp",
        prev_hot,
        prev_sum,
        precision=HIGHEST_PRECISION,
        preferred_element_type=jnp.float32,
    )
    return from_diag + from_prev + far_hot[:, None] * far_sum[None, :]


def block_bias(parts, block_index, block_len):
    diag_tile, prev_tile, far_value = parts
    if block_index == 0:
        return diag_tile
    if block_index == 1:
        return jnp.concatenate([prev_tile, diag_tile], axis=2)
    far_len = (block_index - 1) * block_len
    far_tile = jnp.broadcast_to(far_value[:, None, None], (far_value.shape[0], block_len, far_len))
    return jnp.concatenate([far_tile, prev_tile, diag_tile], axis=2)


def block_scores(queries, keys_all, seg_row, pos_bias, row_start, key_len, score_scale):
    block_len = pos_bias.shape[1]
    row_ids = row_start + jnp.arange(block_len, dtype=jnp.int32)
    key_ids = jnp.arange(key_len, dtype=jnp.int32)
    same_seq = seg_row[row_start : row_start + block_len][:, None] == seg_row[:key_len][None, :]
    allowed = same_seq & (row_ids[:, None] >= key_ids[None, :])
    raw_scores = jnp.einsum(
        "hqd,hkd->hqk",
        queries[:, row_start : row_start + block_len],
        keys_all[:, :key_len],
        preferred_element_type=jnp.float32,
    )
    return jnp.where(allowed[None], raw_scores * score_scale + pos_bias, MASKED_SCORE)


def body(
    tokens,
    seg_ids,
    bucket_of,
    ln1_gain,
    ln1_bias,
    w_qkv,
    rel_table,
    w_out,
    ln2_gain,
    ln2_bias,
    w_up,
    up_bias,
    w_down,
    down_bias,
    out_grad,
):
    seg_row = seg_ids[0]
    group_len = seg_row.shape[0]
    blocks = group_len // BLOCK
    part_rows = tokens.shape[0]
    model_width = tokens.shape[1]
    local_heads = rel_table.shape[1]
    head_size = w_out.shape[0] // local_heads
    score_scale = head_size ** (-0.5)
    qkv_heads = w_qkv.reshape(3, model_width, local_heads, head_size)
    out_heads = w_out.reshape(local_heads, head_size, model_width)
    x_part = tokens.astype(jnp.float32)
    normed = lax.all_gather(
        layer_norm(x_part, ln1_gain, ln1_bias).astype(jnp.bfloat16), "mp", axis=0, tiled=True
    )
    queries, keys_all, values_all = [
        jnp.einsum(
            "tc,chd->htd", normed, qkv_heads[slot_index], preferred_element_type=jnp.float32
        ).astype(jnp.bfloat16)
        for slot_index in range(3)
    ]
    hot_tables = bucket_tables(bucket_of, rel_table.shape[0], BLOCK)
    parts = bias_parts(rel_table, hot_tables)
    pieces_out = []
    log_totals = []
    for block_index in range(blocks):
        row_start = block_index * BLOCK
        key_len = row_start + BLOCK
        pos_bias = block_bias(parts, block_index, BLOCK)
        masked = block_scores(queries, keys_all, seg_row, pos_bias, row_start, key_len, score_scale)
        row_max = jnp.max(masked, axis=-1, keepdims=True)
        log_total = row_max + jnp.log(jnp.sum(jnp.exp(masked - row_max), axis=-1, keepdims=True))
        soft_low = jnp.exp(masked - log_total).astype(jnp.bfloat16)
        pieces_out.append(
            jnp.einsum(
                "hqk,hkd->hqd",
                soft_low,
                values_all[:, :key_len],
                preferred_element_type=jnp.float32,
            ).astype(jnp.bfloat16)
        )
        log_totals.append(log_total)
    attended = jnp.transpose(jnp.concatenate(pieces_out, axis=1), (1, 0, 2)).reshape(
        group_len, local_heads * head_size
    )
    branch = lax.psum_scatter(
        jnp.dot(attended, w_out, preferred_element_type=jnp.float32).astype(jnp.bfloat16),
        "mp",
        scatter_dimension=0,
        tiled=True,
    ).astype(jnp.float32)
    hidden_in = x_part + branch
    second = lax.all_gather(
        layer_norm(hidden_in, ln2_gain, ln2_bias).astype(jnp.bfloat16), "mp", axis=0, tiled=True
    )
    pre_act = jnp.dot(second, w_up, preferred_element_type=jnp.float32) + up_bias
    activated, gelu_pull = jax.vjp(gelu_exact, pre_act)
    activated_low = activated.astype(jnp.bfloat16)
    ff_part = lax.psum_scatter(
        jnp.dot(activated_low, w_down, preferred_element_type=jnp.float32).astype(jnp.bfloat16),
        "mp",
        scatter_dimension=0,
        tiled=True,
    ).astype(jnp.float32)
    layer_out = (hidden_in + ff_part + down_bias).astype(jnp.bfloat16)
    grad_part = out_grad.astype(jnp.float32)
    grad_rows = lax.all_gather(out_grad, "mp", axis=0, tiled=True)
    grad_down = jnp.einsum(
        "tf,td->fd", activated_low, grad_rows, preferred_element_type=jnp.float32
    )
    grad_act = jnp.einsum("td,fd->tf", grad_rows, w_down, preferred_element_type=jnp.float32)
    grad_pre = gelu_pull(grad_act)[0].astype(jnp.bfloat16)
    second_back = lax.all_gather(
        layer_norm(hidden_in, ln2_gain, ln2_bias).astype(jnp.bfloat16), "mp", axis=0, tiled=True
    )
    grad_up = jnp.einsum("td,tf->df", second_back, grad_pre, preferred_element_type=jnp.float32)
    grad_up_bias = jnp.sum(grad_pre, axis=0, dtype=jnp.float32)
    grad_second = lax.psum_scatter(
        jnp.einsum("tf,df->td", grad_pre, w_up, preferred_element_type=jnp.float32).astype(
            jnp.bfloat16
        ),
        "mp",
        scatter_dimension=0,
        tiled=True,
    ).astype(jnp.float32)
    norm2_value, norm2_pull = jax.vjp(layer_norm, hidden_in, ln2_gain, ln2_bias)
    grad_from_norm, grad_ln2_gain, grad_ln2_bias = norm2_pull(grad_second)
    grad_hidden = grad_part + grad_from_norm
    grad_branch = lax.all_gather(grad_hidden.astype(jnp.bfloat16), "mp", axis=0, tiled=True)
    grad_wout = jnp.einsum("tc,td->cd", attended, grad_branch, preferred_element_type=jnp.float32)
    grad_att = jnp.einsum(
        "tc,hdc->htd", grad_branch, out_heads, preferred_element_type=jnp.float32
    ).astype(jnp.bfloat16)
    grad_q_parts = []
    key_pieces = [[] for key_block in range(blocks)]
    value_pieces = [[] for key_block in range(blocks)]
    diag_sum = jnp.zeros(parts[0].shape, jnp.float32)
    prev_sum = jnp.zeros(parts[1].shape, jnp.float32)
    far_sum = jnp.zeros(parts[2].shape, jnp.float32)
    for block_index in range(blocks):
        row_start = block_index * BLOCK
        key_len = row_start + BLOCK
        pos_bias = block_bias(parts, block_index, BLOCK)
        masked = block_scores(queries, keys_all, seg_row, pos_bias, row_start, key_len, score_scale)
        soft = jnp.exp(masked - log_totals[block_index])
        soft_low = soft.astype(jnp.bfloat16)
        grad_block = grad_att[:, row_start:key_len]
        query_block = queries[:, row_start:key_len]
        grad_soft = jnp.einsum(
            "hqd,hkd->hqk", grad_block, values_all[:, :key_len], preferred_element_type=jnp.float32
        )
        inner_sum = jnp.sum(soft * grad_soft, axis=-1, keepdims=True)
        grad_scores = (soft * (grad_soft - inner_sum)).astype(jnp.bfloat16)
        diag_sum = diag_sum + grad_scores[:, :, row_start:key_len].astype(jnp.float32)
        if block_index >= 1:
            prev_sum = prev_sum + grad_scores[:, :, row_start - BLOCK : row_start].astype(
                jnp.float32
            )
        if block_index >= 2:
            far_sum = jnp.sum(
                grad_scores[:, :, : row_start - BLOCK], axis=(1, 2), dtype=jnp.float32
            )
        grad_q_parts.append(
            (
                jnp.einsum(
                    "hqk,hkd->hqd",
                    grad_scores,
                    keys_all[:, :key_len],
                    preferred_element_type=jnp.float32,
                )
                * score_scale
            ).astype(jnp.bfloat16)
        )
        for key_block in range(block_index + 1):
            key_lo = key_block * BLOCK
            key_pieces[key_block].append(
                jnp.einsum(
                    "hqk,hqd->hkd",
                    grad_scores[:, :, key_lo : key_lo + BLOCK],
                    query_block,
                    preferred_element_type=jnp.float32,
                )
            )
            value_pieces[key_block].append(
                jnp.einsum(
                    "hqk,hqd->hkd",
                    soft_low[:, :, key_lo : key_lo + BLOCK],
                    grad_block,
                    preferred_element_type=jnp.float32,
                )
            )
    grad_table = table_gradient(hot_tables, diag_sum, prev_sum, far_sum)
    grad_keys = jnp.concatenate(
        [
            (sum(key_pieces[key_block]) * score_scale).astype(jnp.bfloat16)
            for key_block in range(blocks)
        ],
        axis=1,
    )
    grad_values = jnp.concatenate(
        [sum(value_pieces[key_block]).astype(jnp.bfloat16) for key_block in range(blocks)], axis=1
    )
    grad_proj = [jnp.concatenate(grad_q_parts, axis=1), grad_keys, grad_values]
    normed_back = lax.all_gather(
        layer_norm(x_part, ln1_gain, ln1_bias).astype(jnp.bfloat16), "mp", axis=0, tiled=True
    )
    grad_qkv = jnp.stack(
        [
            jnp.einsum(
                "tc,htd->chd", normed_back, grad_one, preferred_element_type=jnp.float32
            ).reshape(model_width, local_heads * head_size)
            for grad_one in grad_proj
        ]
    )
    running = jnp.zeros((part_rows * lax.axis_size("mp"), model_width), jnp.float32)
    for slot_index in range(3):
        running = running + jnp.einsum(
            "htd,chd->tc",
            grad_proj[slot_index],
            qkv_heads[slot_index],
            preferred_element_type=jnp.float32,
        )
    grad_first = lax.psum_scatter(
        running.astype(jnp.bfloat16), "mp", scatter_dimension=0, tiled=True
    ).astype(jnp.float32)
    norm1_value, norm1_pull = jax.vjp(layer_norm, x_part, ln1_gain, ln1_bias)
    grad_from_first, grad_ln1_gain, grad_ln1_bias = norm1_pull(grad_first)
    grad_tokens = (grad_hidden + grad_from_first).astype(jnp.bfloat16)
    grad_down_bias = jnp.sum(grad_part, axis=0)
    grad_qkv, grad_table, grad_wout, grad_up, grad_up_bias, grad_down = lax.psum(
        (grad_qkv, grad_table, grad_wout, grad_up, grad_up_bias, grad_down), "dp"
    )
    grad_ln1_gain, grad_ln1_bias, grad_ln2_gain, grad_ln2_bias, grad_down_bias = lax.psum(
        (grad_ln1_gain, grad_ln1_bias, grad_ln2_gain, grad_ln2_bias, grad_down_bias), ("dp", "mp")
    )
    return (
        layer_out,
        grad_tokens,
        grad_ln1_gain,
        grad_ln1_bias,
        grad_qkv,
        grad_table,
        grad_wout,
        grad_ln2_gain,
        grad_ln2_bias,
        grad_up,
        grad_up_bias,
        grad_down,
        grad_down_bias,
    )


def solution(mesh):
    return jax.shard_map(
        body,
        mesh=mesh,
        in_specs=(
            P(("dp", "mp"), None),
            P("dp", None),
            P(),
            P(),
            P(),
            P(None, None, "mp"),
            P(None, "mp"),
            P("mp", None),
            P(),
            P(),
            P(None, "mp"),
            P("mp"),
            P("mp", None),
            P(),
            P(("dp", "mp"), None),
        ),
        out_specs=(
            P(("dp", "mp"), None),
            P(("dp", "mp"), None),
            P(),
            P(),
            P(None, None, "mp"),
            P(None, "mp"),
            P("mp", None),
            P(),
            P(),
            P(None, "mp"),
            P("mp"),
            P("mp", None),
            P(),
        ),
        check_vma=False,
    )
```

profile of v0, /device:TPU:0, one launch (start us, length us, event | category | flops | bytes accessed | tf_op | source)
XLA Modules:
  0.0 5097.5 jit_solution(3017814470427177623)
XLA Ops:
  11.4 2.4 fusion.59
  17.8 2679.1 %gather_fusion.1 = s32[262144]{0:T(1024)} fusion(s32[128]{0:T(128)S(1)} %copy-done.1, s32[262144]{0:T(1024)S(1)} %broadcast_clamp_fusion), kind=kCustom, calls=%fused_computation.1 | custom fusion | bytes 3145728 | tf_op jit(solution)/shard_map/gather | solution.py:31
  2696.9 2.3 reshape.387
  2699.2 1556.2 %gather_fusion = s32[262144]{0:T(1024)S(1)} fusion(s32[128]{0:T(128)S(1)} %copy-done.1, s32[262144]{0:T(1024)} %broadcast_clamp_fusion.1), kind=kCustom, calls=%fused_computation | custom fusion | bytes 3145728 | tf_op jit(solution)/shard_map/gather | solution.py:30
  4256.6 12.6 fusion.3
  4269.1 5.3 copy.64
  4274.4 11.5 fusion.1
  4286.0 5.4 copy.68
  4295.9 3.2 fusion.131
  4301.7 2.5 copy-done.9
  4309.1 2.1 fusion.181
  4311.2 2.9 broadcast_in_dim.63
  4314.2 10.5 fusion.180
  4324.7 6.2 exponential_reduce_fusion
  4337.1 9.1 fusion.9
  4346.2 4.0 convolution_convert_fusion.3
  4351.2 2.7 convolution_convert_fusion
  4353.9 63.1 %reduce-scatter.5.cloned.1.call-done = bf16[384,1024]{1,0:T(8,128)(2,1)} async-done(((bf16[1536,1024]{1,0:T(8,128)(2,1)}), bf16[384,1024]{1,0:T(8,128)(2,1)}) %reduce-scatter.5.cloned.1.call-update) | async-done | bytes 786448 | tf_op jit(solution)/shard_map/reduce_scatter | solution.py:166
  4420.0 2.4 add_convert_fusion.3
  4423.5 62.6 %all-gather.7.cloned.1.call-done = bf16[1536,1024]{1,0:T(8,128)(2,1)} async-done(((bf16[384,1024]{1,0:T(8,128)(2,1)}), bf16[1536,1024]{1,0:T(8,128)(2,1)}) %all-gather.7.cloned.1.call-update) | async-done | bytes 3145744 | tf_op jit(solution)/shard_map/all_gather | solution.py:173
  4486.1 8.6 fusion.183
  4494.7 55.0 %all-gather.9.cloned.1.call-done = bf16[1536,1024]{1,0:T(8,128)(2,1)} async-done(((bf16[384,1024]{1,0:T(8,128)(2,1)}), bf16[1536,1024]{1,0:T(8,128)(2,1)}) %all-gather.9.cloned.1.call-update) | async-done | bytes 3145744 | tf_op jit(solution)/shard_map/all_gather | solution.py:187
  4549.7 20.8 convert_reduce_fusion
  4570.6 1.7 copy-done.79
  4572.2 4.9 convolution_convert_fusion.1
  4577.4 6.4 multiply_convert_fusion.2
  4585.4 4.7 convolution_convert_fusion.2
  4590.3 46.0 reduce-scatter.9.cloned.1.call-done
  4636.2 2.1 fusion.63
  4638.4 60.9 %reduce-scatter.7.cloned.1.call-done = bf16[384,1024]{1,0:T(8,128)(2,1)} async-done(((bf16[1536,1024]{1,0:T(8,128)(2,1)}), bf16[384,1024]{1,0:T(8,128)(2,1)}) %reduce-scatter.7.cloned.1.call-update) | async-done | bytes 786448 | tf_op jit(solution)/shard_map/reduce_scatter | solution.py:179
  4699.3 3.4 fusion.177
  4705.1 2.3 fusion.178
  4707.3 2.1 copy.65
  4711.4 57.3 %all-gather.11.cloned.1.call-done = bf16[1536,1024]{1,0:T(8,128)(2,1)} async-done(((bf16[384,1024]{1,0:T(8,128)(2,1)}), bf16[1536,1024]{1,0:T(8,128)(2,1)}) %all-gather.11.cloned.1.call-update) | async-done | bytes 3145744 | tf_op jit(solution)/shard_map/all_gather | solution.py:209
  4768.7 3.0 fusion.26
  4771.7 3.4 fusion.104
  4775.1 3.3 fusion.39
  4778.4 3.2 fusion.35
  4783.3 3.0 multiply_reduce_fusion.2
  4786.3 4.9 multiply_reduce_fusion.1
  4791.8 8.2 multiply_reduce_fusion
  4799.9 9.7 multiply_convert_fusion
  4809.6 2.3 fusion.111
  4812.0 4.1 fusion.103
  4819.8 4.6 multiply_convert_fusion.1
  4826.6 4.8 convert_add_fusion.1
  4839.5 2.7 fusion.13
  4842.3 8.4 fusion.186
  4850.7 5.6 fusion.185
  4862.4 1.8 pad_maximum_fusion
  4865.7 2.1 fusion.184
  4868.4 5.5 copy.94
  4873.9 5.5 copy.95
  4879.4 17.9 fusion.115
  4897.4 16.1 fusion.118
  4913.5 15.5 all-reduce.1
  4929.1 1.8 convert_reduce_fusion.2
  4930.9 2.0 fusion.64
  4932.9 3.1 convert_reduce_fusion.5
  4936.1 38.9 all-reduce
  4975.0 105.1 %all-reduce.5.cloned.1.call-done = (f32[3,1024,256]{2,1,0:T(8,128)}, f32[256,1024]{1,0:T(8,128)}, f32[1024,1024]{1,0:T(8,128)}, f32[1024,1024]{1,0:T(8,128)}) async-done(((f32[3,1024,256]{2,1,0:T(8,128)}, f32[256,1024]{1,0:T(8,128)}, f32[1024,1024]{1,0:T(8,128)}, f32[1024,1024]{1,0:T(8,128)}), (f32[3,1024,256]{2,1,0:T(8,128)}, f32[256,1024]{1,0:T(8,128)}, f32[1024,1024]{1,0:T(8,128)}, ...) | async-done | bytes 12582928 | tf_op jit(solution)/shard_map/psum | solution.py:310
  5080.1 3.9 copy.124
  5085.0 2.1 copy.126
  5088.7 2.0 copy.127
  (259 shorter events, 65.3 us)
Async XLA Ops:
  7.2 4542.5 %copy-start = (bf16[1024,1024]{1,0:T(8,128)(2,1)S(1)}, bf16[1024,1024]{1,0:T(8,128)(2,1)}, u32[]{:S(2)}) copy-start(bf16[1024,1024]{1,0:T(8,128)(2,1)} %param.27) | copy-start | bytes 6291460
  7.2 4288.7 %all-gather.5.cloned.1.call-start = ((), (), s32[]{:S(2)}) async-start(), calls=%async_computation.4 | async-start | bytes 3932160 | tf_op jit(solution)/shard_map/all_gather | solution.py:133
  13.8 4403.2 %reduce-scatter.5.cloned.1.call-start = ((), (), s32[]{:S(2)}) async-start(), calls=%async_computation.5 | async-start | bytes 3932160 | tf_op jit(solution)/shard_map/reduce_scatter | solution.py:166
  2699.2 1557.3 %copy-start.69 = (f32[32,4]{0,1:T(4,128)S(1)}, f32[32,4]{0,1:T(4,128)}, u32[]{:S(2)}) copy-start(f32[32,4]{0,1:T(4,128)} %param.21) | copy-start | bytes 1540
  4269.1 5.3 copy-start.36
  4286.0 6.2 copy-start.57
  4286.0 7.1 slice-start.5
  4286.0 7.1 copy-start.63
  4286.0 8.4 copy-start.61
  4295.9 3.5 copy-start.70
  4299.4 46.8 copy-start.12
  4301.7 12.5 copy-start.16
  4301.7 12.5 copy-start.26
  4304.3 3.3 copy-start.31
  4305.4 3.7 copy-start.15
  4311.2 20.9 copy-start.2
  4346.2 5.0 copy-start.43
  4351.2 65.8 %copy-start.6 = (bf16[384,1024]{1,0:T(8,128)(2,1)S(1)}, bf16[384,1024]{1,0:T(8,128)(2,1)}, u32[]{:S(2)}) copy-start(bf16[384,1024]{1,0:T(8,128)(2,1)} %param.15) | copy-start | bytes 2359300
  4353.9 66.1 %copy-start.58 = (f32[1024]{0:T(1024)S(1)}, f32[1024]{0:T(1024)}, u32[]{:S(2)}) copy-start(f32[1024]{0:T(1024)} %param.23) | copy-start | bytes 12292
  4353.9 66.1 %copy-start.66 = (f32[1024]{0:T(1024)S(1)}, f32[1024]{0:T(1024)}, u32[]{:S(2)}) copy-start(f32[1024]{0:T(1024)} %param.24) | copy-start | bytes 12292
  4353.9 132.2 %all-gather.7.cloned.1.call-start = ((), (), s32[]{:S(2)}) async-start(), calls=%async_computation.6 | async-start | bytes 3932160 | tf_op jit(solution)/shard_map/all_gather | solution.py:173
  4422.4 127.3 %all-gather.9.cloned.1.call-start = ((), (), s32[]{:S(2)}) async-start(), calls=%async_computation.8 | async-start | bytes 3932160 | tf_op jit(solution)/shard_map/all_gather | solution.py:187
  4423.0 126.7 %copy-start.67 = (f32[1024]{0:T(1024)S(1)}, f32[1024]{0:T(1024)}, u32[]{:S(2)}) copy-start(f32[1024]{0:T(1024)} %param.26) | copy-start | bytes 12292
  4423.0 213.2 %reduce-scatter.9.cloned.1.call-start = ((), (), s32[]{:S(2)}) async-start(), calls=%async_computation.9 | async-start | bytes 3932160 | tf_op jit(solution)/shard_map/reduce_scatter | solution.py:198
  4549.7 22.5 copy-start.74
  4577.2 122.1 %reduce-scatter.7.cloned.1.call-start = ((), (), s32[]{:S(2)}) async-start(), calls=%async_computation.7 | async-start | bytes 3932160 | tf_op jit(solution)/shard_map/reduce_scatter | solution.py:179
  4590.2 109.1 %copy-start.68 = (f32[1024]{0:T(1024)S(1)}, f32[1024]{0:T(1024)}, u32[]{:S(2)}) copy-start(f32[1024]{0:T(1024)} %param.28) | copy-start | bytes 12292
  4590.2 178.5 %all-gather.11.cloned.1.call-start = ((), (), s32[]{:S(2)}) async-start(), calls=%async_computation.10 | async-start | bytes 3932160 | tf_op jit(solution)/shard_map/all_gather | solution.py:209
  4699.3 4.6 copy-start.20
  4705.0 224.0 %reduce-scatter.11.cloned.1.call-start = ((), (), s32[]{:S(2)}) async-start(), calls=%async_computation.11 | async-start | bytes 3932160 | tf_op jit(solution)/shard_map/reduce_scatter | solution.py:303
  4771.7 14.5 copy-start.33
  4771.7 9.9 copy-start.5
  4775.1 11.2 slice-start
  4778.4 4.8 copy-start.13
  4781.7 4.6 slice-start.1
  4783.2 8.0 slice-start.2
  4783.3 8.0 slice-start.3
  4786.3 5.5 slice-start.4
  4799.9 9.7 copy-start.27
  4799.9 12.0 copy-start.17
  4812.0 26.3 copy-start.47
  4812.0 4.7 copy-start.8
  4826.6 6.4 copy-start.28
  4831.4 3.4 copy-start.78
  4833.0 4.2 copy-start.40
  4842.2 237.9 %all-reduce.5.cloned.1.call-start = ((), (), s32[]{:S(2)}) async-start(), calls=%async_computation.12 | async-start | bytes 25165824 | tf_op jit(solution)/shard_map/psum | solution.py:310
  4842.3 8.5 copy-start.72
  4842.3 8.4 copy-start.80
  4850.7 5.7 copy-start.48
  4850.7 5.7 copy-start.50
  4850.7 5.7 copy-start.52
  4850.7 5.8 copy-start.41
  4873.9 5.5 copy-start.38
  4879.4 17.9 copy-start.25
  4879.4 17.9 copy-start.37
  4897.4 31.7 copy-start.7
  4897.4 31.7 copy-start.54
  4897.4 31.7 copy-start.55
  4897.4 33.5 copy-start.65
  4897.4 33.5 copy-start.60
  4929.1 3.9 copy-start.19
  5080.1 3.9 copy-start.39
  5080.1 4.9 copy-start.24
  5085.0 3.7 copy-start.23
  (32 other events, 58.5 us)
Sparse Core Ops, SparseCore 0:
  13.9 66.1 all-gather.4
  4354.0 62.9 reduce-scatter.4
  4422.6 63.4 all-gather.6
  4487.5 62.1 all-gather.8
  4577.3 58.8 reduce-scatter.8
  4639.0 60.2 reduce-scatter.6
  4705.1 63.5 all-gather.10
  4842.3 58.8 reduce-scatter.10
  4905.3 174.8 all-reduce.4
where the time goes:
time: 5110 us; the launch traced here: 5100 us
  local copies, waits for them, and re-layouts  4300 us (84%)
  waiting for transfers between devices  451 us (9%)
  matrix products  196 us (4%)
  other arithmetic  77.2 us (2%)
  blocking collectives  54.4 us (1%)
    gather x2, local copies, waits for them, and re-layouts, bucket_tables(): prev_map = bucket_of[prev_index]  2680 us
    gather x2, local copies, waits for them, and re-layouts, bucket_tables(): diag_map = bucket_of[diag_index]  1560 us
    psum x1, waiting for transfers between devices, body(): lax.psum((grad_qkv, grad_table, grad_wout, grad_up, grad_up_bias, grad_do...  105 us
  transfers between devices with their start and end apart: 9, of which 7 were waited for; matrix products, arithmetic and copies ran while one was open for 86% of the time, Pallas kernels for 0%

commit v1 on v0

v1 whole, which is shorter than its diff:
```python
import jax
import jax.numpy as jnp
from jax import lax
from jax.experimental import pallas as pl
from jax.experimental.pallas import tpu as pltpu
from jax.sharding import PartitionSpec as P


EPSILON = 1e-05
HIGHEST_PRECISION = lax.Precision.HIGHEST


def layer_norm(inputs, norm_gain, norm_bias):
    center = inputs - jnp.mean(inputs, axis=-1, keepdims=True)
    spread = jnp.mean(center * center, axis=-1, keepdims=True)
    return center * lax.rsqrt(spread + EPSILON) * norm_gain + norm_bias


def gelu_exact(inputs):
    return jax.nn.gelu(inputs, approximate=False)


BLK = 256
HEAD_LANES = 64
NEAR = 128


def head_mask(rows, width, head, axis):
    place = lax.broadcasted_iota(jnp.int32, (rows, width), axis)
    return (place >= head * HEAD_LANES) & (place < (head + 1) * HEAD_LANES)


def one_head(value, head):
    keep = head_mask(value.shape[0], value.shape[1], head, 1)
    return jnp.where(keep, value, jnp.zeros_like(value))


def dot_nt(left, right):
    return lax.dot_general(
        left, right, (((1,), (1,)), ((), ())), preferred_element_type=jnp.float32
    )


def dot_nn(left, right):
    return lax.dot_general(
        left, right, (((1,), (0,)), ((), ())), preferred_element_type=jnp.float32
    )


def attention_forward_kernel(
    cut_ref, q_ref, k_ref, v_ref, bias_ref, out_ref, lse_ref, tile_ref, masked_v, score_ref
):
    heads = masked_v.shape[0]
    block = pl.program_id(0)
    cut = cut_ref[0]

    @pl.when(block == 0)
    def _():
        for head in range(heads):
            wide = jnp.broadcast_to(bias_ref[head : head + 1, :], (BLK, 2 * BLK))
            tile_ref[head] = pltpu.roll(wide, 0, 1, stride=1, stride_axis=0)
            masked_v[head] = one_head(v_ref[...], head)

    row_start = block * BLK
    first = jnp.where(row_start >= cut, cut // BLK, 0)
    rows = row_start + lax.broadcasted_iota(jnp.int32, (BLK, BLK), 0)
    seg_start = jnp.where(rows >= cut, cut, 0)
    columns = lax.broadcasted_iota(jnp.int32, (BLK, BLK), 1)
    q_block = q_ref[...]
    q_heads = [one_head(q_block, head) for head in range(heads)]

    def scores_of(key_block, tops):
        key_start = pl.multiple_of(key_block * BLK, BLK)
        keys = k_ref[pl.ds(key_start, BLK), :]
        places = key_start + columns
        allowed = (places <= rows) & (places >= seg_start)
        offset = pl.multiple_of(jnp.maximum(key_block - block + 1, 0) * BLK, BLK)
        near = key_block - block + 1 >= 0
        new_tops = []
        for head in range(heads):
            raw = dot_nt(q_heads[head], keys)
            far = bias_ref[head : head + 1, 2 * BLK - 1 : 2 * BLK]
            bias = jnp.where(near, tile_ref[head, :, pl.ds(offset, BLK)], far)
            scores = jnp.where(allowed, raw + bias, -1e30)
            score_ref[head, :, pl.ds(key_start, BLK)] = scores
            top = tops[head]
            for lane in range(0, BLK, 128):
                top = jnp.maximum(top, scores[:, lane : lane + 128])
            new_tops.append(top)
        return tuple(new_tops)

    start = tuple(jnp.full((BLK, 128), -1e30, jnp.float32) for _ in range(heads))
    tops = lax.fori_loop(first, block + 1, scores_of, start)
    tops = [jnp.max(top, axis=1, keepdims=True) for top in tops]

    def weighted(key_block, carry):
        total, sums = carry
        key_start = pl.multiple_of(key_block * BLK, BLK)
        new_sums = []
        pieces = []
        values = []
        for head in range(heads):
            soft = jnp.exp(score_ref[head, :, pl.ds(key_start, BLK)] - tops[head])
            part = sums[head]
            for lane in range(0, BLK, 128):
                part = part + soft[:, lane : lane + 128]
            new_sums.append(part)
            pieces.append(soft.astype(jnp.bfloat16))
            values.append(masked_v[head, pl.ds(key_start, BLK), :])
        total = total + dot_nn(
            jnp.concatenate(pieces, axis=1), jnp.concatenate(values, axis=0)
        )
        return total, tuple(new_sums)

    total, sums = lax.fori_loop(
        first,
        block + 1,
        weighted,
        (
            jnp.zeros((BLK, heads * HEAD_LANES), jnp.float32),
            tuple(jnp.zeros((BLK, 128), jnp.float32) for _ in range(heads)),
        ),
    )
    lanes = lax.broadcasted_iota(jnp.int32, (BLK, heads * HEAD_LANES), 1)
    narrow = lax.broadcasted_iota(jnp.int32, (BLK, 128), 1)
    scale = jnp.zeros((BLK, heads * HEAD_LANES), jnp.float32)
    logs = jnp.zeros((BLK, 128), jnp.float32)
    for head in range(heads):
        sum_one = jnp.sum(sums[head], axis=1, keepdims=True)
        scale = jnp.where(lanes // HEAD_LANES == head, 1.0 / sum_one, scale)
        logs = jnp.where(narrow == head, tops[head] + jnp.log(sum_one), logs)
    out_ref[...] = (total * scale).astype(jnp.bfloat16)
    lse_ref[...] = jnp.transpose(logs)[0:8, :]


def attention_forward(cut, queries, keys, values, near_bias):
    length, width = queries.shape
    heads = width // HEAD_LANES
    whole = lambda block, cut: (0, 0)
    return pl.pallas_call(
        attention_forward_kernel,
        grid_spec=pltpu.PrefetchScalarGridSpec(
            num_scalar_prefetch=1,
            grid=(length // BLK,),
            in_specs=[
                pl.BlockSpec((BLK, width), lambda block, cut: (block, 0)),
                pl.BlockSpec((length, width), whole),
                pl.BlockSpec((length, width), whole),
                pl.BlockSpec((8, 2 * BLK), whole),
            ],
            out_specs=[
                pl.BlockSpec((BLK, width), lambda block, cut: (block, 0)),
                pl.BlockSpec((8, BLK), lambda block, cut: (0, block)),
            ],
            scratch_shapes=[
                pltpu.VMEM((heads, BLK, 2 * BLK), jnp.float32),
                pltpu.VMEM((heads, length, width), jnp.bfloat16),
                pltpu.VMEM((heads, BLK, length), jnp.float32),
            ],
        ),
        out_shape=[
            jax.ShapeDtypeStruct((length, width), jnp.bfloat16),
            jax.ShapeDtypeStruct((8, length), jnp.float32),
        ],
        compiler_params=pltpu.CompilerParams(
            dimension_semantics=("arbitrary",), vmem_limit_bytes=48 * 1024 * 1024
        ),
        cost_estimate=pl.CostEstimate(
            flops=8 * length * length * width, bytes_accessed=8 * length * width,
            transcendentals=heads * length * length // 2,
        ),
        name="attention_forward",
    )(cut, queries, keys, values, near_bias)


def attention_backward_kernel(
    cut_ref, q_ref, k_ref, v_ref, grad_ref, att_ref, lse_ref, bias_ref,
    dq_ref, dk_ref, dv_ref, table_ref,
    tile_ref, q_masked, grad_masked, delta_ref, dq_sum, near_sum, far_sum,
):
    heads = q_masked.shape[0]
    block = pl.program_id(0)
    n_blocks = pl.num_programs(0)
    length, width = q_ref.shape
    cut = cut_ref[0]

    @pl.when(block == 0)
    def _():
        product = grad_ref[...].astype(jnp.float32) * att_ref[...].astype(jnp.float32)
        high = product.astype(jnp.bfloat16)
        rest = (product - high.astype(jnp.float32)).astype(jnp.bfloat16)
        row = lax.broadcasted_iota(jnp.int32, (16, width), 0)
        lane = lax.broadcasted_iota(jnp.int32, (16, width), 1)
        pick = jnp.where(lane // HEAD_LANES == row, 1.0, 0.0).astype(jnp.bfloat16)
        delta_ref[...] = (dot_nt(pick, high) + dot_nt(pick, rest))[0:8, :]
        for head in range(heads):
            wide = jnp.broadcast_to(bias_ref[head : head + 1, :], (BLK, 2 * BLK))
            tile_ref[head] = pltpu.roll(wide, 0, 1, stride=1, stride_axis=0)
            q_masked[head] = one_head(q_ref[...], head)
            grad_masked[head] = one_head(grad_ref[...], head)
        dq_sum[...] = jnp.zeros_like(dq_sum)
        near_sum[...] = jnp.zeros_like(near_sum)
        far_sum[...] = jnp.zeros_like(far_sum)

    key_start = pl.multiple_of(block * BLK, BLK)
    keys = k_ref[pl.ds(key_start, BLK), :]
    values = v_ref[pl.ds(key_start, BLK), :]
    keys_t = jnp.transpose(keys)
    places = key_start + lax.broadcasted_iota(jnp.int32, (BLK, BLK), 0)
    columns = lax.broadcasted_iota(jnp.int32, (BLK, BLK), 1)
    last = jnp.where(key_start + BLK <= cut, (cut + BLK - 1) // BLK, n_blocks)

    def one_block(query_block, carry):
        dk, dv = carry
        row_start = pl.multiple_of(query_block * BLK, BLK)
        rows = row_start + columns
        allowed = (places <= rows) & (places >= jnp.where(rows >= cut, cut, 0))
        distance = query_block - block
        near = distance <= 1
        offset = pl.multiple_of(jnp.minimum(distance, 1) * BLK, BLK)
        soft_pieces, grad_pieces, q_pieces, out_pieces = [], [], [], []
        for head in range(heads):
            q_head = q_masked[head, pl.ds(row_start, BLK), :]
            grad_head = grad_masked[head, pl.ds(row_start, BLK), :]
            far = bias_ref[head : head + 1, BLK - 1 : BLK]
            bias = jnp.where(near, tile_ref[head, :, pl.ds(offset, BLK)], far)
            scores = dot_nt(keys, q_head) + bias
            log_total = lse_ref[head : head + 1, pl.ds(row_start, BLK)]
            soft = jnp.exp(jnp.where(allowed, scores - log_total, -1e30))
            grad_soft = dot_nt(values, grad_head)
            delta = delta_ref[head : head + 1, pl.ds(row_start, BLK)]
            grad_scores = soft * (grad_soft - delta)
            grad_low = grad_scores.astype(jnp.bfloat16)

            @pl.when(near)
            def _():
                near_sum[head, :, pl.ds(offset, BLK)] += grad_scores

            @pl.when(jnp.logical_not(near))
            def _():
                far_sum[head] += jnp.sum(
                    grad_scores.reshape(BLK // 8, 8, BLK), axis=0
                )

            spot = slice(head * HEAD_LANES, (head + 1) * HEAD_LANES)
            dq_sum[spot, pl.ds(row_start, BLK)] += dot_nn(keys_t[spot, :], grad_low)
            soft_pieces.append(soft.astype(jnp.bfloat16))
            grad_pieces.append(grad_low)
            q_pieces.append(q_head)
            out_pieces.append(grad_head)
        dv = dv + dot_nn(
            jnp.concatenate(soft_pieces, axis=1), jnp.concatenate(out_pieces, axis=0)
        )
        dk = dk + dot_nn(
            jnp.concatenate(grad_pieces, axis=1), jnp.concatenate(q_pieces, axis=0)
        )
        return dk, dv

    empty = jnp.zeros((BLK, width), jnp.float32)
    dk, dv = lax.fori_loop(block, last, one_block, (empty, empty))
    dk_ref[...] = dk.astype(jnp.bfloat16)
    dv_ref[...] = dv.astype(jnp.bfloat16)

    @pl.when(block == n_blocks - 1)
    def _():
        for query_block in range(length // BLK):
            spot = slice(query_block * BLK, (query_block + 1) * BLK)
            dq_ref[spot, :] = (
                jnp.transpose(dq_sum[:, spot]) * (HEAD_LANES ** -0.5)
            ).astype(jnp.bfloat16)
        for head in range(heads):
            lined = jnp.zeros((8, 2 * BLK), jnp.float32)
            for group in range(BLK // 8):
                piece = near_sum[head, group * 8 : group * 8 + 8, :]
                shift = (2 * BLK - group * 8) % (2 * BLK)
                lined = lined + (pltpu.roll(piece, shift, 1) if shift else piece)
            total = lined[0:1, :]
            for row in range(1, 8):
                total = total + pltpu.roll(lined, 2 * BLK - row, 1)[row : row + 1, :]
            table_ref[head : head + 1, :] = total
            rest = jnp.sum(far_sum[head], axis=0, keepdims=True)
            table_ref[heads + head : heads + head + 1, :] = jnp.concatenate(
                [rest, jnp.zeros_like(rest)], axis=1
            )


def attention_backward(cut, queries, keys, values, grad_att, attended, logs, near_bias):
    length, width = queries.shape
    heads = width // HEAD_LANES
    whole = lambda block, cut: (0, 0)
    full = pl.BlockSpec((length, width), whole)
    return pl.pallas_call(
        attention_backward_kernel,
        grid_spec=pltpu.PrefetchScalarGridSpec(
            num_scalar_prefetch=1,
            grid=(length // BLK,),
            in_specs=[
                full, full, full, full, full,
                pl.BlockSpec((8, length), whole),
                pl.BlockSpec((8, 2 * BLK), whole),
            ],
            out_specs=[
                full,
                pl.BlockSpec((BLK, width), lambda block, cut: (block, 0)),
                pl.BlockSpec((BLK, width), lambda block, cut: (block, 0)),
                pl.BlockSpec((8, 2 * BLK), whole),
            ],
            scratch_shapes=[
                pltpu.VMEM((heads, BLK, 2 * BLK), jnp.float32),
                pltpu.VMEM((heads, length, width), jnp.bfloat16),
                pltpu.VMEM((heads, length, width), jnp.bfloat16),
                pltpu.VMEM((8, length), jnp.float32),
                pltpu.VMEM((width, length), jnp.float32),
                pltpu.VMEM((heads, BLK, 2 * BLK), jnp.float32),
                pltpu.VMEM((heads, 8, BLK), jnp.float32),
            ],
        ),
        out_shape=[
            jax.ShapeDtypeStruct((length, width), jnp.bfloat16),
            jax.ShapeDtypeStruct((length, width), jnp.bfloat16),
            jax.ShapeDtypeStruct((length, width), jnp.bfloat16),
            jax.ShapeDtypeStruct((8, 2 * BLK), jnp.float32),
        ],
        compiler_params=pltpu.CompilerParams(
            dimension_semantics=("arbitrary",), vmem_limit_bytes=56 * 1024 * 1024
        ),
        cost_estimate=pl.CostEstimate(
            flops=20 * length * length * width, bytes_accessed=16 * length * width,
            transcendentals=heads * length * length // 2,
        ),
        name="attention_backward",
    )(cut, queries, keys, values, grad_att, attended, logs, near_bias)


def distance_bias(rel_table, bucket_of):
    hot = (
        bucket_of[:, None] == jnp.arange(rel_table.shape[0], dtype=jnp.int32)[None, :]
    ).astype(jnp.float32)
    by_distance = jnp.einsum(
        "dn,nh->hd", hot, rel_table, precision=HIGHEST_PRECISION,
        preferred_element_type=jnp.float32,
    )
    return hot, by_distance


def near_tables(by_distance):
    heads, reach = by_distance.shape
    far = by_distance[:, reach - 1 :]
    forward = jnp.concatenate(
        [
            jnp.broadcast_to(far, (heads, BLK - reach + 1)),
            by_distance[:, ::-1],
            jnp.broadcast_to(far, (heads, BLK - 1)),
        ],
        axis=1,
    )
    backward = jnp.concatenate(
        [by_distance, jnp.broadcast_to(far, (heads, 2 * BLK - reach))], axis=1
    )
    rows = ((0, 8 - heads), (0, 0))
    return jnp.pad(forward, rows), jnp.pad(backward, rows)


def table_gradient(hot, table_sums, heads):
    reach = hot.shape[0]
    near = table_sums[:heads, : reach - 1]
    far = jnp.sum(table_sums[:heads, reach - 1 :], axis=1) + jnp.sum(
        table_sums[heads : 2 * heads], axis=1
    )
    by_distance = jnp.concatenate([near, far[:, None]], axis=1)
    return jnp.einsum(
        "dn,hd->nh", hot, by_distance, precision=HIGHEST_PRECISION,
        preferred_element_type=jnp.float32,
    )


def body(
    tokens,
    seg_ids,
    bucket_of,
    ln1_gain,
    ln1_bias,
    w_qkv,
    rel_table,
    w_out,
    ln2_gain,
    ln2_bias,
    w_up,
    up_bias,
    w_down,
    down_bias,
    out_grad,
):
    seg_row = seg_ids[0]
    group_len = seg_row.shape[0]
    part_rows = tokens.shape[0]
    model_width = tokens.shape[1]
    local_heads = rel_table.shape[1]
    head_size = w_out.shape[0] // local_heads
    score_scale = head_size ** (-0.5)
    x_part = tokens.astype(jnp.float32)
    normed = lax.all_gather(
        layer_norm(x_part, ln1_gain, ln1_bias).astype(jnp.bfloat16), "mp", axis=0, tiled=True
    )
    queries, keys_all, values_all = [
        jnp.dot(normed, w_qkv[slot_index], preferred_element_type=jnp.float32).astype(jnp.bfloat16)
        for slot_index in range(3)
    ]
    queries = queries * jnp.asarray(score_scale, jnp.bfloat16)
    hot, by_distance = distance_bias(rel_table, bucket_of)
    forward_bias, backward_bias = near_tables(by_distance)
    cut = jnp.sum((seg_row == seg_row[0]).astype(jnp.int32)).reshape(1)
    attended, logs = attention_forward(cut, queries, keys_all, values_all, forward_bias)
    branch = lax.psum_scatter(
        jnp.dot(attended, w_out, preferred_element_type=jnp.float32).astype(jnp.bfloat16),
        "mp",
        scatter_dimension=0,
        tiled=True,
    ).astype(jnp.float32)
    hidden_in = x_part + branch
    second = lax.all_gather(
        layer_norm(hidden_in, ln2_gain, ln2_bias).astype(jnp.bfloat16), "mp", axis=0, tiled=True
    )
    pre_act = jnp.dot(second, w_up, preferred_element_type=jnp.float32) + up_bias
    activated, gelu_pull = jax.vjp(gelu_exact, pre_act)
    activated_low = activated.astype(jnp.bfloat16)
    ff_part = lax.psum_scatter(
        jnp.dot(activated_low, w_down, preferred_element_type=jnp.float32).astype(jnp.bfloat16),
        "mp",
        scatter_dimension=0,
        tiled=True,
    ).astype(jnp.float32)
    layer_out = (hidden_in + ff_part + down_bias).astype(jnp.bfloat16)
    grad_part = out_grad.astype(jnp.float32)
    grad_rows = lax.all_gather(out_grad, "mp", axis=0, tiled=True)
    grad_down = jnp.einsum(
        "tf,td->fd", activated_low, grad_rows, preferred_element_type=jnp.float32
    )
    grad_act = jnp.einsum("td,fd->tf", grad_rows, w_down, preferred_element_type=jnp.float32)
    grad_pre = gelu_pull(grad_act)[0].astype(jnp.bfloat16)
    second_back = lax.all_gather(
        layer_norm(hidden_in, ln2_gain, ln2_bias).astype(jnp.bfloat16), "mp", axis=0, tiled=True
    )
    grad_up = jnp.einsum("td,tf->df", second_back, grad_pre, preferred_element_type=jnp.float32)
    grad_up_bias = jnp.sum(grad_pre, axis=0, dtype=jnp.float32)
    grad_second = lax.psum_scatter(
        jnp.einsum("tf,df->td", grad_pre, w_up, preferred_element_type=jnp.float32).astype(
            jnp.bfloat16
        ),
        "mp",
        scatter_dimension=0,
        tiled=True,
    ).astype(jnp.float32)
    norm2_value, norm2_pull = jax.vjp(layer_norm, hidden_in, ln2_gain, ln2_bias)
    grad_from_norm, grad_ln2_gain, grad_ln2_bias = norm2_pull(grad_second)
    grad_hidden = grad_part + grad_from_norm
    grad_branch = lax.all_gather(grad_hidden.astype(jnp.bfloat16), "mp", axis=0, tiled=True)
    grad_wout = jnp.einsum("tc,td->cd", attended, grad_branch, preferred_element_type=jnp.float32)
    grad_att = jnp.einsum(
        "td,cd->tc", grad_branch, w_out, preferred_element_type=jnp.float32
    ).astype(jnp.bfloat16)
    grad_queries, grad_keys, grad_values, table_sums = attention_backward(
        cut, queries, keys_all, values_all, grad_att, attended, logs, backward_bias
    )
    grad_table = table_gradient(hot, table_sums, local_heads)
    grad_proj = [grad_queries, grad_keys, grad_values]
    normed_back = lax.all_gather(
        layer_norm(x_part, ln1_gain, ln1_bias).astype(jnp.bfloat16), "mp", axis=0, tiled=True
    )
    grad_qkv = jnp.stack(
        [
            jnp.einsum("tc,td->cd", normed_back, grad_one, preferred_element_type=jnp.float32)
            for grad_one in grad_proj
        ]
    )
    running = jnp.zeros((part_rows * lax.axis_size("mp"), model_width), jnp.float32)
    for slot_index in range(3):
        running = running + jnp.einsum(
            "td,cd->tc",
            grad_proj[slot_index],
            w_qkv[slot_index],
            preferred_element_type=jnp.float32,
        )
    grad_first = lax.psum_scatter(
        running.astype(jnp.bfloat16), "mp", scatter_dimension=0, tiled=True
    ).astype(jnp.float32)
    norm1_value, norm1_pull = jax.vjp(layer_norm, x_part, ln1_gain, ln1_bias)
    grad_from_first, grad_ln1_gain, grad_ln1_bias = norm1_pull(grad_first)
    grad_tokens = (grad_hidden + grad_from_first).astype(jnp.bfloat16)
    grad_down_bias = jnp.sum(grad_part, axis=0)
    grad_qkv, grad_table, grad_wout, grad_up, grad_up_bias, grad_down = lax.psum(
        (grad_qkv, grad_table, grad_wout, grad_up, grad_up_bias, grad_down), "dp"
    )
    grad_ln1_gain, grad_ln1_bias, grad_ln2_gain, grad_ln2_bias, grad_down_bias = lax.psum(
        (grad_ln1_gain, grad_ln1_bias, grad_ln2_gain, grad_ln2_bias, grad_down_bias), ("dp", "mp")
    )
    return (
        layer_out,
        grad_tokens,
        grad_ln1_gain,
        grad_ln1_bias,
        grad_qkv,
        grad_table,
        grad_wout,
        grad_ln2_gain,
        grad_ln2_bias,
        grad_up,
        grad_up_bias,
        grad_down,
        grad_down_bias,
    )


def solution(mesh):
    return jax.shard_map(
        body,
        mesh=mesh,
        in_specs=(
            P(("dp", "mp"), None),
            P("dp", None),
            P(),
            P(),
            P(),
            P(None, None, "mp"),
            P(None, "mp"),
            P("mp", None),
            P(),
            P(),
            P(None, "mp"),
            P("mp"),
            P("mp", None),
            P(),
            P(("dp", "mp"), None),
        ),
        out_specs=(
            P(("dp", "mp"), None),
            P(("dp", "mp"), None),
            P(),
            P(),
            P(None, None, "mp"),
            P(None, "mp"),
            P("mp", None),
            P(),
            P(),
            P(None, "mp"),
            P("mp"),
            P("mp", None),
            P(),
        ),
        check_vma=False,
    )
```

time: 5110 us -> 824 us (0.16)
  local copies, waits for them, and re-layouts: 4300 us -> 19.6 us
  matrix products: 196 us -> 75.7 us
  waiting for transfers between devices: 451 us -> 565 us
  Pallas kernels: 0 us -> 53.4 us
    gather x4 -> x0, local copies, waits for them, and re-layouts: 4240 us -> none  [the longest x2 2680 us: bucket_tables(): prev_map = bucket_of[prev_index]]
    dot_general x33 -> x12, matrix products: 129 us -> 18.4 us  [the longest x3 6.07 us: body(): jnp.einsum('td,cd->tc', grad_proj[slot_index], w_qkv[slot_index], preferr...]
    all_gather x1, waiting for transfers between devices: 0.01 us -> 63.7 us  [body(): lax.all_gather(layer_norm(x_part, ln1_gain, ln1_bias).astype(jnp.bfloat16...]
    pallas_call x0 -> x2, Pallas kernels: none -> 53.4 us  [the longest x1 35.1 us: attention_backward(): pl.pallas_call(attention_backward_kernel, grid_spec=pltpu.PrefetchScalarG...]
  transfers between devices with their start and end apart: 9 -> 9, of which waited for: 7 -> 9; matrix products, arithmetic and copies ran while one was open for 86% -> 6% of each run, Pallas kernels for 0% -> 0%
where the time goes in v1:
time: 824 us; the launch traced here: 817 us
  waiting for transfers between devices  565 us (69%)
  matrix products  75.7 us (9%)
  blocking collectives  54.5 us (7%)
  Pallas kernels  53.4 us (6%)
  other arithmetic  33 us (4%)
  local copies, waits for them, and re-layouts  19.6 us (2%)
  between operations  14.7 us (2%)
    psum x1, waiting for transfers between devices, body(): lax.psum((grad_qkv, grad_table, grad_wout, grad_up, grad_up_bias, grad_do...  132 us
    all_gather x1, waiting for transfers between devices, body(): lax.all_gather(layer_norm(x_part, ln1_gain, ln1_bias).astype(jnp.bfloat16...  63.7 us
    all_gather x1, waiting for transfers between devices, body(): lax.all_gather(layer_norm(hidden_in, ln2_gain, ln2_bias).astype(jnp.bfloa...  62.9 us
    all_gather x1, waiting for transfers between devices, body(): lax.all_gather(grad_hidden.astype(jnp.bfloat16), 'mp', axis=0, tiled=True)  62.7 us
    reduce_scatter x1, waiting for transfers between devices, body(): lax.psum_scatter(jnp.dot(activated_low, w_down, preferred_element_type=jn...  61.1 us
    reduce_scatter x1, waiting for transfers between devices, body(): lax.psum_scatter(jnp.dot(attended, w_out, preferred_element_type=jnp.floa...  59 us
    all_gather x1, waiting for transfers between devices, body(): grad_rows = lax.all_gather(out_grad, 'mp', axis=0, tiled=True)  55 us
    reduce_scatter x1, waiting for transfers between devices, body(): lax.psum_scatter(jnp.einsum('tf,df->td', grad_pre, w_up, preferred_elemen...  45.9 us
  transfers between devices with their start and end apart: 9, of which 9 were waited for; matrix products, arithmetic and copies ran while one was open for 6% of the time, Pallas kernels for 0%

profile of v1, /device:TPU:0, one launch (start us, length us, event | category | flops | bytes accessed | tf_op | source)
XLA Modules:
  0.0 817.3 jit_solution(529359539380984748)
XLA Ops:
  7.3 1.4 convert_reduce_fusion.3
  8.7 1.5 fusion.18
  10.2 2.4 fusion.16
  13.0 0.6 slice.28
  14.0 1.3 fusion.43
  15.3 63.7 %all-gather.5.cloned.1.call-done = bf16[1536,1024]{1,0:T(8,128)(2,1)} async-done(((bf16[384,1024]{1,0:T(8,128)(2,1)}), bf16[1536,1024]{1,0:T(8,128)(2,1)}) %all-gather.5.cloned.1.call-update) | async-done | bytes 3145744 | tf_op jit(solution)/shard_map/all_gather | solution.py:402
  79.0 3.1 convolution_convert_fusion.4.v_ref
  82.1 0.3 copy-done.34
  82.5 1.0 convolution_convert_fusion.5.k_ref
  83.5 1.0 fusion.6.q_ref
  84.5 18.3 %attention_forward.1 = (bf16[1536,256]{1,0:T(8,128)(2,1)S(1)}, f32[8,1536]{1,0:T(8,128)S(1)}) custom-call(s32[1]{0:T(128)} %bitcast.1.cut_ref, bf16[1536,256]{1,0:T(8,128)(2,1)S(1)} %fusion.6.q_ref, bf16[1536,256]{1,0:T(8,128)(2,1)S(1)} %convolution_convert_fusion.5.k_ref, bf16[1536,256]{1,0:T(8,128)(2,1)S(1)} %convolution_convert_fusion.4.v_ref, ...), custom_call_target="tpu_custom_call" | custom-call | flops 4831838208 | bytes 3145728 | tf_op jit(solution)/shard_map/attention_forward/pallas_call | solution.py:140
  102.8 0.6 copy-done.7
  103.5 2.6 convolution_convert_fusion
  106.2 59.0 %reduce-scatter.5.cloned.1.call-done = bf16[384,1024]{1,0:T(8,128)(2,1)} async-done(((bf16[1536,1024]{1,0:T(8,128)(2,1)}), bf16[384,1024]{1,0:T(8,128)(2,1)}) %reduce-scatter.5.cloned.1.call-update) | async-done | bytes 786448 | tf_op jit(solution)/shard_map/reduce_scatter | solution.py:414
  165.2 1.5 fusion.23
  166.7 1.5 multiply_reduce_fusion
  168.3 1.3 add_convert_fusion.4
  169.7 0.5 all-gather.9.cloned.1.call-update
  170.4 62.9 %all-gather.7.cloned.1.call-done = bf16[1536,1024]{1,0:T(8,128)(2,1)} async-done(((bf16[384,1024]{1,0:T(8,128)(2,1)}), bf16[1536,1024]{1,0:T(8,128)(2,1)}) %all-gather.7.cloned.1.call-update) | async-done | bytes 3145744 | tf_op jit(solution)/shard_map/all_gather | solution.py:421
  233.3 8.6 %fusion.52 = f32[1536,1024]{1,0:T(8,128)} fusion(bf16[1536,1024]{1,0:T(8,128)(2,1)} %all-gather.7.cloned.1.call-done, bf16[1024,1024]{1,0:T(8,128)(2,1)} %param.25), kind=kOutput, calls=%fused_computation.111 | convolution fusion | flops 3221225472 | bytes 11534336 | tf_op jit(solution)/shard_map/dot_general | solution.py:424
  241.9 55.0 %all-gather.9.cloned.1.call-done = bf16[1536,1024]{1,0:T(8,128)(2,1)} async-done(((bf16[384,1024]{1,0:T(8,128)(2,1)}), bf16[1536,1024]{1,0:T(8,128)(2,1)}) %all-gather.9.cloned.1.call-update) | async-done | bytes 3145744 | tf_op jit(solution)/shard_map/all_gather | solution.py:435
  296.9 20.9 %convert_reduce_fusion = (f32[1024]{0:T(1024)S(1)}, bf16[1536,1024]{1,0:T(8,128)(2,1)S(1)}, f32[1536,1024]{1,0:T(8,128)}) fusion(f32[1536,1024]{1,0:T(8,128)} %fusion.52, f32[1024]{0:T(1024)S(1)} %copy-done.32, bf16[1536,1024]{1,0:T(8,128)(2,1)} %all-gather.9.cloned.1.call-done, bf16[1024,1024]{1,0:T(8,128)(2,1)S(1)} %copy-done), kind=kOutput, calls=%fused_computation.2 | convolution fusion | flops 3339189248 | bytes 20979712 | tf_op jit(solution)/shard_map/td,fd->tf/dot_general | solution.py:439
  317.8 1.7 copy-done.41
  319.5 4.9 convolution_convert_fusion.1
  324.4 0.3 reduce-scatter.7.cloned.1.call-start
  324.7 6.4 multiply_convert_fusion
  331.1 1.6 copy-done.17
  332.7 4.7 convolution_convert_fusion.2
  337.6 45.9 %reduce-scatter.9.cloned.1.call-done = bf16[384,1024]{1,0:T(8,128)(2,1)} async-done(((bf16[1536,1024]{1,0:T(8,128)(2,1)}), bf16[384,1024]{1,0:T(8,128)(2,1)}) %reduce-scatter.9.cloned.1.call-update) | async-done | bytes 786448 | tf_op jit(solution)/shard_map/reduce_scatter | solution.py:446
  383.5 1.9 fusion.20
  385.4 61.1 %reduce-scatter.7.cloned.1.call-done = bf16[384,1024]{1,0:T(8,128)(2,1)} async-done(((bf16[1536,1024]{1,0:T(8,128)(2,1)}), bf16[384,1024]{1,0:T(8,128)(2,1)}) %reduce-scatter.7.cloned.1.call-update) | async-done | bytes 786448 | tf_op jit(solution)/shard_map/reduce_scatter | solution.py:427
  446.5 3.1 fusion.51
  449.6 1.1 copy-done.11
  450.8 1.1 fusion.25
  451.9 0.3 reduce-scatter.11.cloned.1.call-start
  452.3 0.6 select_maximum_fusion.bias_ref
  452.9 62.7 %all-gather.11.cloned.1.call-done = bf16[1536,1024]{1,0:T(8,128)(2,1)} async-done(((bf16[384,1024]{1,0:T(8,128)(2,1)}), bf16[1536,1024]{1,0:T(8,128)(2,1)}) %all-gather.11.cloned.1.call-update) | async-done | bytes 3145744 | tf_op jit(solution)/shard_map/all_gather | solution.py:457
  515.6 3.8 convolution_convert_fusion.3.grad_ref
  519.4 35.1 %attention_backward.1 = (bf16[1536,256]{1,0:T(8,128)(2,1)}, bf16[1536,256]{1,0:T(8,128)(2,1)}, bf16[1536,256]{1,0:T(8,128)(2,1)}, f32[8,512]{1,0:T(8,128)}) custom-call(s32[1]{0:T(128)} %bitcast.1.cut_ref, bf16[1536,256]{1,0:T(8,128)(2,1)} %copy-done.6, bf16[1536,256]{1,0:T(8,128)(2,1)} %copy-done.5, bf16[1536,256]{1,0:T(8,128)(2,1)} %copy-done.4, ...), custom_call_target="tpu_custom_call" | custom-call | flops 12079595520 | bytes 6291456 | tf_op jit(solution)/shard_map/attention_backward/pallas_call | solution.py:292
  554.5 2.2 fusion.28
  556.7 1.0 fusion.31
  557.9 2.8 add_convert_fusion
  560.7 0.3 all-reduce.7.cloned.1.call-start
  561.1 8.5 %fusion.54 = f32[1024,1024]{1,0:T(8,128)} fusion(bf16[1536,1024]{1,0:T(8,128)(2,1)} %all-gather.7.cloned.1.call-done, bf16[1536,1024]{1,0:T(8,128)(2,1)} %copy-done.41), kind=kOutput, calls=%fused_computation.113 | convolution fusion | flops 3221225472 | bytes 10485760 | tf_op jit(solution)/shard_map/td,tf->df/dot_general | solution.py:444
  569.6 5.0 fusion.55
  574.6 1.0 convolution_bitcast_fusion
  575.7 1.0 convolution_bitcast_fusion.1
  576.8 1.0 convolution_bitcast_fusion.2
  577.8 1.9 pad_maximum_fusion
  579.7 1.4 copy-done.37
  581.1 2.0 fusion.53
  583.1 0.7 copy-done.29
  584.4 13.1 %all-reduce.3 = (f32[32,4]{0,1:T(4,128)}, f32[1024]{0:T(1024)}) all-reduce(f32[32,4]{0,1:T(4,128)S(1)} %fusion.40, f32[1024]{0:T(1024)S(1)} %get-tuple-element.43), channel_id=1, replica_groups=mesh['dp'=8,'mp'=4] {'dp'}, use_global_device_ids=true, to_apply=%region_20.21 | all-reduce | flops 1152 | bytes 9216 | tf_op jit(solution)/shard_map/psum | solution.py:491
  597.5 22.3 %reduce-scatter.11.cloned.1.call-done = bf16[384,1024]{1,0:T(8,128)(2,1)} async-done(((bf16[1536,1024]{1,0:T(8,128)(2,1)}), bf16[384,1024]{1,0:T(8,128)(2,1)}) %reduce-scatter.11.cloned.1.call-update) | async-done | bytes 786448 | tf_op jit(solution)/shard_map/reduce_scatter | solution.py:484
  619.8 1.7 convert_reduce_fusion.1
  621.5 2.0 fusion.21
  623.6 2.8 convert_reduce_fusion.4
  626.4 41.5 %all-reduce.2 = (f32[1024]{0:T(1024)}, f32[1024]{0:T(1024)}, f32[1024]{0:T(1024)}, f32[1024]{0:T(1024)}, f32[1024]{0:T(1024)}) all-reduce(f32[1024]{0:T(1024)S(1)} %get-tuple-element.27, f32[1024]{0:T(1024)S(1)} %get-tuple-element.30, f32[1024]{0:T(1024)S(1)} %get-tuple-element.25, ...), channel_id=1, replica_groups=mesh['dp'=8,'mp'=4] {'dp','mp'}, use_global_device_ids=true, to_apply=%region_14.15 | all-reduce | flops 5120 | bytes 40960 | tf_op jit(solution)/shard_map/psum | solution.py:494
  667.9 131.7 %all-reduce.7.cloned.1.call-done = (f32[3,1024,256]{2,1,0:T(8,128)}, f32[256,1024]{1,0:T(8,128)}, f32[1024,1024]{1,0:T(8,128)}, f32[1024,1024]{1,0:T(8,128)}) async-done(((f32[3,1024,256]{2,1,0:T(8,128)}, f32[256,1024]{1,0:T(8,128)}, f32[1024,1024]{1,0:T(8,128)}, f32[1024,1024]{1,0:T(8,128)}), (f32[3,1024,256]{2,1,0:T(8,128)}, f32[256,1024]{1,0:T(8,128)}, f32[1024,1024]{1,0:T(8,128)}, ...) | async-done | bytes 12582928 | tf_op jit(solution)/shard_map/psum | solution.py:491
  799.6 3.9 copy.34
  803.5 1.0 copy.35
  804.5 2.1 copy.36
  806.7 1.6 copy-done.15
  808.2 2.0 copy.37
  (111 shorter events, 2.4 us)
Async XLA Ops:
  7.2 289.7 %copy-start = (bf16[1024,1024]{1,0:T(8,128)(2,1)S(1)}, bf16[1024,1024]{1,0:T(8,128)(2,1)}, u32[]{:S(2)}) copy-start(bf16[1024,1024]{1,0:T(8,128)(2,1)} %param.27) | copy-start | bytes 6291460
  7.2 5.5 copy-start.40
  7.2 5.5 copy-start.39
  7.2 5.8 copy-start.30
  7.2 71.8 %all-gather.5.cloned.1.call-start = ((), (), s32[]{:S(2)}) async-start(), calls=%async_computation.4 | async-start | bytes 3932160 | tf_op jit(solution)/shard_map/all_gather | solution.py:402
  12.6 152.6 %reduce-scatter.5.cloned.1.call-start = ((), (), s32[]{:S(2)}) async-start(), calls=%async_computation.5 | async-start | bytes 3932160 | tf_op jit(solution)/shard_map/reduce_scatter | solution.py:414
  79.0 3.1 copy-start.21
  79.0 3.5 copy-start.34
  82.5 2.0 copy-start.4
  83.5 1.0 copy-start.5
  84.5 18.4 %copy-start.6 = (bf16[1536,256]{1,0:T(8,128)(2,1)}, bf16[1536,256]{1,0:T(8,128)(2,1)S(1)}, u32[]{:S(2)}) copy-start(bf16[1536,256]{1,0:T(8,128)(2,1)S(1)} %fusion.6.q_ref) | copy-start | bytes 2359300
  84.5 19.0 %copy-start.26 = (bf16[256,1024]{1,0:T(8,128)(2,1)S(1)}, bf16[256,1024]{1,0:T(8,128)(2,1)}, u32[]{:S(2)}) copy-start(bf16[256,1024]{1,0:T(8,128)(2,1)} %param.22) | copy-start | bytes 1572868
  102.8 0.6 copy-start.7
  103.5 2.7 copy-start.2
  106.1 59.1 %copy-start.8 = (bf16[384,1024]{1,0:T(8,128)(2,1)S(1)}, bf16[384,1024]{1,0:T(8,128)(2,1)}, u32[]{:S(2)}) copy-start(bf16[384,1024]{1,0:T(8,128)(2,1)} %param.15) | copy-start | bytes 2359300
  106.1 62.1 %copy-start.28 = (f32[1024]{0:T(1024)S(1)}, f32[1024]{0:T(1024)}, u32[]{:S(2)}) copy-start(f32[1024]{0:T(1024)} %param.23) | copy-start | bytes 12292
  106.1 62.1 %copy-start.31 = (f32[1024]{0:T(1024)S(1)}, f32[1024]{0:T(1024)}, u32[]{:S(2)}) copy-start(f32[1024]{0:T(1024)} %param.24) | copy-start | bytes 12292
  106.2 127.1 %all-gather.7.cloned.1.call-start = ((), (), s32[]{:S(2)}) async-start(), calls=%async_computation.6 | async-start | bytes 3932160 | tf_op jit(solution)/shard_map/all_gather | solution.py:421
  165.2 3.0 copy-start.9
  169.6 127.3 %all-gather.9.cloned.1.call-start = ((), (), s32[]{:S(2)}) async-start(), calls=%async_computation.8 | async-start | bytes 3932160 | tf_op jit(solution)/shard_map/all_gather | solution.py:435
  170.2 126.7 %copy-start.32 = (f32[1024]{0:T(1024)S(1)}, f32[1024]{0:T(1024)}, u32[]{:S(2)}) copy-start(f32[1024]{0:T(1024)} %param.26) | copy-start | bytes 12292
  170.2 213.3 %reduce-scatter.9.cloned.1.call-start = ((), (), s32[]{:S(2)}) async-start(), calls=%async_computation.9 | async-start | bytes 3932160 | tf_op jit(solution)/shard_map/reduce_scatter | solution.py:446
  296.9 22.6 %copy-start.38 = (bf16[1024,1024]{1,0:T(8,128)(2,1)S(1)}, bf16[1024,1024]{1,0:T(8,128)(2,1)}, u32[]{:S(2)}) copy-start(bf16[1024,1024]{1,0:T(8,128)(2,1)} %param.25) | copy-start | bytes 6291460
  317.8 1.7 copy-start.41
  324.4 122.1 %reduce-scatter.7.cloned.1.call-start = ((), (), s32[]{:S(2)}) async-start(), calls=%async_computation.7 | async-start | bytes 3932160 | tf_op jit(solution)/shard_map/reduce_scatter | solution.py:427
  331.1 1.7 copy-start.17
  337.5 46.0 %copy-start.10 = (bf16[384,1024]{1,0:T(8,128)(2,1)S(1)}, bf16[384,1024]{1,0:T(8,128)(2,1)}, u32[]{:S(2)}) copy-start(bf16[384,1024]{1,0:T(8,128)(2,1)} %reduce-scatter.5.cloned.1.call-done) | copy-start | bytes 2359300
  337.5 109.0 %copy-start.33 = (f32[1024]{0:T(1024)S(1)}, f32[1024]{0:T(1024)}, u32[]{:S(2)}) copy-start(f32[1024]{0:T(1024)} %param.28) | copy-start | bytes 12292
  337.5 178.1 %all-gather.11.cloned.1.call-start = ((), (), s32[]{:S(2)}) async-start(), calls=%async_computation.10 | async-start | bytes 3932160 | tf_op jit(solution)/shard_map/all_gather | solution.py:457
  385.4 65.4 %copy-start.14 = (bf16[384,1024]{1,0:T(8,128)(2,1)S(1)}, bf16[384,1024]{1,0:T(8,128)(2,1)}, u32[]{:S(2)}) copy-start(bf16[384,1024]{1,0:T(8,128)(2,1)} %param.29) | copy-start | bytes 2359300
  449.6 1.2 copy-start.11
  451.9 167.9 %reduce-scatter.11.cloned.1.call-start = ((), (), s32[]{:S(2)}) async-start(), calls=%async_computation.11 | async-start | bytes 3932160 | tf_op jit(solution)/shard_map/reduce_scatter | solution.py:484
  519.4 35.1 %copy-start.22 = (bf16[3,1024,256]{2,1,0:T(8,128)(2,1)S(1)}, bf16[3,1024,256]{2,1,0:T(8,128)(2,1)}, u32[]{:S(2)}) copy-start(bf16[3,1024,256]{2,1,0:T(8,128)(2,1)} %param.20) | copy-start | bytes 4718596
  554.5 2.2 copy-start.19
  556.7 1.1 copy-start.24
  560.7 238.9 %all-reduce.7.cloned.1.call-start = ((), (), s32[]{:S(2)}) async-start(), calls=%async_computation.12 | async-start | bytes 25165824 | tf_op jit(solution)/shard_map/psum | solution.py:491
  561.1 8.5 %copy-start.18 = (bf16[1536,1024]{1,0:T(8,128)(2,1)S(1)}, bf16[1536,1024]{1,0:T(8,128)(2,1)}, u32[]{:S(2)}) copy-start(bf16[1536,1024]{1,0:T(8,128)(2,1)} %copy-done.17) | copy-start | bytes 9437188
  561.1 8.5 %copy-start.36 = (bf16[1536,1024]{1,0:T(8,128)(2,1)S(1)}, bf16[1536,1024]{1,0:T(8,128)(2,1)}, u32[]{:S(2)}) copy-start(bf16[1536,1024]{1,0:T(8,128)(2,1)} %all-gather.9.cloned.1.call-done) | copy-start | bytes 9437188
  569.6 5.0 copy-start.25
  569.6 5.0 copy-start.35
  574.6 1.1 copy-start.20
  577.8 1.9 copy-start.3
  577.8 3.3 copy-start.37
  583.1 0.7 copy-start.29
  583.1 36.7 %copy-start.27 = (f32[1024]{0:T(1024)S(1)}, f32[1024]{0:T(1024)}, u32[]{:S(2)}) copy-start(f32[1024]{0:T(1024)} %param.18) | copy-start | bytes 12292
  583.1 40.5 %copy-start.12 = (f32[384,1024]{1,0:T(8,128)S(1)}, f32[384,1024]{1,0:T(8,128)}, u32[]{:S(2)}) copy-start(f32[384,1024]{1,0:T(8,128)} %copy-done.11) | copy-start | bytes 4718596
  619.8 3.8 copy-start.13
  799.6 3.9 copy-start.23
  799.6 4.9 copy-start.16
  804.5 3.7 copy-start.15
  804.5 5.7 copy-start.1
Sparse Core Ops, SparseCore 0:
  12.8 66.1 all-gather.4
  106.3 58.8 reduce-scatter.4
  169.7 63.5 all-gather.6
  234.7 62.1 all-gather.8
  324.5 58.8 reduce-scatter.8
  386.2 60.2 reduce-scatter.6
  452.1 63.5 all-gather.10
  560.9 58.8 reduce-scatter.10
  624.9 174.6 all-reduce.6

commit v2 on v1

--- a/solution.py
+++ b/solution.py
@@ -1,25 +1,15 @@
+import functools
+
 import jax
 import jax.numpy as jnp
 from jax import lax
 from jax.experimental import pallas as pl
 from jax.experimental.pallas import tpu as pltpu
-from jax.sharding import PartitionSpec as P
-
+from jax.sharding import Mesh, PartitionSpec as P
 
 EPSILON = 1e-05
 HIGHEST_PRECISION = lax.Precision.HIGHEST
-
-
-def layer_norm(inputs, norm_gain, norm_bias):
-    center = inputs - jnp.mean(inputs, axis=-1, keepdims=True)
-    spread = jnp.mean(center * center, axis=-1, keepdims=True)
-    return center * lax.rsqrt(spread + EPSILON) * norm_gain + norm_bias
-
-
-def gelu_exact(inputs):
-    return jax.nn.gelu(inputs, approximate=False)
-
-
+TIE = 1
 BLK = 256
 HEAD_LANES = 64
 NEAR = 128
@@ -35,6 +25,10 @@
     return jnp.where(keep, value, jnp.zeros_like(value))
 
 
+def scaled(queries):
+    return queries * jnp.asarray(HEAD_LANES ** -0.5, queries.dtype)
+
+
 def dot_nt(left, right):
     return lax.dot_general(
         left, right, (((1,), (1,)), ((), ())), preferred_element_type=jnp.float32
@@ -48,9 +42,10 @@
 
 
 def attention_forward_kernel(
-    cut_ref, q_ref, k_ref, v_ref, bias_ref, out_ref, lse_ref, tile_ref, masked_v, score_ref
+    cut_ref, qkv_ref, bias_ref, out_ref, lse_ref, tile_ref, masked_v, score_ref
 ):
     heads = masked_v.shape[0]
+    width = out_ref.shape[1]
     block = pl.program_id(0)
     cut = cut_ref[0]
 
@@ -59,19 +54,19 @@
         for head in range(heads):
             wide = jnp.broadcast_to(bias_ref[head : head + 1, :], (BLK, 2 * BLK))
             tile_ref[head] = pltpu.roll(wide, 0, 1, stride=1, stride_axis=0)
-            masked_v[head] = one_head(v_ref[...], head)
+            masked_v[head] = one_head(qkv_ref[:, 2 * width :], head)
 
     row_start = block * BLK
     first = jnp.where(row_start >= cut, cut // BLK, 0)
     rows = row_start + lax.broadcasted_iota(jnp.int32, (BLK, BLK), 0)
     seg_start = jnp.where(rows >= cut, cut, 0)
     columns = lax.broadcasted_iota(jnp.int32, (BLK, BLK), 1)
-    q_block = q_ref[...]
+    q_block = scaled(qkv_ref[pl.ds(pl.multiple_of(row_start, BLK), BLK), 0:width])
     q_heads = [one_head(q_block, head) for head in range(heads)]
 
     def scores_of(key_block, tops):
         key_start = pl.multiple_of(key_block * BLK, BLK)
-        keys = k_ref[pl.ds(key_start, BLK), :]
+        keys = qkv_ref[pl.ds(key_start, BLK), width : 2 * width]
         places = key_start + columns
         allowed = (places <= rows) & (places >= seg_start)
         offset = pl.multiple_of(jnp.maximum(key_block - block + 1, 0) * BLK, BLK)
@@ -133,8 +128,8 @@
     lse_ref[...] = jnp.transpose(logs)[0:8, :]
 
 
-def attention_forward(cut, queries, keys, values, near_bias):
-    length, width = queries.shape
+def attention_forward(cut, projected, near_bias):
+    length, width = projected.shape[0], projected.shape[1] // 3
     heads = width // HEAD_LANES
     whole = lambda block, cut: (0, 0)
     return pl.pallas_call(
@@ -143,9 +138,7 @@
             num_scalar_prefetch=1,
             grid=(length // BLK,),
             in_specs=[
-                pl.BlockSpec((BLK, width), lambda block, cut: (block, 0)),
-                pl.BlockSpec((length, width), whole),
-                pl.BlockSpec((length, width), whole),
+                pl.BlockSpec((length, 3 * width), whole),
                 pl.BlockSpec((8, 2 * BLK), whole),
             ],
             out_specs=[
@@ -170,18 +163,17 @@
             transcendentals=heads * length * length // 2,
         ),
         name="attention_forward",
-    )(cut, queries, keys, values, near_bias)
+    )(cut, projected, near_bias)
 
 
 def attention_backward_kernel(
-    cut_ref, q_ref, k_ref, v_ref, grad_ref, att_ref, lse_ref, bias_ref,
-    dq_ref, dk_ref, dv_ref, table_ref,
+    cut_ref, qkv_ref, grad_ref, att_ref, lse_ref, bias_ref, dqkv_ref, table_ref,
     tile_ref, q_masked, grad_masked, delta_ref, dq_sum, near_sum, far_sum,
 ):
     heads = q_masked.shape[0]
     block = pl.program_id(0)
     n_blocks = pl.num_programs(0)
-    length, width = q_ref.shape
+    length, width = grad_ref.shape
     cut = cut_ref[0]
 
     @pl.when(block == 0)
@@ -196,15 +188,15 @@
         for head in range(heads):
             wide = jnp.broadcast_to(bias_ref[head : head + 1, :], (BLK, 2 * BLK))
             tile_ref[head] = pltpu.roll(wide, 0, 1, stride=1, stride_axis=0)
-            q_masked[head] = one_head(q_ref[...], head)
+            q_masked[head] = one_head(scaled(qkv_ref[:, 0:width]), head)
             grad_masked[head] = one_head(grad_ref[...], head)
         dq_sum[...] = jnp.zeros_like(dq_sum)
         near_sum[...] = jnp.zeros_like(near_sum)
         far_sum[...] = jnp.zeros_like(far_sum)
 
     key_start = pl.multiple_of(block * BLK, BLK)
-    keys = k_ref[pl.ds(key_start, BLK), :]
-    values = v_ref[pl.ds(key_start, BLK), :]
+    keys = qkv_ref[pl.ds(key_start, BLK), width : 2 * width]
+    values = qkv_ref[pl.ds(key_start, BLK), 2 * width :]
     keys_t = jnp.transpose(keys)
     places = key_start + lax.broadcasted_iota(jnp.int32, (BLK, BLK), 0)
     columns = lax.broadcasted_iota(jnp.int32, (BLK, BLK), 1)
@@ -258,14 +250,14 @@
 
     empty = jnp.zeros((BLK, width), jnp.float32)
     dk, dv = lax.fori_loop(block, last, one_block, (empty, empty))
-    dk_ref[...] = dk.astype(jnp.bfloat16)
-    dv_ref[...] = dv.astype(jnp.bfloat16)
+    dqkv_ref[pl.ds(key_start, BLK), width : 2 * width] = dk.astype(jnp.bfloat16)
+    dqkv_ref[pl.ds(key_start, BLK), 2 * width :] = dv.astype(jnp.bfloat16)
 
     @pl.when(block == n_blocks - 1)
     def _():
         for query_block in range(length // BLK):
             spot = slice(query_block * BLK, (query_block + 1) * BLK)
-            dq_ref[spot, :] = (
+            dqkv_ref[spot, 0:width] = (
                 jnp.transpose(dq_sum[:, spot]) * (HEAD_LANES ** -0.5)
             ).astype(jnp.bfloat16)
         for head in range(heads):
@@ -284,8 +276,8 @@
             )
 
 
-def attention_backward(cut, queries, keys, values, grad_att, attended, logs, near_bias):
-    length, width = queries.shape
+def attention_backward(cut, projected, grad_att, attended, logs, near_bias):
+    length, width = attended.shape
     heads = width // HEAD_LANES
     whole = lambda block, cut: (0, 0)
     full = pl.BlockSpec((length, width), whole)
@@ -295,14 +287,12 @@
             num_scalar_prefetch=1,
             grid=(length // BLK,),
             in_specs=[
-                full, full, full, full, full,
+                pl.BlockSpec((length, 3 * width), whole), full, full,
                 pl.BlockSpec((8, length), whole),
                 pl.BlockSpec((8, 2 * BLK), whole),
             ],
             out_specs=[
-                full,
-                pl.BlockSpec((BLK, width), lambda block, cut: (block, 0)),
-                pl.BlockSpec((BLK, width), lambda block, cut: (block, 0)),
+                pl.BlockSpec((length, 3 * width), whole),
                 pl.BlockSpec((8, 2 * BLK), whole),
             ],
             scratch_shapes=[
@@ -316,9 +306,7 @@
             ],
         ),
         out_shape=[
-            jax.ShapeDtypeStruct((length, width), jnp.bfloat16),
-            jax.ShapeDtypeStruct((length, width), jnp.bfloat16),
-            jax.ShapeDtypeStruct((length, width), jnp.bfloat16),
+            jax.ShapeDtypeStruct((length, 3 * width), jnp.bfloat16),
             jax.ShapeDtypeStruct((8, 2 * BLK), jnp.float32),
         ],
         compiler_params=pltpu.CompilerParams(
@@ -329,7 +317,7 @@
             transcendentals=heads * length * length // 2,
         ),
         name="attention_backward",
-    )(cut, queries, keys, values, grad_att, attended, logs, near_bias)
+    )(cut, projected, grad_att, attended, logs, near_bias)
 
 
 def distance_bias(rel_table, bucket_of):
@@ -374,178 +362,432 @@
     )
 
 
+TEAM = 4
+
+
+def place_of(axis):
+    return lax.axis_index(axis)
+
+
+def flip(value, axis, bit):
+    size = lax.axis_size(axis)
+    return lax.ppermute(value, axis, [(i, i ^ bit) for i in range(size)])
+
+
+def halve(value, dim, axis, bit):
+    mine = (lax.axis_index(axis) // bit) % 2
+    keep = lax.dynamic_index_in_dim(value, mine, dim, keepdims=False)
+    send = lax.dynamic_index_in_dim(value, 1 - mine, dim, keepdims=False)
+    received = flip(send.astype(jnp.bfloat16), axis, bit)
+    return (keep.astype(jnp.float32) + received.astype(jnp.float32)).astype(jnp.bfloat16)
+
+
+def double(value, axis, bit):
+    mine = (lax.axis_index(axis) // bit) % 2
+    other = flip(value, axis, bit)
+    pair = jnp.zeros((2,) + value.shape, value.dtype)
+    pair = lax.dynamic_update_index_in_dim(pair, value, mine, 0)
+    return lax.dynamic_update_index_in_dim(pair, other, 1 - mine, 0)
+
+
+def bits_of(size):
+    bits = []
+    bit = 1
+    while bit < size:
+        bits.append(bit)
+        bit *= 2
+    return bits
+
+
+def chain_gather(own):
+    size = lax.axis_size("mp")
+    spot = lax.axis_index("mp")
+    rows = own.shape[0]
+    right = left = own
+    rights, lefts = {}, {}
+    for step in range(1, size):
+        right = lax.ppermute(right, "mp", [(i, i + 1) for i in range(step - 1, size - 1)])
+        left = lax.ppermute(left, "mp", [(i, i - 1) for i in range(1, size - step + 1)])
+        rights[step], lefts[step] = right, left
+    whole = jnp.zeros((size * rows,) + own.shape[1:], own.dtype)
+    whole = lax.dynamic_update_slice_in_dim(whole, own, spot * rows, 0)
+    for step in range(1, size):
+        block = rights[step] + lefts[size - step]
+        source = lax.rem(spot + size - step, size)
+        whole = lax.dynamic_update_slice_in_dim(whole, block, source * rows, 0)
+    return whole, rights
+
+
+def chain_scatter(value):
+    size = lax.axis_size("mp")
+    spot = lax.axis_index("mp")
+    rows = value.shape[0] // size
+
+    def block(place):
+        return lax.dynamic_slice_in_dim(value, place * rows, rows, 0).astype(jnp.float32)
+
+    from_left = from_right = None
+    for step in range(1, size):
+        reach = size - step
+        to_right = block(jnp.minimum(spot + reach, size - 1))
+        to_left = block(jnp.maximum(spot - reach, 0))
+        if from_left is not None:
+            to_right = to_right + from_left.astype(jnp.float32)
+            to_left = to_left + from_right.astype(jnp.float32)
+        from_left = lax.ppermute(
+            to_right.astype(jnp.bfloat16), "mp", [(i, i + 1) for i in range(step)]
+        )
+        from_right = lax.ppermute(
+            to_left.astype(jnp.bfloat16), "mp", [(i, i - 1) for i in range(size - step, size)]
+        )
+    return block(spot) + from_left.astype(jnp.float32) + from_right.astype(jnp.float32)
+
+
+def swap_over_chain(stack):
+    size = lax.axis_size("mp")
+    spot = lax.axis_index("mp")
+    own = lax.dynamic_index_in_dim(stack, spot, 0, keepdims=True)
+    result = lax.dynamic_update_slice_in_dim(jnp.zeros_like(stack), own, spot, 0)
+    for step in [2, 1, 3] if size == 4 else range(1, size):
+        send = lax.dynamic_index_in_dim(stack, lax.rem(spot + step, size), 0, keepdims=True)
+        received = lax.ppermute(send, "mp", [(i, (i + step) % size) for i in range(size)])
+        result = lax.dynamic_update_slice_in_dim(
+            result, received, lax.rem(spot + size - step, size), 0
+        )
+    return result
+
+
+def team_gather(own):
+    core = flip(own, "team", 1)
+    across = flip(own, "team", 2)
+    return jnp.concatenate([own, core], axis=0), jnp.concatenate(
+        [across, flip(across, "team", 1)], axis=0
+    )
+
+
+def normalize(inputs):
+    center = inputs - jnp.mean(inputs, axis=-1, keepdims=True)
+    spread = jnp.mean(center * center, axis=-1, keepdims=True)
+    inverse = lax.rsqrt(spread + EPSILON)
+    return center * inverse, inverse
+
+
+def normalize_backward(grad, gain, unit, inverse):
+    scaled_grad = grad * gain
+    middle = jnp.mean(scaled_grad, axis=-1, keepdims=True)
+    along = jnp.mean(scaled_grad * unit, axis=-1, keepdims=True)
+    return (scaled_grad - middle - unit * along) * inverse
+
+
+def dot_tn(left, right):
+    return lax.dot_general(
+        left, right, (((0,), (0,)), ((), ())), preferred_element_type=jnp.float32
+    )
+
+
+def feed_kernel(
+    weight_ref, bias_ref, second_ref, grad_ref,
+    act_ref, pre_ref, back_ref, out_ref, sum_ref, back_sum, out_sum, *, unit,
+):
+    step = pl.program_id(0)
+    parts, copies, _, depth = weight_ref.shape
+    hidden = parts * copies * unit
+    w_up = weight_ref[:, :, 0:unit, :].reshape(hidden, depth)
+    w_down = weight_ref[:, :, unit : 2 * unit, :].reshape(hidden, depth)
+    pre = dot_nt(second_ref[...], w_up) + bias_ref[...]
+    grad_act = dot_nt(grad_ref[...], w_down)
+    cdf = 0.5 + 0.5 * lax.erf(pre * 0.7071067811865476)
+    pdf = jnp.exp(pre * pre * -0.5) * 0.3989422804014327
+    active = (pre * cdf).astype(jnp.bfloat16)
+    grad_pre = ((cdf + pre * pdf) * grad_act).astype(jnp.bfloat16)
+    act_ref[...] = active
+    pre_ref[...] = grad_pre
+    sum_ref[...] = jnp.sum(grad_pre.astype(jnp.float32), axis=0, keepdims=True)
+    back = dot_nn(grad_pre, w_up)
+    out = dot_nn(active, w_down)
+
+    @pl.when(step == 0)
+    def _():
+        back_sum[...] = back
+        out_sum[...] = out
+
+    @pl.when(step > 0)
+    def _():
+        back_sum[...] += back
+        out_sum[...] += out
+
+    @pl.when(step == pl.num_programs(0) - 1)
+    def _():
+        back_ref[...] = back_sum[...].astype(jnp.bfloat16)
+        out_ref[...] = out_sum[...].astype(jnp.bfloat16)
+
+
+def feed_forward(weights, bias_row, second, grad, unit):
+    parts, copies, per, depth = weights.shape
+    rows = second.shape[0]
+    width = parts * copies * unit
+    take = 2 if parts % 2 == 0 else 1
+    hidden = take * copies * unit
+    whole = pl.BlockSpec((rows, depth), lambda step: (0, 0))
+    column = pl.BlockSpec((rows, hidden), lambda step: (0, step))
+    line = pl.BlockSpec((1, hidden), lambda step: (0, step))
+    return pl.pallas_call(
+        functools.partial(feed_kernel, unit=unit),
+        grid=(parts // take,),
+        in_specs=[
+            pl.BlockSpec((take, copies, per, depth), lambda step: (step, 0, 0, 0)),
+            line, whole, whole,
+        ],
+        out_specs=[column, column, whole, whole, line],
+        out_shape=[
+            jax.ShapeDtypeStruct((rows, width), jnp.bfloat16),
+            jax.ShapeDtypeStruct((rows, width), jnp.bfloat16),
+            jax.ShapeDtypeStruct((rows, depth), jnp.bfloat16),
+            jax.ShapeDtypeStruct((rows, depth), jnp.bfloat16),
+            jax.ShapeDtypeStruct((1, width), jnp.float32),
+        ],
+        scratch_shapes=[
+            pltpu.VMEM((rows, depth), jnp.float32),
+            pltpu.VMEM((rows, depth), jnp.float32),
+        ],
+        compiler_params=pltpu.CompilerParams(
+            dimension_semantics=("arbitrary",), vmem_limit_bytes=56 * 1024 * 1024
+        ),
+        cost_estimate=pl.CostEstimate(
+            flops=8 * rows * width * depth, bytes_accessed=8 * rows * depth + 4 * width * depth,
+            transcendentals=2 * rows * width,
+        ),
+        name="feed_forward",
+    )(weights, bias_row, second, grad)
+
+
+def weight_grad_kernel(
+    act_a, act_b, pre_a, pre_b, second_a, second_b, grad_a, grad_b, out_ref
+):
+    _, copies, _, unit, depth = out_ref.shape
+    up = dot_tn(pre_a[...], second_a[...]) + dot_tn(pre_b[...], second_b[...])
+    out_ref[0, :, 0] = up.astype(jnp.bfloat16).reshape(copies, unit, depth)
+    down = dot_tn(act_a[...], grad_a[...]) + dot_tn(act_b[...], grad_b[...])
+    out_ref[0, :, 1] = down.astype(jnp.bfloat16).reshape(copies, unit, depth)
+
+
+def weight_grads(acts, pres, seconds, grads, parts, copies):
+    rows, width = acts[0].shape
+    depth = seconds[0].shape[1]
+    unit = width // (parts * copies)
+    column = pl.BlockSpec((rows, width // parts), lambda step: (0, step))
+    whole = pl.BlockSpec((rows, depth), lambda step: (0, 0))
+    return pl.pallas_call(
+        weight_grad_kernel,
+        grid=(parts,),
+        in_specs=[column] * 4 + [whole] * 4,
+        out_specs=pl.BlockSpec((1, copies, 2, unit, depth), lambda step: (step, 0, 0, 0, 0)),
+        out_shape=jax.ShapeDtypeStruct((parts, copies, 2, unit, depth), jnp.bfloat16),
+        compiler_params=pltpu.CompilerParams(
+            dimension_semantics=("arbitrary",), vmem_limit_bytes=56 * 1024 * 1024
+        ),
+        cost_estimate=pl.CostEstimate(
+            flops=8 * rows * width * depth, bytes_accessed=16 * rows * depth + 4 * width * depth,
+            transcendentals=0,
+        ),
+        name="weight_grads",
+    )(*acts, *pres, *seconds, *grads)
+
+
 def body(
-    tokens,
-    seg_ids,
-    bucket_of,
-    ln1_gain,
-    ln1_bias,
-    w_qkv,
-    rel_table,
-    w_out,
-    ln2_gain,
-    ln2_bias,
-    w_up,
-    up_bias,
-    w_down,
-    down_bias,
-    out_grad,
+    tokens, seg_ids, bucket_of, ln1_gain, ln1_bias, w_qkv, rel_table, w_out,
+    ln2_gain, ln2_bias, w_up, up_bias, w_down, down_bias, out_grad,
 ):
+    low = jnp.bfloat16
+    wide = jnp.float32
+    copies = lax.axis_size("copy")
+    parts = lax.axis_size("mp")
+    copy = lax.axis_index("copy")
+    member = lax.axis_index("team")
+    part = lax.axis_index("mp")
+    core = member % 2
+    rows, depth = tokens.shape
+    heads = rel_table.shape[1]
+    head_width = w_out.shape[0]
+    team_units = w_up.shape[1] // TEAM
+    unit = team_units // copies
     seg_row = seg_ids[0]
-    group_len = seg_row.shape[0]
-    part_rows = tokens.shape[0]
-    model_width = tokens.shape[1]
-    local_heads = rel_table.shape[1]
-    head_size = w_out.shape[0] // local_heads
-    score_scale = head_size ** (-0.5)
-    x_part = tokens.astype(jnp.float32)
-    normed = lax.all_gather(
-        layer_norm(x_part, ln1_gain, ln1_bias).astype(jnp.bfloat16), "mp", axis=0, tiled=True
-    )
-    queries, keys_all, values_all = [
-        jnp.dot(normed, w_qkv[slot_index], preferred_element_type=jnp.float32).astype(jnp.bfloat16)
-        for slot_index in range(3)
-    ]
-    queries = queries * jnp.asarray(score_scale, jnp.bfloat16)
+
+    x_part = tokens.astype(wide)
+    unit1, inverse1 = normalize(x_part)
+    normed, rights = chain_gather((unit1 * ln1_gain + ln1_bias).astype(low))
+
+    spot = member * team_units + copy * unit
+    out_rows = head_width // (2 * copies)
+    piece = jnp.concatenate(
+        [
+            jnp.transpose(lax.dynamic_slice_in_dim(w_up, spot, unit, 1)),
+            lax.dynamic_slice_in_dim(w_down, spot, unit, 0),
+            lax.dynamic_slice_in_dim(w_out, (copy * 2 + core) * out_rows, out_rows, 0),
+        ],
+        axis=0,
+    )
+    piece = lax.optimization_barrier((piece, rights[TIE]))[0]
+    weights = lax.all_gather(piece, ("mp", "copy"), axis=0, tiled=False).reshape(
+        parts, copies, piece.shape[0], depth
+    )
+    own_out = weights[:, :, 2 * unit :, :]
+    other_out = flip(own_out, "team", 1)
+    is_first = core == 0
+    w_out_full = jnp.stack(
+        [jnp.where(is_first, own_out, other_out), jnp.where(is_first, other_out, own_out)], axis=2
+    ).reshape(parts, head_width, depth)
+    bias_all = up_bias[None]
+    for bit in bits_of(parts):
+        bias_all = double(bias_all, "mp", bit).reshape(-1, up_bias.shape[0])
+    bias_row = lax.dynamic_slice_in_dim(bias_all, member * team_units, team_units, 1).reshape(1, -1)
+    grad_near, grad_far = team_gather(out_grad)
+
+    w_cat = jnp.transpose(w_qkv, (1, 0, 2)).reshape(depth, -1)
+    projected = jnp.dot(normed, w_cat, preferred_element_type=wide).astype(low)
     hot, by_distance = distance_bias(rel_table, bucket_of)
     forward_bias, backward_bias = near_tables(by_distance)
     cut = jnp.sum((seg_row == seg_row[0]).astype(jnp.int32)).reshape(1)
-    attended, logs = attention_forward(cut, queries, keys_all, values_all, forward_bias)
-    branch = lax.psum_scatter(
-        jnp.dot(attended, w_out, preferred_element_type=jnp.float32).astype(jnp.bfloat16),
-        "mp",
-        scatter_dimension=0,
-        tiled=True,
-    ).astype(jnp.float32)
+    attended, logs = attention_forward(cut, projected, forward_bias)
+    own_rows = swap_over_chain(attended.reshape(parts, rows, head_width))
+    branch = jnp.einsum("jtc,jcd->td", own_rows, w_out_full, preferred_element_type=wide)
     hidden_in = x_part + branch
-    second = lax.all_gather(
-        layer_norm(hidden_in, ln2_gain, ln2_bias).astype(jnp.bfloat16), "mp", axis=0, tiled=True
-    )
-    pre_act = jnp.dot(second, w_up, preferred_element_type=jnp.float32) + up_bias
-    activated, gelu_pull = jax.vjp(gelu_exact, pre_act)
-    activated_low = activated.astype(jnp.bfloat16)
-    ff_part = lax.psum_scatter(
-        jnp.dot(activated_low, w_down, preferred_element_type=jnp.float32).astype(jnp.bfloat16),
-        "mp",
-        scatter_dimension=0,
-        tiled=True,
-    ).astype(jnp.float32)
-    layer_out = (hidden_in + ff_part + down_bias).astype(jnp.bfloat16)
-    grad_part = out_grad.astype(jnp.float32)
-    grad_rows = lax.all_gather(out_grad, "mp", axis=0, tiled=True)
-    grad_down = jnp.einsum(
-        "tf,td->fd", activated_low, grad_rows, preferred_element_type=jnp.float32
-    )
-    grad_act = jnp.einsum("td,fd->tf", grad_rows, w_down, preferred_element_type=jnp.float32)
-    grad_pre = gelu_pull(grad_act)[0].astype(jnp.bfloat16)
-    second_back = lax.all_gather(
-        layer_norm(hidden_in, ln2_gain, ln2_bias).astype(jnp.bfloat16), "mp", axis=0, tiled=True
-    )
-    grad_up = jnp.einsum("td,tf->df", second_back, grad_pre, preferred_element_type=jnp.float32)
-    grad_up_bias = jnp.sum(grad_pre, axis=0, dtype=jnp.float32)
-    grad_second = lax.psum_scatter(
-        jnp.einsum("tf,df->td", grad_pre, w_up, preferred_element_type=jnp.float32).astype(
-            jnp.bfloat16
-        ),
-        "mp",
-        scatter_dimension=0,
-        tiled=True,
-    ).astype(jnp.float32)
-    norm2_value, norm2_pull = jax.vjp(layer_norm, hidden_in, ln2_gain, ln2_bias)
-    grad_from_norm, grad_ln2_gain, grad_ln2_bias = norm2_pull(grad_second)
-    grad_hidden = grad_part + grad_from_norm
-    grad_branch = lax.all_gather(grad_hidden.astype(jnp.bfloat16), "mp", axis=0, tiled=True)
-    grad_wout = jnp.einsum("tc,td->cd", attended, grad_branch, preferred_element_type=jnp.float32)
-    grad_att = jnp.einsum(
-        "td,cd->tc", grad_branch, w_out, preferred_element_type=jnp.float32
-    ).astype(jnp.bfloat16)
-    grad_queries, grad_keys, grad_values, table_sums = attention_backward(
-        cut, queries, keys_all, values_all, grad_att, attended, logs, backward_bias
-    )
-    grad_table = table_gradient(hot, table_sums, local_heads)
-    grad_proj = [grad_queries, grad_keys, grad_values]
-    normed_back = lax.all_gather(
-        layer_norm(x_part, ln1_gain, ln1_bias).astype(jnp.bfloat16), "mp", axis=0, tiled=True
-    )
-    grad_qkv = jnp.stack(
-        [
-            jnp.einsum("tc,td->cd", normed_back, grad_one, preferred_element_type=jnp.float32)
-            for grad_one in grad_proj
-        ]
-    )
-    running = jnp.zeros((part_rows * lax.axis_size("mp"), model_width), jnp.float32)
-    for slot_index in range(3):
-        running = running + jnp.einsum(
-            "td,cd->tc",
-            grad_proj[slot_index],
-            w_qkv[slot_index],
-            preferred_element_type=jnp.float32,
+    unit2, inverse2 = normalize(hidden_in)
+    second = (unit2 * ln2_gain + ln2_bias).astype(low)
+    second_near, second_far = team_gather(second)
+
+    act_near, pre_near, back_near, feed_near, sums_near = feed_forward(
+        weights, bias_row, second_near, grad_near, unit
+    )
+    act_far, pre_far, back_far, feed_far, sums_far = feed_forward(
+        weights, bias_row, second_far, grad_far, unit
+    )
+    beside = flip(back_near[rows:], "team", 1)
+    onward = back_far[:rows].astype(wide) + flip(back_far[rows:], "team", 1).astype(wide)
+    across = flip(onward.astype(low), "team", 2)
+    grad_second = back_near[:rows].astype(wide) + beside.astype(wide) + across.astype(wide)
+    grad_part = out_grad.astype(wide)
+    grad_hidden = grad_part + normalize_backward(grad_second, ln2_gain, unit2, inverse2)
+    grad_branch = grad_hidden.astype(low)
+    grad_stack = jnp.einsum("td,jcd->jtc", grad_branch, w_out_full, preferred_element_type=wide)
+    grad_att = swap_over_chain(grad_stack.astype(low)).reshape(parts * rows, head_width)
+
+    ff_grads = weight_grads(
+        (act_near, act_far), (pre_near, pre_far), (second_near, second_far),
+        (grad_near, grad_far), parts, copies,
+    )
+    ff_piece = lax.psum_scatter(
+        ff_grads.reshape(parts * copies, 2 * unit, depth), ("mp", "copy"),
+        scatter_dimension=0, tiled=False,
+    )
+    ff_all = lax.all_gather(ff_piece, ("team", "copy"), axis=0, tiled=False).reshape(
+        TEAM * copies, 2, unit, depth
+    )
+    grad_up = jnp.transpose(ff_all[:, 0].reshape(TEAM * team_units, depth)).astype(wide)
+    grad_down = ff_all[:, 1].reshape(TEAM * team_units, depth).astype(wide)
+
+    beside = flip(jnp.stack([feed_far[rows:], feed_near[rows:]]), "team", 1)
+    onward = feed_far[:rows].astype(wide) + beside[0].astype(wide)
+    feed_own = (
+        feed_near[:rows].astype(wide) + beside[1].astype(wide)
+        + flip(onward.astype(low), "team", 2).astype(wide)
+    )
+    layer_out = (hidden_in + feed_own + down_bias).astype(low)
+
+    wout_grad = jnp.einsum("jtc,td->jcd", own_rows, grad_branch, preferred_element_type=wide)
+    wout_grad = wout_grad.astype(low).reshape(parts, 2, 2, copies, -1, depth)
+    wout_grad = halve(halve(wout_grad, 1, "team", 1), 1, "team", 2)
+    for bit in reversed(bits_of(copies)):
+        wout_grad = halve(
+            wout_grad.reshape((parts, 2, -1) + wout_grad.shape[2:]), 1, "copy", bit
         )
-    grad_first = lax.psum_scatter(
-        running.astype(jnp.bfloat16), "mp", scatter_dimension=0, tiled=True
-    ).astype(jnp.float32)
-    norm1_value, norm1_pull = jax.vjp(layer_norm, x_part, ln1_gain, ln1_bias)
-    grad_from_first, grad_ln1_gain, grad_ln1_bias = norm1_pull(grad_first)
-    grad_tokens = (grad_hidden + grad_from_first).astype(jnp.bfloat16)
-    grad_down_bias = jnp.sum(grad_part, axis=0)
-    grad_qkv, grad_table, grad_wout, grad_up, grad_up_bias, grad_down = lax.psum(
-        (grad_qkv, grad_table, grad_wout, grad_up, grad_up_bias, grad_down), "dp"
-    )
-    grad_ln1_gain, grad_ln1_bias, grad_ln2_gain, grad_ln2_bias, grad_down_bias = lax.psum(
-        (grad_ln1_gain, grad_ln1_bias, grad_ln2_gain, grad_ln2_bias, grad_down_bias), ("dp", "mp")
+    wout_grad = wout_grad.reshape(parts, -1, depth)
+    for bit in reversed(bits_of(parts)):
+        wout_grad = halve(wout_grad.reshape((2, -1) + wout_grad.shape[1:]), 0, "mp", bit)
+    wout_grad = wout_grad.reshape(-1, depth)
+
+    dqkv, table_sums = attention_backward(
+        cut, projected, grad_att, attended, logs, backward_bias
+    )
+    running = lax.dot_general(
+        dqkv, w_cat, (((1,), (1,)), ((), ())), preferred_element_type=wide
+    ).astype(low)
+    grad_first = chain_scatter(running)
+    grad_first_norm = normalize_backward(grad_first, ln1_gain, unit1, inverse1)
+    grad_tokens = (grad_hidden + grad_first_norm).astype(low)
+
+    qkv_grad = dot_tn(normed, dqkv).astype(low)
+    qkv_grad = qkv_grad.reshape(2, 2, copies, -1, qkv_grad.shape[1])
+    qkv_grad = halve(halve(qkv_grad, 0, "team", 1), 0, "team", 2)
+    for bit in reversed(bits_of(copies)):
+        qkv_grad = halve(qkv_grad.reshape((2, -1) + qkv_grad.shape[1:]), 0, "copy", bit)
+    qkv_grad = qkv_grad.reshape(-1, 3 * head_width)
+    flat = jnp.concatenate([qkv_grad.reshape(-1, head_width), wout_grad.reshape(-1, head_width)])
+    for bit in bits_of(copies):
+        flat = double(flat, "copy", bit)
+    flat = double(double(flat, "team", 2), "team", 1)
+    flat = flat.reshape(TEAM * copies, -1, head_width)
+    qkv_rows = qkv_grad.shape[0] * 3
+    grad_qkv = jnp.transpose(
+        flat[:, :qkv_rows].reshape(depth, 3, head_width), (1, 0, 2)
+    ).astype(wide)
+    grad_wout = flat[:, qkv_rows:].reshape(head_width, depth).astype(wide)
+
+    running_wide = running.astype(wide)
+    unit_all = (normed.astype(wide) - ln1_bias) / ln1_gain
+    sums = (sums_near + sums_far).reshape(parts, team_units)
+    up_sums = lax.dynamic_update_slice_in_dim(
+        jnp.zeros((parts, TEAM * team_units), wide), sums, member * team_units, 1
+    )
+    table_line = table_gradient(hot, table_sums, heads).reshape(1, -1)
+    table_all = lax.dynamic_update_slice_in_dim(
+        jnp.zeros((parts, table_line.shape[1]), wide), table_line, part, 0
+    )
+    lines = [
+        jnp.sum(running_wide * unit_all, axis=0), jnp.sum(running_wide, axis=0),
+        jnp.sum(grad_second * unit2, axis=0), jnp.sum(grad_second, axis=0),
+        jnp.sum(grad_part, axis=0),
+    ]
+    small = jnp.concatenate(lines + [up_sums.reshape(-1), table_all.reshape(-1)])
+    small = jnp.pad(small, (0, -small.shape[0] % 1024)).reshape(-1, 1024)
+    for axis, size in (("team", TEAM), ("copy", copies), ("mp", parts)):
+        for bit in bits_of(size):
+            small = small + flip(small, axis, bit)
+    small = small.reshape(-1)
+    lines = [small[index * depth : (index + 1) * depth] for index in range(5)]
+    start = 5 * depth
+    count = TEAM * team_units
+    up_sums = small[start : start + parts * count].reshape(parts, count)
+    grad_up_bias = lax.dynamic_index_in_dim(up_sums, part, 0, keepdims=False)
+    start = start + parts * count
+    count = rel_table.size
+    table_all = small[start : start + parts * count].reshape(parts, count)
+    grad_table = lax.dynamic_index_in_dim(table_all, part, 0, keepdims=False).reshape(
+        rel_table.shape
     )
     return (
-        layer_out,
-        grad_tokens,
-        grad_ln1_gain,
-        grad_ln1_bias,
-        grad_qkv,
-        grad_table,
-        grad_wout,
-        grad_ln2_gain,
-        grad_ln2_bias,
-        grad_up,
-        grad_up_bias,
-        grad_down,
-        grad_down_bias,
+        layer_out, grad_tokens, lines[0], lines[1], grad_qkv, grad_table, grad_wout,
+        lines[2], lines[3], grad_up, grad_up_bias, grad_down, lines[4],
     )
 
 
 def solution(mesh):
+    groups, parts = mesh.shape["dp"], mesh.shape["mp"]
+    split = Mesh(
+        mesh.devices.reshape(groups // TEAM, TEAM, parts), ("copy", "team", "mp")
+    )
+    every = ("copy", "team", "mp")
     return jax.shard_map(
         body,
-        mesh=mesh,
+        mesh=split,
         in_specs=(
-            P(("dp", "mp"), None),
-            P("dp", None),
-            P(),
-            P(),
-            P(),
-            P(None, None, "mp"),
-            P(None, "mp"),
-            P("mp", None),
-            P(),
-            P(),
-            P(None, "mp"),
-            P("mp"),
-            P("mp", None),
-            P(),
-            P(("dp", "mp"), None),
+            P(every, None), P(("copy", "team"), None), P(), P(), P(), P(None, None, "mp"),
+            P(None, "mp"), P("mp", None), P(), P(), P(None, "mp"), P("mp"), P("mp", None), P(),
+            P(every, None),
         ),
         out_specs=(
-            P(("dp", "mp"), None),
-            P(("dp", "mp"), None),
-            P(),
-            P(),
-            P(None, None, "mp"),
-            P(None, "mp"),
-            P("mp", None),
-            P(),
-            P(),
-            P(None, "mp"),
-            P("mp"),
-            P("mp", None),
-            P(),
+            P(every, None), P(every, None), P(), P(), P(None, None, "mp"), P(None, "mp"),
+            P("mp", None), P(), P(), P(None, "mp"), P("mp"), P("mp", None), P(),
         ),
         check_vma=False,
     )

time: 824 us -> 553 us (0.67)
  waiting for transfers between devices: 565 us -> 237 us
  starting transfers between devices: 1.3 us -> 69.4 us
  matrix products: 75.7 us -> 20.7 us
  blocking collectives: 54.5 us -> 0 us
  local copies, waits for them, and re-layouts: 19.6 us -> 58.8 us
  Pallas kernels: 53.4 us -> 87 us
  other arithmetic: 33 us -> 56.5 us
    all_gather x4 -> x2, waiting for transfers between devices: 244 us -> 0.02 us  [the longest x1 0.02 us: body(): lax.all_gather(piece, ('mp', 'copy'), axis=0, tiled=False)]
    ppermute x0 -> x48, waiting for transfers between devices: none -> 237 us  [the longest x3 97.6 us: chain_gather(): lax.ppermute(left, 'mp', [(i, i - 1) for i in range(1, size - step + 1)])]
    reduce_scatter x4 -> x1, waiting for transfers between devices: 188 us -> 0.01 us  [body(): lax.psum_scatter(ff_grads.reshape(parts * copies, 2 * unit, depth), ('mp'...]
    psum x1 -> x0, waiting for transfers between devices: 132 us -> none  [body(): lax.psum((grad_qkv, grad_table, grad_wout, grad_up, grad_up_bias, grad_do...]
    ppermute x0 -> x48, starting transfers between devices: none -> 69.2 us  [the longest x30 38.9 us: flip(): return lax.ppermute(value, axis, [(i, i ^ bit) for i in range(size)])]
    dot_general x18 -> x6, matrix products: 75.3 us -> 20.2 us  [the longest x1 6.72 us: body(): lax.dot_general(dqkv, w_cat, (((1,), (1,)), ((), ())), preferred_element_...]
    psum x2 -> x0, blocking collectives: 54.5 us -> none  [the longest x1 41.5 us: body(): lax.psum((grad_ln1_gain, grad_ln1_bias, grad_ln2_gain, grad_ln2_bias, gra...]
    pallas_call x0 -> x3, Pallas kernels: none -> 38.7 us  [the longest x2 26.8 us: feed_forward(): pl.pallas_call(functools.partial(feed_kernel, unit=unit), grid=(parts //...]
  transfers between devices with their start and end apart: 9 -> 51, of which waited for: 9 -> 24; matrix products, arithmetic and copies ran while one was open for 6% -> 19% of each run, Pallas kernels for 0% -> 14%
where the time goes in v2:
time: 553 us; the launch traced here: 544 us
  waiting for transfers between devices  237 us (43%)
  Pallas kernels  87 us (16%)
  starting transfers between devices  69.4 us (13%)
  local copies, waits for them, and re-layouts  58.8 us (11%)
  other arithmetic  56.5 us (10%)
  matrix products  20.7 us (4%)
  between operations  15.3 us (3%)
    ppermute x3, waiting for transfers between devices, chain_gather(): lax.ppermute(left, 'mp', [(i, i - 1) for i in range(1, size - step + 1)])  97.6 us
    ppermute x30, waiting for transfers between devices, flip(): return lax.ppermute(value, axis, [(i, i ^ bit) for i in range(size)])  71.6 us
    ppermute x30, starting transfers between devices, flip(): return lax.ppermute(value, axis, [(i, i ^ bit) for i in range(size)])  38.9 us
    pallas_call x1, Pallas kernels, attention_backward(): pl.pallas_call(attention_backward_kernel, grid_spec=pltpu.PrefetchScalarG...  31.8 us
    ppermute x6, waiting for transfers between devices, swap_over_chain(): lax.ppermute(send, 'mp', [(i, (i + step) % size) for i in range(size)])  30.4 us
    pallas_call x2, Pallas kernels, feed_forward(): pl.pallas_call(functools.partial(feed_kernel, unit=unit), grid=(parts //...  26.8 us
    unnamed x100, local copies, waits for them, and re-layouts  22.6 us
    pallas_call x1, Pallas kernels, attention_forward(): pl.pallas_call(attention_forward_kernel, grid_spec=pltpu.PrefetchScalarGr...  16.6 us
  transfers between devices with their start and end apart: 51, of which 24 were waited for; matrix products, arithmetic and copies ran while one was open for 19% of the time, Pallas kernels for 14%

profile of v2, /device:TPU:0, one launch (start us, length us, event | category | flops | bytes accessed | tf_op | source)
XLA Modules:
  0.0 544.3 jit_solution(9484941863643094111)
XLA Ops:
  14.3 5.0 collective-permute-start
  22.4 13.9 %collective-permute-done = bf16[384,1024]{1,0:T(8,128)(2,1)S(1)} collective-permute-done((bf16[384,1024]{1,0:T(8,128)(2,1)}, bf16[384,1024]{1,0:T(8,128)(2,1)S(1)}, u32[]{:S(2)}, u32[]{:S(2)}) %collective-permute-start) | collective-permute-done | bytes 786464 | tf_op jit(solution)/shard_map/ppermute | solution.py:409
  37.7 38.6 %collective-permute-done.1 = bf16[384,1024]{1,0:T(8,128)(2,1)S(1)} collective-permute-done((bf16[384,1024]{1,0:T(8,128)(2,1)}, bf16[384,1024]{1,0:T(8,128)(2,1)S(1)}, u32[]{:S(2)}, u32[]{:S(2)}) %collective-permute-start.1) | collective-permute-done | bytes 786464 | tf_op jit(solution)/shard_map/ppermute | solution.py:410
  79.1 41.1 %collective-permute-done.2 = bf16[384,1024]{1,0:T(8,128)(2,1)} collective-permute-done((bf16[384,1024]{1,0:T(8,128)(2,1)S(1)}, bf16[384,1024]{1,0:T(8,128)(2,1)}, u32[]{:S(2)}, u32[]{:S(2)}) %collective-permute-start.2) | collective-permute-done | bytes 786464 | tf_op jit(solution)/shard_map/ppermute | solution.py:410
  123.1 8.4 %collective-permute-start.10 = (f32[1,1024]{1,0:T(1,128)S(1)}, f32[1,1024]{1,0:T(1,128)S(1)}, u32[]{:S(2)}, u32[]{:S(2)}) collective-permute-start(f32[1,1024]{1,0:T(1,128)S(1)} %bitcast.158), channel_id=1, source_target_pairs={{0,1},{1,0},{2,3},{3,2},{4,5},{5,4},{6,7},{7,6},{8,9},{9,8},{10,11... | collective-permute-start | bytes 12296 | tf_op jit(solution)/shard_map/ppermute | solution.py:374
  132.1 1.8 copy.55
  136.7 17.9 %collective-permute-done.3 = bf16[384,1024]{1,0:T(8,128)(2,1)} collective-permute-done((bf16[384,1024]{1,0:T(8,128)(2,1)}, bf16[384,1024]{1,0:T(8,128)(2,1)}, u32[]{:S(2)}, u32[]{:S(2)}) %collective-permute-start.3) | collective-permute-done | bytes 786464 | tf_op jit(solution)/shard_map/ppermute | solution.py:410
  154.6 2.3 add_dynamic-update-slice_fusion.2
  156.9 2.6 add_dynamic-update-slice_fusion.1
  161.1 4.6 convolution_convert_fusion.1.qkv_ref
  165.7 3.1 slice.134
  168.8 16.6 %attention_forward.1 = (bf16[1536,256]{1,0:T(8,128)(2,1)S(1)}, f32[8,1536]{1,0:T(8,128)S(1)}) custom-call(s32[1]{0:T(128)} %bitcast.1.cut_ref, bf16[1536,768]{1,0:T(8,128)(2,1)S(1)} %convolution_convert_fusion.1.qkv_ref, f32[8,512]{1,0:T(8,128)S(1)} %select_maximum_fusion.1.bias_ref), custom_call_target="tpu_custom_call" | custom-call | flops 4831838208 | bytes 3145728 | tf_op jit(solution)/shard_map/attention_forward/pallas_call | solution.py:135
  186.3 2.1 constant_dynamic-update-slice_fusion.1
  189.2 13.1 %collective-permute-done.6 = bf16[1,384,256]{1,2,0:T(8,128)(2,1)S(1)} collective-permute-done((bf16[1,384,256]{1,2,0:T(8,128)(2,1)S(1)}, bf16[1,384,256]{1,2,0:T(8,128)(2,1)S(1)}, u32[]{:S(2)}, u32[]{:S(2)}) %collective-permute-start.6) | collective-permute-done | bytes 196640 | tf_op jit(solution)/shard_map/ppermute | solution.py:453
  203.1 6.7 %collective-permute-done.8 = bf16[1,384,256]{1,2,0:T(8,128)(2,1)S(1)} collective-permute-done((bf16[1,384,256]{1,2,0:T(8,128)(2,1)S(1)}, bf16[1,384,256]{1,2,0:T(8,128)(2,1)S(1)}, u32[]{:S(2)}, u32[]{:S(2)}) %collective-permute-start.8) | collective-permute-done | bytes 196640 | tf_op jit(solution)/shard_map/ppermute | solution.py:453
  215.9 2.8 collective-permute-start.14
  221.9 1.8 constant_dynamic-update-slice_fusion.4.grad_ref.grad_b
  223.6 12.3 %collective-permute-done.14 = bf16[384,1024]{1,0:T(8,128)(2,1)} collective-permute-done((bf16[384,1024]{1,0:T(8,128)(2,1)}, bf16[384,1024]{1,0:T(8,128)(2,1)}, u32[]{:S(2)}, u32[]{:S(2)}) %collective-permute-start.14) | collective-permute-done | bytes 786464 | tf_op jit(solution)/shard_map/ppermute | solution.py:374
  237.1 2.7 pad_maximum_fusion.1.second_ref.second_a
  239.8 13.4 %feed_forward.2 = (bf16[768,1024]{1,0:T(8,128)(2,1)}, bf16[768,1024]{1,0:T(8,128)(2,1)}, bf16[768,1024]{1,0:T(8,128)(2,1)}, bf16[768,1024]{1,0:T(8,128)(2,1)}, f32[1,1024]{1,0:T(1,128)}) custom-call(bf16[4,2,320,1024]{3,2,1,0:T(8,128)(2,1)} %bitcast.149, f32[1,1024]{1,0:T(1,128)} %bitcast.161, bf16[768,1024]{1,0:T(8,128)(2,1)} %pad_maximum_fusion.1.second_ref.second_a, ...), custom_call_target="tpu_custom_call" | custom-call | flops 6442450944 | bytes 10485760 | tf_op jit(solution)/shard_map/feed_forward/pallas_call | solution.py:534
  255.7 13.4 %feed_forward.3 = (bf16[768,1024]{1,0:T(8,128)(2,1)}, bf16[768,1024]{1,0:T(8,128)(2,1)}, bf16[768,1024]{1,0:T(8,128)(2,1)}, bf16[768,1024]{1,0:T(8,128)(2,1)}, f32[1,1024]{1,0:T(1,128)}) custom-call(bf16[4,2,320,1024]{3,2,1,0:T(8,128)(2,1)} %bitcast.150, f32[1,1024]{1,0:T(1,128)} %bitcast.162, bf16[768,1024]{1,0:T(8,128)(2,1)} %copy-done.27, ...), custom_call_target="tpu_custom_call" | custom-call | flops 6442450944 | bytes 10485760 | tf_op jit(solution)/shard_map/feed_forward/pallas_call | solution.py:534
  274.7 11.8 %weight_grads.1 = bf16[4,2,2,128,1024]{4,3,2,1,0:T(8,128)(2,1)} custom-call(bf16[768,1024]{1,0:T(8,128)(2,1)} %get-tuple-element.39.act_a, bf16[768,1024]{1,0:T(8,128)(2,1)} %get-tuple-element.40.act_b, bf16[768,1024]{1,0:T(8,128)(2,1)} %get-tuple-element.41.pre_a, bf16[768,1024]{1,0:T(8,128)(2,1)} %get-tuple-element.42.pre_b, ...), custom_call_target="tpu_custom_call" | custom-call | flops 6442450944 | bytes 16777216 | tf_op jit(solution)/shard_map/weight_grads/pallas_call | solution.py:580
  286.8 2.6 add_convert_fusion.4
  291.8 2.6 fusion.16
  294.7 15.3 %collective-permute-done.22 = bf16[384,1024]{1,0:T(8,128)(2,1)} collective-permute-done((bf16[384,1024]{1,0:T(8,128)(2,1)}, bf16[384,1024]{1,0:T(8,128)(2,1)}, u32[]{:S(2)}, u32[]{:S(2)}) %collective-permute-start.22) | collective-permute-done | bytes 786464 | tf_op jit(solution)/shard_map/ppermute | solution.py:374
  310.0 2.6 multiply_reduce_fusion
  312.6 13.8 %collective-permute-done.19 = bf16[384,1024]{1,0:T(8,128)(2,1)} collective-permute-done((bf16[384,1024]{1,0:T(8,128)(2,1)}, bf16[384,1024]{1,0:T(8,128)(2,1)}, u32[]{:S(2)}, u32[]{:S(2)}) %collective-permute-start.19) | collective-permute-done | bytes 786464 | tf_op jit(solution)/shard_map/ppermute | solution.py:374
  326.5 3.9 convert_add_fusion.2
  331.8 2.9 collective-permute-start.24
  338.3 9.1 %collective-permute-done.23 = bf16[1,384,256]{1,2,0:T(8,128)(2,1)S(1)} collective-permute-done((bf16[1,384,256]{1,2,0:T(8,128)(2,1)S(1)}, bf16[1,384,256]{1,2,0:T(8,128)(2,1)S(1)}, u32[]{:S(2)}, u32[]{:S(2)}) %collective-permute-start.23) | collective-permute-done | bytes 196640 | tf_op jit(solution)/shard_map/ppermute | solution.py:453
  350.1 31.8 %attention_backward.1 = (bf16[1536,768]{1,0:T(8,128)(2,1)}, f32[8,512]{1,0:T(8,128)}) custom-call(s32[1]{0:T(128)} %bitcast.1.cut_ref, bf16[1536,768]{1,0:T(8,128)(2,1)} %copy-done.3, bf16[1536,256]{1,0:T(8,128)(2,1)} %bitcast.151, bf16[1536,256]{1,0:T(8,128)(2,1)} %copy-done.2, f32[8,1536]{1,0:T(8,128)} %copy-done.4, f32[8,512]{1,0:T(8,128)} %select_maximum_fusion.bias_ref), custom_call_target="tpu_custom_call" | custom-call | flops 12079595520 | bytes 6291456 | tf_op jit(solution)/shard_map/attention_backward/pallas_call | solution.py:284
  384.8 5.3 convolution_convert_fusion.3
  392.2 2.2 collective-permute-start.37
  394.4 6.7 %convert_reduce_fusion = (f32[1024]{0:T(1024)S(1)}, f32[1024]{0:T(1024)S(1)}, bf16[1536,1024]{1,0:T(8,128)(2,1)}) fusion(f32[1024]{0:T(1024)S(1)} %copy-done.30, f32[1024]{0:T(1024)S(1)} %copy-done.34, bf16[1536,1024]{1,0:T(8,128)(2,1)} %add_dynamic-update-slice_fusion, bf16[1536,768]{1,0:T(8,128)(2,1)} %get-tuple-element.35, bf16[1024,768]{0,1:T(8,128)(2,1)S(1)} %bitcast.141), kind=kOutput, calls=%fused_computation | convolution fusion | flops 2428499968 | bytes 10240000 | tf_op jit(solution)/shard_map/dot_general | solution.py:712
  402.6 3.4 collective-permute-start.33
  406.0 2.6 collective-permute-done.33
  408.6 1.8 collective-permute-start.34
  410.5 2.5 collective-permute-done.34
  413.0 3.2 collective-permute-start.35
  416.2 2.2 collective-permute-done.35
  418.5 2.2 collective-permute-start.36
  420.7 2.5 constant_dynamic-slice_fusion.5
  423.2 1.9 collective-permute-start.26
  425.2 1.8 collective-permute-start.29
  427.1 1.8 fusion.1
  428.9 1.8 collective-permute-start.41
  432.5 7.0 %collective-permute-done.26 = bf16[384,1024]{1,0:T(8,128)(2,1)S(1)} collective-permute-done((bf16[384,1024]{1,0:T(8,128)(2,1)S(1)}, bf16[384,1024]{1,0:T(8,128)(2,1)S(1)}, u32[]{:S(2)}, u32[]{:S(2)}) %collective-permute-start.26) | collective-permute-done | bytes 786464 | tf_op jit(solution)/shard_map/ppermute | solution.py:437
  439.5 2.3 add_convert_fusion.3
  441.8 4.4 collective-permute-start.27
  446.2 2.2 collective-permute-done.41
  450.4 10.1 %collective-permute-done.38 = bf16[2,128,768]{2,1,0:T(8,128)(2,1)S(1)} collective-permute-done((bf16[2,128,768]{2,1,0:T(8,128)(2,1)S(1)}, bf16[2,128,768]{2,1,0:T(8,128)(2,1)S(1)}, u32[]{:S(2)}, u32[]{:S(2)}) %collective-permute-start.38) | collective-permute-done | bytes 393248 | tf_op jit(solution)/shard_map/ppermute | solution.py:374
  460.6 1.8 collective-permute-start.39
  463.1 5.3 collective-permute-done.39
  470.0 3.4 add_convert_fusion.2
  477.3 3.7 collective-permute-start.28
  483.2 2.6 add_convert_fusion
  488.6 2.2 collective-permute-done.46
  492.1 15.2 %collective-permute-done.31 = bf16[384,1024]{1,0:T(8,128)(2,1)S(1)} collective-permute-done((bf16[384,1024]{1,0:T(8,128)(2,1)}, bf16[384,1024]{1,0:T(8,128)(2,1)S(1)}, u32[]{:S(2)}, u32[]{:S(2)}) %collective-permute-start.31) | collective-permute-done | bytes 786464 | tf_op jit(solution)/shard_map/ppermute | solution.py:440
  511.5 3.0 reshape.245
  514.5 4.5 copy.67
  521.3 4.1 fusion.43
  525.4 2.6 bitcast_convert_fusion.1
  528.0 5.3 copy.71
  533.3 4.2 bitcast_convert_fusion
  (289 shorter events, 82.6 us)
Async XLA Ops:
  7.2 12.1 %copy-start = (bf16[1024,1024]{1,0:T(8,128)(2,1)S(1)}, bf16[1024,1024]{1,0:T(8,128)(2,1)}, u32[]{:S(2)}) copy-start(bf16[1024,1024]{1,0:T(8,128)(2,1)} %param.25) | copy-start | bytes 6291460
  7.2 158.5 %all-gather.6.cloned.1.call-start = ((), (), s32[]{:S(2)}) async-start(), calls=%async_computation.3 | async-start | bytes 5898240 | tf_op jit(solution)/shard_map/all_gather | solution.py:631
  14.3 22.0 %collective-permute-start = (bf16[384,1024]{1,0:T(8,128)(2,1)}, bf16[384,1024]{1,0:T(8,128)(2,1)S(1)}, u32[]{:S(2)}, u32[]{:S(2)}) collective-permute-start(bf16[384,1024]{1,0:T(8,128)(2,1)} %get-tuple-element.91), channel_id=1, source_target_pairs={{0,1},{1,2},{2,3},{4,5},{5,6},{6,7},{8,9},{9,10},{10,11},{12,13},{... | collective-permute-start | bytes 2359304 | tf_op jit(solution)/shard_map/ppermute | solution.py:409
  19.3 103.8 %copy-start.37 = (f32[1024]{0:T(1024)S(1)}, f32[1024]{0:T(1024)}, u32[]{:S(2)}) copy-start(f32[1024]{0:T(1024)} %param.26) | copy-start | bytes 12292
  19.4 112.2 %copy-start.31 = (s32[1,1536]{1,0:T(1,128)S(1)}, s32[1,1536]{1,0:T(1,128)}, u32[]{:S(2)}) copy-start(s32[1,1536]{1,0:T(1,128)} %param.16) | copy-start | bytes 18436
  19.4 112.7 %copy-start.18 = (bf16[3,1024,256]{2,1,0:T(8,128)(2,1)S(1)}, bf16[3,1024,256]{2,1,0:T(8,128)(2,1)}, u32[]{:S(2)}) copy-start(bf16[3,1024,256]{2,1,0:T(8,128)(2,1)} %param.20) | copy-start | bytes 4718596
  36.3 384.4 %reduce-scatter.2.cloned.1.call-start = ((), (), s32[]{:S(2)}) async-start(), calls=%async_computation.1 | async-start | bytes 4718592 | tf_op jit(solution)/shard_map/reduce_scatter | solution.py:679
  36.4 39.9 %collective-permute-start.1 = (bf16[384,1024]{1,0:T(8,128)(2,1)}, bf16[384,1024]{1,0:T(8,128)(2,1)S(1)}, u32[]{:S(2)}, u32[]{:S(2)}) collective-permute-start(bf16[384,1024]{1,0:T(8,128)(2,1)} %get-tuple-element.91), channel_id=1, source_target_pairs={{1,0},{2,1},{3,2},{5,4},{6,5},{7,6},{9,8},{10,9},{11,10},{13,12},{... | collective-permute-start | bytes 2359304 | tf_op jit(solution)/shard_map/ppermute | solution.py:410
  76.3 43.9 %collective-permute-start.2 = (bf16[384,1024]{1,0:T(8,128)(2,1)S(1)}, bf16[384,1024]{1,0:T(8,128)(2,1)}, u32[]{:S(2)}, u32[]{:S(2)}) collective-permute-start(bf16[384,1024]{1,0:T(8,128)(2,1)S(1)} %collective-permute-done.1), channel_id=1, source_target_pairs={{1,0},{2,1},{5,4},{6,5},{9,8},{10,9},{13,12},{14,13},{17,16},{18,1... | collective-permute-start | bytes 2359304 | tf_op jit(solution)/shard_map/ppermute | solution.py:410
  77.6 56.8 %collective-permute-start.4 = (bf16[384,1024]{1,0:T(8,128)(2,1)S(1)}, bf16[384,1024]{1,0:T(8,128)(2,1)}, u32[]{:S(2)}, u32[]{:S(2)}) collective-permute-start(bf16[384,1024]{1,0:T(8,128)(2,1)S(1)} %collective-permute-done), channel_id=1, source_target_pairs={{1,2},{2,3},{5,6},{6,7},{9,10},{10,11},{13,14},{14,15},{17,18},{18... | collective-permute-start | bytes 2359304 | tf_op jit(solution)/shard_map/ppermute | solution.py:409
  120.2 34.4 %collective-permute-start.3 = (bf16[384,1024]{1,0:T(8,128)(2,1)}, bf16[384,1024]{1,0:T(8,128)(2,1)}, u32[]{:S(2)}, u32[]{:S(2)}) collective-permute-start(bf16[384,1024]{1,0:T(8,128)(2,1)} %collective-permute-done.2), channel_id=1, source_target_pairs={{1,0},{5,4},{9,8},{13,12},{17,16},{21,20},{25,24},{29,28}} | collective-permute-start | bytes 2359304 | tf_op jit(solution)/shard_map/ppermute | solution.py:410
  121.5 81.3 %collective-permute-start.16 = (bf16[384,1024]{1,0:T(8,128)(2,1)}, bf16[384,1024]{1,0:T(8,128)(2,1)}, u32[]{:S(2)}, u32[]{:S(2)}) collective-permute-start(bf16[384,1024]{1,0:T(8,128)(2,1)} %param.29), channel_id=1, source_target_pairs={{0,8},{4,12},{8,0},{12,4},{1,9},{5,13},{9,1},{13,5},{2,10},{6,14},... | collective-permute-start | bytes 2359304 | tf_op jit(solution)/shard_map/ppermute | solution.py:374
  123.1 97.5 %collective-permute-start.13 = (bf16[384,1024]{1,0:T(8,128)(2,1)}, bf16[384,1024]{1,0:T(8,128)(2,1)}, u32[]{:S(2)}, u32[]{:S(2)}) collective-permute-start(bf16[384,1024]{1,0:T(8,128)(2,1)} %param.29), channel_id=1, source_target_pairs={{0,4},{4,0},{8,12},{12,8},{1,5},{5,1},{9,13},{13,9},{2,6},{6,2},{1... | collective-permute-start | bytes 2359304 | tf_op jit(solution)/shard_map/ppermute | solution.py:374
  123.1 65.3 %collective-permute-start.10 = (f32[1,1024]{1,0:T(1,128)S(1)}, f32[1,1024]{1,0:T(1,128)S(1)}, u32[]{:S(2)}, u32[]{:S(2)}) collective-permute-start(f32[1,1024]{1,0:T(1,128)S(1)} %bitcast.158), channel_id=1, source_target_pairs={{0,1},{1,0},{2,3},{3,2},{4,5},{5,4},{6,7},{7,6},{8,9},{9,8},{10,11... | collective-permute-start | bytes 12296 | tf_op jit(solution)/shard_map/ppermute | solution.py:374
  134.4 25.0 %collective-permute-start.5 = (bf16[384,1024]{1,0:T(8,128)(2,1)}, bf16[384,1024]{1,0:T(8,128)(2,1)S(1)}, u32[]{:S(2)}, u32[]{:S(2)}) collective-permute-start(bf16[384,1024]{1,0:T(8,128)(2,1)} %collective-permute-done.4), channel_id=1, source_target_pairs={{2,3},{6,7},{10,11},{14,15},{18,19},{22,23},{26,27},{30,31}} | collective-permute-start | bytes 2359304 | tf_op jit(solution)/shard_map/ppermute | solution.py:409
  165.7 19.7 %copy-start.3 = (bf16[1536,768]{1,0:T(8,128)(2,1)}, bf16[1536,768]{1,0:T(8,128)(2,1)S(1)}, u32[]{:S(2)}) copy-start(bf16[1536,768]{1,0:T(8,128)(2,1)S(1)} %convolution_convert_fusion.1.qkv_ref) | copy-start | bytes 7077892
  168.8 41.0 %collective-permute-start.9 = (bf16[4,2,64,1024]{3,2,1,0:T(8,128)(2,1)}, bf16[4,2,64,1024]{3,2,1,0:T(8,128)(2,1)}, u32[]{:S(2)}, u32[]{:S(2)}) collective-permute-start(bf16[4,2,64,1024]{3,2,1,0:T(8,128)(2,1)} %slice.134), channel_id=1, source_target_pairs={{0,4},{4,0},{8,12},{12,8},{1,5},{5,1},{9,13},{13,9},{2,6},{6,2},{1... | collective-permute-start | bytes 3145736 | tf_op jit(solution)/shard_map/ppermute | solution.py:374
  186.2 16.1 %collective-permute-start.6 = (bf16[1,384,256]{1,2,0:T(8,128)(2,1)S(1)}, bf16[1,384,256]{1,2,0:T(8,128)(2,1)S(1)}, u32[]{:S(2)}, u32[]{:S(2)}) collective-permute-start(bf16[1,384,256]{1,2,0:T(8,128)(2,1)S(1)} %copy.73), channel_id=1, source_target_pairs={{0,2},{1,3},{2,0},{3,1},{4,6},{5,7},{6,4},{7,5},{8,10},{9,11},{10,... | collective-permute-start | bytes 589832 | tf_op jit(solution)/shard_map/ppermute | solution.py:453
  188.9 14.0 %collective-permute-start.7 = (bf16[1,384,256]{1,2,0:T(8,128)(2,1)S(1)}, bf16[1,384,256]{1,2,0:T(8,128)(2,1)S(1)}, u32[]{:S(2)}, u32[]{:S(2)}) collective-permute-start(bf16[1,384,256]{1,2,0:T(8,128)(2,1)S(1)} %copy.74), channel_id=1, source_target_pairs={{0,1},{1,2},{2,3},{3,0},{4,5},{5,6},{6,7},{7,4},{8,9},{9,10},{10,1... | collective-permute-start | bytes 589832 | tf_op jit(solution)/shard_map/ppermute | solution.py:453
  202.3 7.5 %collective-permute-start.8 = (bf16[1,384,256]{1,2,0:T(8,128)(2,1)S(1)}, bf16[1,384,256]{1,2,0:T(8,128)(2,1)S(1)}, u32[]{:S(2)}, u32[]{:S(2)}) collective-permute-start(bf16[1,384,256]{1,2,0:T(8,128)(2,1)S(1)} %copy.75), channel_id=1, source_target_pairs={{0,3},{1,0},{2,1},{3,2},{4,7},{5,4},{6,5},{7,6},{8,11},{9,8},{10,9... | collective-permute-start | bytes 589832 | tf_op jit(solution)/shard_map/ppermute | solution.py:453
  202.8 16.0 %collective-permute-start.11 = (f32[2,1024]{1,0:T(2,128)S(1)}, f32[2,1024]{1,0:T(2,128)S(1)}, u32[]{:S(2)}, u32[]{:S(2)}) collective-permute-start(f32[2,1024]{1,0:T(2,128)S(1)} %dynamic_update_slice.88), channel_id=1, source_target_pairs={{0,2},{1,3},{2,0},{3,1},{4,6},{5,7},{6,4},{7,5},{8,10},{9,11},{10,... | collective-permute-start | bytes 24584 | tf_op jit(solution)/shard_map/ppermute | solution.py:374
  202.9 19.0 %collective-permute-start.17 = (bf16[384,1024]{1,0:T(8,128)(2,1)}, bf16[384,1024]{1,0:T(8,128)(2,1)}, u32[]{:S(2)}, u32[]{:S(2)}) collective-permute-start(bf16[384,1024]{1,0:T(8,128)(2,1)} %collective-permute-done.16), channel_id=1, source_target_pairs={{0,4},{4,0},{8,12},{12,8},{1,5},{5,1},{9,13},{13,9},{2,6},{6,2},{1... | collective-permute-start | bytes 2359304 | tf_op jit(solution)/shard_map/ppermute | solution.py:374
  215.9 20.0 %collective-permute-start.14 = (bf16[384,1024]{1,0:T(8,128)(2,1)}, bf16[384,1024]{1,0:T(8,128)(2,1)}, u32[]{:S(2)}, u32[]{:S(2)}) collective-permute-start(bf16[384,1024]{1,0:T(8,128)(2,1)} %add_convert_fusion.5), channel_id=1, source_target_pairs={{0,8},{4,12},{8,0},{12,4},{1,9},{5,13},{9,1},{13,5},{2,10},{6,14},... | collective-permute-start | bytes 2359304 | tf_op jit(solution)/shard_map/ppermute | solution.py:374
  218.7 18.4 %collective-permute-start.12 = (bf16[384,1024]{1,0:T(8,128)(2,1)}, bf16[384,1024]{1,0:T(8,128)(2,1)}, u32[]{:S(2)}, u32[]{:S(2)}) collective-permute-start(bf16[384,1024]{1,0:T(8,128)(2,1)} %add_convert_fusion.5), channel_id=1, source_target_pairs={{0,4},{4,0},{8,12},{12,8},{1,5},{5,1},{9,13},{13,9},{2,6},{6,2},{1... | collective-permute-start | bytes 2359304 | tf_op jit(solution)/shard_map/ppermute | solution.py:374
  221.8 15.3 %copy-start.26 = (bf16[768,1024]{1,0:T(8,128)(2,1)}, bf16[768,1024]{1,0:T(8,128)(2,1)S(1)}, u32[]{:S(2)}) copy-start(bf16[768,1024]{1,0:T(8,128)(2,1)S(1)} %constant_dynamic-update-slice_fusion.grad_ref.grad_a) | copy-start | bytes 4718596
  223.6 12.3 %copy-start.28 = (bf16[768,1024]{1,0:T(8,128)(2,1)}, bf16[768,1024]{1,0:T(8,128)(2,1)S(1)}, u32[]{:S(2)}) copy-start(bf16[768,1024]{1,0:T(8,128)(2,1)S(1)} %constant_dynamic-update-slice_fusion.4.grad_ref.grad_b) | copy-start | bytes 4718596
  235.9 18.5 %collective-permute-start.15 = (bf16[384,1024]{1,0:T(8,128)(2,1)}, bf16[384,1024]{1,0:T(8,128)(2,1)S(1)}, u32[]{:S(2)}, u32[]{:S(2)}) collective-permute-start(bf16[384,1024]{1,0:T(8,128)(2,1)} %collective-permute-done.14), channel_id=1, source_target_pairs={{0,4},{4,0},{8,12},{12,8},{1,5},{5,1},{9,13},{13,9},{2,6},{6,2},{1... | collective-permute-start | bytes 2359304 | tf_op jit(solution)/shard_map/ppermute | solution.py:374
  271.6 20.2 %collective-permute-start.18 = (bf16[2,384,1024]{2,1,0:T(8,128)(2,1)}, bf16[2,384,1024]{2,1,0:T(8,128)(2,1)}, u32[]{:S(2)}, u32[]{:S(2)}) collective-permute-start(bf16[2,384,1024]{2,1,0:T(8,128)(2,1)} %pad_maximum_fusion.2), channel_id=1, source_target_pairs={{0,4},{4,0},{8,12},{12,8},{1,5},{5,1},{9,13},{13,9},{2,6},{6,2},{1... | collective-permute-start | bytes 4718600 | tf_op jit(solution)/shard_map/ppermute | solution.py:374
  273.2 13.5 %collective-permute-start.21 = (bf16[384,1024]{1,0:T(8,128)(2,1)}, bf16[384,1024]{1,0:T(8,128)(2,1)}, u32[]{:S(2)}, u32[]{:S(2)}) collective-permute-start(bf16[384,1024]{1,0:T(8,128)(2,1)} %slice.113), channel_id=1, source_target_pairs={{0,4},{4,0},{8,12},{12,8},{1,5},{5,1},{9,13},{13,9},{2,6},{6,2},{1... | collective-permute-start | bytes 2359304 | tf_op jit(solution)/shard_map/ppermute | solution.py:374
  274.7 20.0 %collective-permute-start.20 = (bf16[384,1024]{1,0:T(8,128)(2,1)}, bf16[384,1024]{1,0:T(8,128)(2,1)}, u32[]{:S(2)}, u32[]{:S(2)}) collective-permute-start(bf16[384,1024]{1,0:T(8,128)(2,1)} %slice.111), channel_id=1, source_target_pairs={{0,4},{4,0},{8,12},{12,8},{1,5},{5,1},{9,13},{13,9},{2,6},{6,2},{1... | collective-permute-start | bytes 2359304 | tf_op jit(solution)/shard_map/ppermute | solution.py:374
  286.5 234.8 %all-gather.4.cloned.1.call-start = ((), (), s32[]{:S(2)}) async-start(), calls=%async_computation.2 | async-start | bytes 4718592 | tf_op jit(solution)/shard_map/all_gather | solution.py:683
  289.3 20.7 %collective-permute-start.22 = (bf16[384,1024]{1,0:T(8,128)(2,1)}, bf16[384,1024]{1,0:T(8,128)(2,1)}, u32[]{:S(2)}, u32[]{:S(2)}) collective-permute-start(bf16[384,1024]{1,0:T(8,128)(2,1)} %add_convert_fusion.4), channel_id=1, source_target_pairs={{0,8},{4,12},{8,0},{12,4},{1,9},{5,13},{9,1},{13,5},{2,10},{6,14},... | collective-permute-start | bytes 2359304 | tf_op jit(solution)/shard_map/ppermute | solution.py:374
  294.3 32.1 %collective-permute-start.19 = (bf16[384,1024]{1,0:T(8,128)(2,1)}, bf16[384,1024]{1,0:T(8,128)(2,1)}, u32[]{:S(2)}, u32[]{:S(2)}) collective-permute-start(bf16[384,1024]{1,0:T(8,128)(2,1)} %fusion.16), channel_id=1, source_target_pairs={{0,8},{4,12},{8,0},{12,4},{1,9},{5,13},{9,1},{13,5},{2,10},{6,14},... | collective-permute-start | bytes 2359304 | tf_op jit(solution)/shard_map/ppermute | solution.py:374
  294.7 31.8 %copy-start.16 = (bf16[768,1024]{1,0:T(8,128)(2,1)S(1)}, bf16[768,1024]{1,0:T(8,128)(2,1)}, u32[]{:S(2)}) copy-start(bf16[768,1024]{1,0:T(8,128)(2,1)} %get-tuple-element.32) | copy-start | bytes 4718596
  294.7 31.8 %copy-start.23 = (bf16[768,1024]{1,0:T(8,128)(2,1)S(1)}, bf16[768,1024]{1,0:T(8,128)(2,1)}, u32[]{:S(2)}) copy-start(bf16[768,1024]{1,0:T(8,128)(2,1)} %get-tuple-element.30) | copy-start | bytes 4718596
  294.7 31.8 %copy-start.33 = (f32[1024]{0:T(1024)S(1)}, f32[1024]{0:T(1024)}, u32[]{:S(2)}) copy-start(f32[1024]{0:T(1024)} %param.28) | copy-start | bytes 12292
  331.7 15.7 %collective-permute-start.23 = (bf16[1,384,256]{1,2,0:T(8,128)(2,1)S(1)}, bf16[1,384,256]{1,2,0:T(8,128)(2,1)S(1)}, u32[]{:S(2)}, u32[]{:S(2)}) collective-permute-start(bf16[1,384,256]{1,2,0:T(8,128)(2,1)S(1)} %get-tuple-element.105), channel_id=1, source_target_pairs={{0,2},{1,3},{2,0},{3,1},{4,6},{5,7},{6,4},{7,5},{8,10},{9,11},{10,... | collective-permute-start | bytes 589832 | tf_op jit(solution)/shard_map/ppermute | solution.py:453
  331.8 15.7 %collective-permute-start.24 = (bf16[1,384,256]{1,2,0:T(8,128)(2,1)S(1)}, bf16[1,384,256]{1,2,0:T(8,128)(2,1)S(1)}, u32[]{:S(2)}, u32[]{:S(2)}) collective-permute-start(bf16[1,384,256]{1,2,0:T(8,128)(2,1)S(1)} %get-tuple-element.104), channel_id=1, source_target_pairs={{0,1},{1,2},{2,3},{3,0},{4,5},{5,6},{6,7},{7,4},{8,9},{9,10},{10,1... | collective-permute-start | bytes 589832 | tf_op jit(solution)/shard_map/ppermute | solution.py:453
  334.6 14.3 %collective-permute-start.25 = (bf16[1,384,256]{1,2,0:T(8,128)(2,1)S(1)}, bf16[1,384,256]{1,2,0:T(8,128)(2,1)S(1)}, u32[]{:S(2)}, u32[]{:S(2)}) collective-permute-start(bf16[1,384,256]{1,2,0:T(8,128)(2,1)S(1)} %get-tuple-element.103), channel_id=1, source_target_pairs={{0,3},{1,0},{2,1},{3,2},{4,7},{5,4},{6,5},{7,6},{8,11},{9,8},{10,9... | collective-permute-start | bytes 589832 | tf_op jit(solution)/shard_map/ppermute | solution.py:453
  337.0 90.1 %collective-permute-start.40 = (bf16[4,2,2,32,1024]{4,3,2,1,0:T(8,128)(2,1)S(1)}, bf16[4,2,2,32,1024]{4,3,2,1,0:T(8,128)(2,1)}, u32[]{:S(2)}, u32[]{:S(2)}) collective-permute-start(bf16[4,2,2,32,1024]{4,3,2,1,0:T(8,128)(2,1)S(1)} %dynamic-slice_bitcast_fusion), channel_id=1, source_target_pairs={{0,4},{4,0},{8,12},{12,8},{1,5},{5,1},{9,13},{13,9},{2,6},{6,2},{1... | collective-permute-start | bytes 3145736 | tf_op jit(solution)/shard_map/ppermute | solution.py:374
  392.2 38.5 %collective-permute-start.37 = (bf16[2,2,128,768]{3,2,1,0:T(8,128)(2,1)}, bf16[2,2,128,768]{3,2,1,0:T(8,128)(2,1)}, u32[]{:S(2)}, u32[]{:S(2)}) collective-permute-start(bf16[2,2,128,768]{3,2,1,0:T(8,128)(2,1)} %dynamic-slice_bitcast_fusion.1), channel_id=1, source_target_pairs={{0,4},{4,0},{8,12},{12,8},{1,5},{5,1},{9,13},{13,9},{2,6},{6,2},{1... | collective-permute-start | bytes 2359304 | tf_op jit(solution)/shard_map/ppermute | solution.py:374
  401.2 1.3 collective-permute-start.32
  402.6 6.1 %collective-permute-start.33 = (f32[10,1024]{1,0:T(8,128)S(1)}, f32[10,1024]{1,0:T(8,128)S(1)}, u32[]{:S(2)}, u32[]{:S(2)}) collective-permute-start(f32[10,1024]{1,0:T(8,128)S(1)} %add.418), channel_id=1, source_target_pairs={{0,8},{4,12},{8,0},{12,4},{1,9},{5,13},{9,1},{13,5},{2,10},{6,14},... | collective-permute-start | bytes 122888 | tf_op jit(solution)/shard_map/ppermute | solution.py:374
  408.6 4.3 collective-permute-start.34
  413.0 5.5 %collective-permute-start.35 = (f32[10,1024]{1,0:T(8,128)S(1)}, f32[10,1024]{1,0:T(8,128)S(1)}, u32[]{:S(2)}, u32[]{:S(2)}) collective-permute-start(f32[10,1024]{1,0:T(8,128)S(1)} %add.420), channel_id=1, source_target_pairs={{0,1},{1,0},{2,3},{3,2},{4,5},{5,4},{6,7},{7,6},{8,9},{9,8},{10,11... | collective-permute-start | bytes 122888 | tf_op jit(solution)/shard_map/ppermute | solution.py:374
  418.5 8.5 %collective-permute-start.36 = (f32[10,1024]{1,0:T(8,128)S(1)}, f32[10,1024]{1,0:T(8,128)S(1)}, u32[]{:S(2)}, u32[]{:S(2)}) collective-permute-start(f32[10,1024]{1,0:T(8,128)S(1)} %add.421), channel_id=1, source_target_pairs={{0,2},{1,3},{2,0},{3,1},{4,6},{5,7},{6,4},{7,5},{8,10},{9,11},{10,... | collective-permute-start | bytes 122888 | tf_op jit(solution)/shard_map/ppermute | solution.py:374
  420.7 6.4 %copy-start.13 = (bf16[4,256,1024]{2,1,0:T(8,128)(2,1)S(1)}, bf16[4,256,1024]{2,1,0:T(8,128)(2,1)}, u32[]{:S(2)}) copy-start(bf16[4,256,1024]{2,1,0:T(8,128)(2,1)} %copy-done.12) | copy-start | bytes 6291460
  423.2 16.2 %collective-permute-start.26 = (bf16[384,1024]{1,0:T(8,128)(2,1)S(1)}, bf16[384,1024]{1,0:T(8,128)(2,1)S(1)}, u32[]{:S(2)}, u32[]{:S(2)}) collective-permute-start(bf16[384,1024]{1,0:T(8,128)(2,1)S(1)} %get-tuple-element.98), channel_id=1, source_target_pairs={{0,1},{4,5},{8,9},{12,13},{16,17},{20,21},{24,25},{28,29}} | collective-permute-start | bytes 2359304 | tf_op jit(solution)/shard_map/ppermute | solution.py:437
  425.2 44.8 %collective-permute-start.29 = (bf16[384,1024]{1,0:T(8,128)(2,1)}, bf16[384,1024]{1,0:T(8,128)(2,1)}, u32[]{:S(2)}, u32[]{:S(2)}) collective-permute-start(bf16[384,1024]{1,0:T(8,128)(2,1)} %get-tuple-element.99), channel_id=1, source_target_pairs={{3,2},{7,6},{11,10},{15,14},{19,18},{23,22},{27,26},{31,30}} | collective-permute-start | bytes 2359304 | tf_op jit(solution)/shard_map/ppermute | solution.py:440
  428.9 19.5 %collective-permute-start.41 = (bf16[4,2,32,1024]{3,2,1,0:T(8,128)(2,1)S(1)}, bf16[4,2,32,1024]{3,2,1,0:T(8,128)(2,1)S(1)}, u32[]{:S(2)}, u32[]{:S(2)}) collective-permute-start(bf16[4,2,32,1024]{3,2,1,0:T(8,128)(2,1)S(1)} %dynamic-slice_bitcast_fusion.2), channel_id=1, source_target_pairs={{0,8},{4,12},{8,0},{12,4},{1,9},{5,13},{9,1},{13,5},{2,10},{6,14},... | collective-permute-start | bytes 1572872 | tf_op jit(solution)/shard_map/ppermute | solution.py:374
  432.1 28.3 %collective-permute-start.38 = (bf16[2,128,768]{2,1,0:T(8,128)(2,1)S(1)}, bf16[2,128,768]{2,1,0:T(8,128)(2,1)S(1)}, u32[]{:S(2)}, u32[]{:S(2)}) collective-permute-start(bf16[2,128,768]{2,1,0:T(8,128)(2,1)S(1)} %dynamic-slice_bitcast_fusion.3), channel_id=1, source_target_pairs={{0,8},{4,12},{8,0},{12,4},{1,9},{5,13},{9,1},{13,5},{2,10},{6,14},... | collective-permute-start | bytes 1179656 | tf_op jit(solution)/shard_map/ppermute | solution.py:374
  441.8 28.2 %collective-permute-start.27 = (bf16[384,1024]{1,0:T(8,128)(2,1)}, bf16[384,1024]{1,0:T(8,128)(2,1)S(1)}, u32[]{:S(2)}, u32[]{:S(2)}) collective-permute-start(bf16[384,1024]{1,0:T(8,128)(2,1)} %add_convert_fusion.3), channel_id=1, source_target_pairs={{0,1},{1,2},{4,5},{5,6},{8,9},{9,10},{12,13},{13,14},{16,17},{17,1... | collective-permute-start | bytes 2359304 | tf_op jit(solution)/shard_map/ppermute | solution.py:437
  448.7 13.7 %collective-permute-start.42 = (bf16[4,1,32,1024]{3,2,1,0:T(8,128)(2,1)S(1)}, bf16[4,1,32,1024]{3,2,1,0:T(8,128)(2,1)S(1)}, u32[]{:S(2)}, u32[]{:S(2)}) collective-permute-start(bf16[4,1,32,1024]{3,2,1,0:T(8,128)(2,1)S(1)} %constant_dynamic-slice_fusion.2), channel_id=1, source_target_pairs={{0,16},{16,0},{1,17},{17,1},{2,18},{18,2},{3,19},{19,3},{4,20},{20... | collective-permute-start | bytes 786440 | tf_op jit(solution)/shard_map/ppermute | solution.py:374
  460.6 7.8 %collective-permute-start.39 = (bf16[1,128,768]{2,1,0:T(8,128)(2,1)S(1)}, bf16[1,128,768]{2,1,0:T(8,128)(2,1)S(1)}, u32[]{:S(2)}, u32[]{:S(2)}) collective-permute-start(bf16[1,128,768]{2,1,0:T(8,128)(2,1)S(1)} %constant_dynamic-slice_fusion.3), channel_id=1, source_target_pairs={{0,16},{16,0},{1,17},{17,1},{2,18},{18,2},{3,19},{19,3},{4,20},{20... | collective-permute-start | bytes 589832 | tf_op jit(solution)/shard_map/ppermute | solution.py:374
  462.5 7.3 %collective-permute-start.43 = (bf16[2,32,1024]{2,1,0:T(8,128)(2,1)S(1)}, bf16[2,32,1024]{2,1,0:T(8,128)(2,1)S(1)}, u32[]{:S(2)}, u32[]{:S(2)}) collective-permute-start(bf16[2,32,1024]{2,1,0:T(8,128)(2,1)S(1)} %dynamic-slice_bitcast_fusion.7), channel_id=1, source_target_pairs={{0,2},{1,3},{2,0},{3,1},{4,6},{5,7},{6,4},{7,5},{8,10},{9,11},{10,... | collective-permute-start | bytes 393224 | tf_op jit(solution)/shard_map/ppermute | solution.py:374
  469.9 5.1 collective-permute-start.44
  473.5 9.8 %collective-permute-start.30 = (bf16[384,1024]{1,0:T(8,128)(2,1)}, bf16[384,1024]{1,0:T(8,128)(2,1)}, u32[]{:S(2)}, u32[]{:S(2)}) collective-permute-start(bf16[384,1024]{1,0:T(8,128)(2,1)} %get-tuple-element.97), channel_id=1, source_target_pairs={{2,1},{3,2},{6,5},{7,6},{10,9},{11,10},{14,13},{15,14},{18,17},{19... | collective-permute-start | bytes 2359304 | tf_op jit(solution)/shard_map/ppermute | solution.py:440
  475.1 6.4 %collective-permute-start.45 = (bf16[512,256]{1,0:T(8,128)(2,1)S(1)}, bf16[512,256]{1,0:T(8,128)(2,1)S(1)}, u32[]{:S(2)}, u32[]{:S(2)}) collective-permute-start(bf16[512,256]{1,0:T(8,128)(2,1)S(1)} %constant_dynamic-update-slice_fusion.7), channel_id=1, source_target_pairs={{0,16},{16,0},{1,17},{17,1},{2,18},{18,2},{3,19},{19,3},{4,20},{20... | collective-permute-start | bytes 786440 | tf_op jit(solution)/shard_map/ppermute | solution.py:374
  477.3 14.7 %collective-permute-start.28 = (bf16[384,1024]{1,0:T(8,128)(2,1)}, bf16[384,1024]{1,0:T(8,128)(2,1)S(1)}, u32[]{:S(2)}, u32[]{:S(2)}) collective-permute-start(bf16[384,1024]{1,0:T(8,128)(2,1)} %get-tuple-element.96), channel_id=1, source_target_pairs={{0,1},{1,2},{2,3},{4,5},{5,6},{6,7},{8,9},{9,10},{10,11},{12,13},{... | collective-permute-start | bytes 2359304 | tf_op jit(solution)/shard_map/ppermute | solution.py:437
  481.6 9.2 %collective-permute-start.46 = (bf16[2,512,256]{2,1,0:T(8,128)(2,1)S(1)}, bf16[2,512,256]{2,1,0:T(8,128)(2,1)S(1)}, u32[]{:S(2)}, u32[]{:S(2)}) collective-permute-start(bf16[2,512,256]{2,1,0:T(8,128)(2,1)S(1)} %bitcast_dynamic-update-slice_fusion.4), channel_id=1, source_target_pairs={{0,8},{4,12},{8,0},{12,4},{1,9},{5,13},{9,1},{13,5},{2,10},{6,14},... | collective-permute-start | bytes 1572872 | tf_op jit(solution)/shard_map/ppermute | solution.py:374
  485.8 21.5 %collective-permute-start.31 = (bf16[384,1024]{1,0:T(8,128)(2,1)}, bf16[384,1024]{1,0:T(8,128)(2,1)S(1)}, u32[]{:S(2)}, u32[]{:S(2)}) collective-permute-start(bf16[384,1024]{1,0:T(8,128)(2,1)} %add_convert_fusion), channel_id=1, source_target_pairs={{1,0},{2,1},{3,2},{5,4},{6,5},{7,6},{9,8},{10,9},{11,10},{13,12},{... | collective-permute-start | bytes 2359304 | tf_op jit(solution)/shard_map/ppermute | solution.py:440
  490.9 18.9 %collective-permute-start.47 = (bf16[2,2,512,256]{3,2,1,0:T(8,128)(2,1)S(1)}, bf16[2,2,512,256]{3,2,1,0:T(8,128)(2,1)S(1)}, u32[]{:S(2)}, u32[]{:S(2)}) collective-permute-start(bf16[2,2,512,256]{3,2,1,0:T(8,128)(2,1)S(1)} %bitcast_dynamic-update-slice_fusion.2), channel_id=1, source_target_pairs={{0,4},{4,0},{8,12},{12,8},{1,5},{5,1},{9,13},{13,9},{2,6},{6,2},{1... | collective-permute-start | bytes 3145736 | tf_op jit(solution)/shard_map/ppermute | solution.py:374
  490.9 16.4 %copy-start.9 = (bf16[1536,1024]{1,0:T(8,128)(2,1)S(1)}, bf16[1536,1024]{1,0:T(8,128)(2,1)}, u32[]{:S(2)}) copy-start(bf16[1536,1024]{1,0:T(8,128)(2,1)} %get-tuple-element.117) | copy-start | bytes 9437188
  491.2 16.9 %copy-start.8 = (f32[384,1024]{1,0:T(8,128)S(1)}, f32[384,1024]{1,0:T(8,128)}, u32[]{:S(2)}) copy-start(f32[384,1024]{1,0:T(8,128)} %copy-done.7) | copy-start | bytes 4718596
  (27 other events, 60.8 us)
Sparse Core Ops, SparseCore 0:
  36.4 110.4 all-gather.5
  286.7 88.3 reduce-scatter.1
  420.8 48.3 all-gather.3

commit v3 on v2

--- a/solution.py
+++ b/solution.py
@@ -9,7 +9,8 @@
 
 EPSILON = 1e-05
 HIGHEST_PRECISION = lax.Precision.HIGHEST
-TIE = 1
+FEED_STEPS = 2
+EARLY = True
 BLK = 256
 HEAD_LANES = 64
 NEAR = 128
@@ -42,7 +43,7 @@
 
 
 def attention_forward_kernel(
-    cut_ref, qkv_ref, bias_ref, out_ref, lse_ref, tile_ref, masked_v, score_ref
+    cut_ref, qkv_ref, bias_ref, out_ref, lse_ref, tile_ref, masked_v, score_ref, *, first_head
 ):
     heads = masked_v.shape[0]
     width = out_ref.shape[1]
@@ -52,7 +53,7 @@
     @pl.when(block == 0)
     def _():
         for head in range(heads):
-            wide = jnp.broadcast_to(bias_ref[head : head + 1, :], (BLK, 2 * BLK))
+            wide = jnp.broadcast_to(bias_ref[first_head + head : first_head + head + 1, :], (BLK, 2 * BLK))
             tile_ref[head] = pltpu.roll(wide, 0, 1, stride=1, stride_axis=0)
             masked_v[head] = one_head(qkv_ref[:, 2 * width :], head)
 
@@ -74,7 +75,7 @@
         new_tops = []
         for head in range(heads):
             raw = dot_nt(q_heads[head], keys)
-            far = bias_ref[head : head + 1, 2 * BLK - 1 : 2 * BLK]
+            far = bias_ref[first_head + head : first_head + head + 1, 2 * BLK - 1 : 2 * BLK]
             bias = jnp.where(near, tile_ref[head, :, pl.ds(offset, BLK)], far)
             scores = jnp.where(allowed, raw + bias, -1e30)
             score_ref[head, :, pl.ds(key_start, BLK)] = scores
@@ -128,12 +129,12 @@
     lse_ref[...] = jnp.transpose(logs)[0:8, :]
 
 
-def attention_forward(cut, projected, near_bias):
+def attention_forward(cut, projected, near_bias, first_head):
     length, width = projected.shape[0], projected.shape[1] // 3
     heads = width // HEAD_LANES
     whole = lambda block, cut: (0, 0)
     return pl.pallas_call(
-        attention_forward_kernel,
+        functools.partial(attention_forward_kernel, first_head=first_head),
         grid_spec=pltpu.PrefetchScalarGridSpec(
             num_scalar_prefetch=1,
             grid=(length // BLK,),
@@ -169,6 +170,7 @@
 def attention_backward_kernel(
     cut_ref, qkv_ref, grad_ref, att_ref, lse_ref, bias_ref, dqkv_ref, table_ref,
     tile_ref, q_masked, grad_masked, delta_ref, dq_sum, near_sum, far_sum,
+    *, first_head,
 ):
     heads = q_masked.shape[0]
     block = pl.program_id(0)
@@ -186,7 +188,7 @@
         pick = jnp.where(lane // HEAD_LANES == row, 1.0, 0.0).astype(jnp.bfloat16)
         delta_ref[...] = (dot_nt(pick, high) + dot_nt(pick, rest))[0:8, :]
         for head in range(heads):
-            wide = jnp.broadcast_to(bias_ref[head : head + 1, :], (BLK, 2 * BLK))
+            wide = jnp.broadcast_to(bias_ref[first_head + head : first_head + head + 1, :], (BLK, 2 * BLK))
             tile_ref[head] = pltpu.roll(wide, 0, 1, stride=1, stride_axis=0)
             q_masked[head] = one_head(scaled(qkv_ref[:, 0:width]), head)
             grad_masked[head] = one_head(grad_ref[...], head)
@@ -214,7 +216,7 @@
         for head in range(heads):
             q_head = q_masked[head, pl.ds(row_start, BLK), :]
             grad_head = grad_masked[head, pl.ds(row_start, BLK), :]
-            far = bias_ref[head : head + 1, BLK - 1 : BLK]
+            far = bias_ref[first_head + head : first_head + head + 1, BLK - 1 : BLK]
             bias = jnp.where(near, tile_ref[head, :, pl.ds(offset, BLK)], far)
             scores = dot_nt(keys, q_head) + bias
             log_total = lse_ref[head : head + 1, pl.ds(row_start, BLK)]
@@ -276,13 +278,13 @@
             )
 
 
-def attention_backward(cut, projected, grad_att, attended, logs, near_bias):
+def attention_backward(cut, projected, grad_att, attended, logs, near_bias, first_head):
     length, width = attended.shape
     heads = width // HEAD_LANES
     whole = lambda block, cut: (0, 0)
     full = pl.BlockSpec((length, width), whole)
     return pl.pallas_call(
-        attention_backward_kernel,
+        functools.partial(attention_backward_kernel, first_head=first_head),
         grid_spec=pltpu.PrefetchScalarGridSpec(
             num_scalar_prefetch=1,
             grid=(length // BLK,),
@@ -349,12 +351,10 @@
     return jnp.pad(forward, rows), jnp.pad(backward, rows)
 
 
-def table_gradient(hot, table_sums, heads):
+def table_gradient(hot, near_sums, far_sums):
     reach = hot.shape[0]
-    near = table_sums[:heads, : reach - 1]
-    far = jnp.sum(table_sums[:heads, reach - 1 :], axis=1) + jnp.sum(
-        table_sums[heads : 2 * heads], axis=1
-    )
+    near = near_sums[:, : reach - 1]
+    far = jnp.sum(near_sums[:, reach - 1 :], axis=1) + jnp.sum(far_sums, axis=1)
     by_distance = jnp.concatenate([near, far[:, None]], axis=1)
     return jnp.einsum(
         "dn,hd->nh", hot, by_distance, precision=HIGHEST_PRECISION,
@@ -365,8 +365,8 @@
 TEAM = 4
 
 
-def place_of(axis):
-    return lax.axis_index(axis)
+def after(value, *gates):
+    return lax.optimization_barrier((value,) + gates)[0]
 
 
 def flip(value, axis, bit):
@@ -385,9 +385,7 @@
 def double(value, axis, bit):
     mine = (lax.axis_index(axis) // bit) % 2
     other = flip(value, axis, bit)
-    pair = jnp.zeros((2,) + value.shape, value.dtype)
-    pair = lax.dynamic_update_index_in_dim(pair, value, mine, 0)
-    return lax.dynamic_update_index_in_dim(pair, other, 1 - mine, 0)
+    return jnp.where(mine == 0, jnp.stack([value, other]), jnp.stack([other, value]))
 
 
 def bits_of(size):
@@ -399,70 +397,89 @@
     return bits
 
 
-def chain_gather(own):
-    size = lax.axis_size("mp")
-    spot = lax.axis_index("mp")
-    rows = own.shape[0]
-    right = left = own
-    rights, lefts = {}, {}
-    for step in range(1, size):
-        right = lax.ppermute(right, "mp", [(i, i + 1) for i in range(step - 1, size - 1)])
-        left = lax.ppermute(left, "mp", [(i, i - 1) for i in range(1, size - step + 1)])
-        rights[step], lefts[step] = right, left
-    whole = jnp.zeros((size * rows,) + own.shape[1:], own.dtype)
-    whole = lax.dynamic_update_slice_in_dim(whole, own, spot * rows, 0)
-    for step in range(1, size):
-        block = rights[step] + lefts[size - step]
-        source = lax.rem(spot + size - step, size)
-        whole = lax.dynamic_update_slice_in_dim(whole, block, source * rows, 0)
-    return whole, rights
-
-
-def chain_scatter(value):
-    size = lax.axis_size("mp")
-    spot = lax.axis_index("mp")
-    rows = value.shape[0] // size
-
-    def block(place):
-        return lax.dynamic_slice_in_dim(value, place * rows, rows, 0).astype(jnp.float32)
-
-    from_left = from_right = None
-    for step in range(1, size):
-        reach = size - step
-        to_right = block(jnp.minimum(spot + reach, size - 1))
-        to_left = block(jnp.maximum(spot - reach, 0))
-        if from_left is not None:
-            to_right = to_right + from_left.astype(jnp.float32)
-            to_left = to_left + from_right.astype(jnp.float32)
-        from_left = lax.ppermute(
-            to_right.astype(jnp.bfloat16), "mp", [(i, i + 1) for i in range(step)]
-        )
-        from_right = lax.ppermute(
-            to_left.astype(jnp.bfloat16), "mp", [(i, i - 1) for i in range(size - step, size)]
-        )
-    return block(spot) + from_left.astype(jnp.float32) + from_right.astype(jnp.float32)
-
-
-def swap_over_chain(stack):
-    size = lax.axis_size("mp")
-    spot = lax.axis_index("mp")
-    own = lax.dynamic_index_in_dim(stack, spot, 0, keepdims=True)
-    result = lax.dynamic_update_slice_in_dim(jnp.zeros_like(stack), own, spot, 0)
-    for step in [2, 1, 3] if size == 4 else range(1, size):
-        send = lax.dynamic_index_in_dim(stack, lax.rem(spot + step, size), 0, keepdims=True)
-        received = lax.ppermute(send, "mp", [(i, (i + step) % size) for i in range(size)])
-        result = lax.dynamic_update_slice_in_dim(
-            result, received, lax.rem(spot + size - step, size), 0
-        )
-    return result
-
-
-def team_gather(own):
-    core = flip(own, "team", 1)
-    across = flip(own, "team", 2)
-    return jnp.concatenate([own, core], axis=0), jnp.concatenate(
-        [across, flip(across, "team", 1)], axis=0
-    )
+def with_partner(own):
+    return jnp.concatenate([own, flip(own, "team", 1)], axis=0)
+
+
+def feed_grads_kernel(piece_ref, up_ref, down_ref):
+    up_ref[...] = jnp.transpose(piece_ref[0, 0].astype(jnp.float32))
+    down_ref[...] = piece_ref[0, 1].astype(jnp.float32)
+
+
+def feed_grads_out(pieces, copies):
+    count, _, unit, depth = pieces.shape
+    merge = max(1, 128 // unit)
+    if merge > 1:
+        pieces = jnp.transpose(
+            pieces.reshape(count // merge, merge, 2, unit, depth), (0, 2, 1, 3, 4)
+        ).reshape(count // merge, 2, merge * unit, depth)
+    count, _, unit, depth = pieces.shape
+    each = copies // merge
+
+    def spot(step):
+        core, side, place = step // (2 * each), (step // each) % 2, step % each
+        return (side * 2 + core) * each + place
+
+    return pl.pallas_call(
+        feed_grads_kernel,
+        grid=(count,),
+        in_specs=[pl.BlockSpec((1, 2, unit, depth), lambda step: (step, 0, 0, 0))],
+        out_specs=[
+            pl.BlockSpec((depth, unit), lambda step: (0, spot(step))),
+            pl.BlockSpec((unit, depth), lambda step: (spot(step), 0)),
+        ],
+        out_shape=[
+            jax.ShapeDtypeStruct((depth, count * unit), jnp.float32),
+            jax.ShapeDtypeStruct((count * unit, depth), jnp.float32),
+        ],
+        compiler_params=pltpu.CompilerParams(dimension_semantics=("arbitrary",)),
+        cost_estimate=pl.CostEstimate(
+            flops=0, bytes_accessed=12 * count * unit * depth, transcendentals=0
+        ),
+        name="feed_grads_out",
+    )(pieces)
+
+
+def attention_grads_kernel(piece_ref, qkv_ref, out_ref):
+    group = piece_ref.shape[0]
+    rows, width = qkv_ref.shape[1] // group, qkv_ref.shape[2]
+    few = out_ref.shape[0] // group
+    for item in range(group):
+        for slot in range(3):
+            qkv_ref[slot, item * rows : (item + 1) * rows, :] = piece_ref[
+                item, slot * rows : (slot + 1) * rows, :
+            ].astype(jnp.float32)
+        for place in range(out_ref.shape[1] // width):
+            start = 3 * rows + place * few
+            out_ref[item * few : (item + 1) * few, place * width : (place + 1) * width] = (
+                piece_ref[item, start : start + few, :].astype(jnp.float32)
+            )
+
+
+def attention_grads_out(pieces, depth, head_width):
+    count = pieces.shape[0]
+    rows, few = depth // count, head_width // count
+    group = max(1, 8 // few)
+    return pl.pallas_call(
+        attention_grads_kernel,
+        grid=(count // group,),
+        in_specs=[
+            pl.BlockSpec((group,) + pieces.shape[1:], lambda step: (step, 0, 0)),
+        ],
+        out_specs=[
+            pl.BlockSpec((3, group * rows, head_width), lambda step: (0, step, 0)),
+            pl.BlockSpec((group * few, depth), lambda step: (step, 0)),
+        ],
+        out_shape=[
+            jax.ShapeDtypeStruct((3, depth, head_width), jnp.float32),
+            jax.ShapeDtypeStruct((head_width, depth), jnp.float32),
+        ],
+        compiler_params=pltpu.CompilerParams(dimension_semantics=("arbitrary",)),
+        cost_estimate=pl.CostEstimate(
+            flops=0, bytes_accessed=24 * depth * head_width, transcendentals=0
+        ),
+        name="attention_grads_out",
+    )(pieces)
 
 
 def normalize(inputs):
@@ -485,60 +502,125 @@
     )
 
 
+def spread(value, axis, size):
+    value = value[None]
+    for bit in bits_of(size):
+        value = double(value, axis, bit)
+        value = value.reshape((-1,) + value.shape[2:])
+    return value
+
+
+def exchange(blocks):
+    return [blocks[0]] + [flip(blocks[k], "mp", k) for k in range(1, len(blocks))]
+
+
+def cotangent_kernel(grad_a, grad_b, weight_a, weight_b, normed_ref, line_ref, out_ref, sum_ref):
+    grad = dot_nt(grad_a[...], weight_a[...]) + dot_nt(grad_b[...], weight_b[...])
+    unit = (normed_ref[...].astype(jnp.float32) - line_ref[0:1, :]) * line_ref[1:2, :]
+    out_ref[...] = grad.astype(jnp.bfloat16)
+    rows, depth = grad.shape
+    both = jnp.concatenate(
+        [
+            jnp.sum((grad * unit).reshape(rows // 8, 8, depth), axis=0),
+            jnp.sum(grad.reshape(rows // 8, 8, depth), axis=0),
+        ],
+        axis=0,
+    )
+
+    @pl.when(pl.program_id(0) == 0)
+    def _():
+        sum_ref[...] = both
+
+    @pl.when(pl.program_id(0) > 0)
+    def _():
+        sum_ref[...] += both
+
+
+def input_cotangent(grads, weights, normed, lines):
+    length, width = grads[0].shape
+    depth = weights[0].shape[0]
+    row = pl.BlockSpec((BLK, width), lambda step: (step, 0))
+    whole = pl.BlockSpec((depth, width), lambda step: (0, 0))
+    return pl.pallas_call(
+        cotangent_kernel,
+        grid=(length // BLK,),
+        in_specs=[
+            row, row, whole, whole,
+            pl.BlockSpec((BLK, depth), lambda step: (step, 0)),
+            pl.BlockSpec((2, depth), lambda step: (0, 0)),
+        ],
+        out_specs=[
+            pl.BlockSpec((BLK, depth), lambda step: (step, 0)),
+            pl.BlockSpec((16, depth), lambda step: (0, 0)),
+        ],
+        out_shape=[
+            jax.ShapeDtypeStruct((length, depth), jnp.bfloat16),
+            jax.ShapeDtypeStruct((16, depth), jnp.float32),
+        ],
+        compiler_params=pltpu.CompilerParams(dimension_semantics=("arbitrary",)),
+        cost_estimate=pl.CostEstimate(
+            flops=4 * length * width * depth,
+            bytes_accessed=4 * (length * width + depth * width + length * depth),
+            transcendentals=0,
+        ),
+        name="input_cotangent",
+    )(*grads, *weights, normed, lines)
+
+
 def feed_kernel(
-    weight_ref, bias_ref, second_ref, grad_ref,
-    act_ref, pre_ref, back_ref, out_ref, sum_ref, back_sum, out_sum, *, unit,
+    own_ref, beside_ref, across_ref, corner_ref, bias_ref, second_ref, grad_ref,
+    act_ref, pre_ref, back_ref, out_ref, sum_ref, *, unit,
 ):
-    step = pl.program_id(0)
-    parts, copies, _, depth = weight_ref.shape
-    hidden = parts * copies * unit
-    w_up = weight_ref[:, :, 0:unit, :].reshape(hidden, depth)
-    w_down = weight_ref[:, :, unit : 2 * unit, :].reshape(hidden, depth)
-    pre = dot_nt(second_ref[...], w_up) + bias_ref[...]
-    grad_act = dot_nt(grad_ref[...], w_down)
-    cdf = 0.5 + 0.5 * lax.erf(pre * 0.7071067811865476)
-    pdf = jnp.exp(pre * pre * -0.5) * 0.3989422804014327
-    active = (pre * cdf).astype(jnp.bfloat16)
-    grad_pre = ((cdf + pre * pdf) * grad_act).astype(jnp.bfloat16)
-    act_ref[...] = active
-    pre_ref[...] = grad_pre
-    sum_ref[...] = jnp.sum(grad_pre.astype(jnp.float32), axis=0, keepdims=True)
-    back = dot_nn(grad_pre, w_up)
-    out = dot_nn(active, w_down)
-
-    @pl.when(step == 0)
+    copies, _, depth = own_ref.shape
+    hidden = copies * unit
+    second = second_ref[...]
+    grad = grad_ref[...]
+    back = out = None
+    sums = []
+    for slot, ref in enumerate((own_ref, beside_ref, across_ref, corner_ref)):
+        spot = slice(slot * hidden, (slot + 1) * hidden)
+        w_up = ref[:, 0:unit, :].reshape(hidden, depth)
+        w_down = ref[:, unit : 2 * unit, :].reshape(hidden, depth)
+        pre = dot_nt(second, w_up) + bias_ref[0:1, spot]
+        grad_act = dot_nt(grad, w_down)
+        cdf = 0.5 + 0.5 * lax.erf(pre * 0.7071067811865476)
+        pdf = jnp.exp(pre * pre * -0.5) * 0.3989422804014327
+        active = (pre * cdf).astype(jnp.bfloat16)
+        grad_pre = ((cdf + pre * pdf) * grad_act).astype(jnp.bfloat16)
+        act_ref[:, spot] = active
+        pre_ref[:, spot] = grad_pre
+        sums.append(jnp.sum(grad_pre.astype(jnp.float32), axis=0, keepdims=True))
+        one_back = dot_nn(grad_pre, w_up)
+        one_out = dot_nn(active, w_down)
+        back = one_back if back is None else back + one_back
+        out = one_out if out is None else out + one_out
+    back_ref[...] = back.astype(jnp.bfloat16)
+    out_ref[...] = out.astype(jnp.bfloat16)
+    line = jnp.concatenate(sums, axis=1)
+
+    @pl.when(pl.program_id(0) == 0)
     def _():
-        back_sum[...] = back
-        out_sum[...] = out
-
-    @pl.when(step > 0)
+        sum_ref[...] = line
+
+    @pl.when(pl.program_id(0) > 0)
     def _():
-        back_sum[...] += back
-        out_sum[...] += out
-
-    @pl.when(step == pl.num_programs(0) - 1)
-    def _():
-        back_ref[...] = back_sum[...].astype(jnp.bfloat16)
-        out_ref[...] = out_sum[...].astype(jnp.bfloat16)
-
-
-def feed_forward(weights, bias_row, second, grad, unit):
-    parts, copies, per, depth = weights.shape
+        sum_ref[...] += line
+
+
+def feed_forward(slots, bias_row, second, grad, unit):
+    copies, _, depth = slots[0].shape
     rows = second.shape[0]
-    width = parts * copies * unit
-    take = 2 if parts % 2 == 0 else 1
-    hidden = take * copies * unit
-    whole = pl.BlockSpec((rows, depth), lambda step: (0, 0))
-    column = pl.BlockSpec((rows, hidden), lambda step: (0, step))
-    line = pl.BlockSpec((1, hidden), lambda step: (0, step))
+    width = len(slots) * copies * unit
+    take = rows // FEED_STEPS
+    whole = lambda step: (0, 0, 0)
+    row = pl.BlockSpec((take, depth), lambda step: (step, 0))
+    wide = pl.BlockSpec((take, width), lambda step: (step, 0))
+    line = pl.BlockSpec((1, width), lambda step: (0, 0))
     return pl.pallas_call(
         functools.partial(feed_kernel, unit=unit),
-        grid=(parts // take,),
-        in_specs=[
-            pl.BlockSpec((take, copies, per, depth), lambda step: (step, 0, 0, 0)),
-            line, whole, whole,
-        ],
-        out_specs=[column, column, whole, whole, line],
+        grid=(FEED_STEPS,),
+        in_specs=[pl.BlockSpec(slot.shape, whole) for slot in slots] + [line, row, row],
+        out_specs=[wide, wide, row, row, line],
         out_shape=[
             jax.ShapeDtypeStruct((rows, width), jnp.bfloat16),
             jax.ShapeDtypeStruct((rows, width), jnp.bfloat16),
@@ -546,10 +628,6 @@
             jax.ShapeDtypeStruct((rows, depth), jnp.bfloat16),
             jax.ShapeDtypeStruct((1, width), jnp.float32),
         ],
-        scratch_shapes=[
-            pltpu.VMEM((rows, depth), jnp.float32),
-            pltpu.VMEM((rows, depth), jnp.float32),
-        ],
         compiler_params=pltpu.CompilerParams(
             dimension_semantics=("arbitrary",), vmem_limit_bytes=56 * 1024 * 1024
         ),
@@ -558,11 +636,11 @@
             transcendentals=2 * rows * width,
         ),
         name="feed_forward",
-    )(weights, bias_row, second, grad)
+    )(*slots, bias_row, second, grad)
 
 
 def weight_grad_kernel(
-    act_a, act_b, pre_a, pre_b, second_a, second_b, grad_a, grad_b, out_ref
+    part_ref, act_a, act_b, pre_a, pre_b, second_a, second_b, grad_a, grad_b, out_ref
 ):
     _, copies, _, unit, depth = out_ref.shape
     up = dot_tn(pre_a[...], second_a[...]) + dot_tn(pre_b[...], second_b[...])
@@ -571,17 +649,22 @@
     out_ref[0, :, 1] = down.astype(jnp.bfloat16).reshape(copies, unit, depth)
 
 
-def weight_grads(acts, pres, seconds, grads, parts, copies):
+def weight_grads(part, acts, pres, seconds, grads, parts, copies):
     rows, width = acts[0].shape
     depth = seconds[0].shape[1]
     unit = width // (parts * copies)
-    column = pl.BlockSpec((rows, width // parts), lambda step: (0, step))
-    whole = pl.BlockSpec((rows, depth), lambda step: (0, 0))
+    column = pl.BlockSpec((rows, width // parts), lambda step, part: (0, step))
+    whole = pl.BlockSpec((rows, depth), lambda step, part: (0, 0))
     return pl.pallas_call(
         weight_grad_kernel,
-        grid=(parts,),
-        in_specs=[column] * 4 + [whole] * 4,
-        out_specs=pl.BlockSpec((1, copies, 2, unit, depth), lambda step: (step, 0, 0, 0, 0)),
+        grid_spec=pltpu.PrefetchScalarGridSpec(
+            num_scalar_prefetch=1,
+            grid=(parts,),
+            in_specs=[column] * 4 + [whole] * 4,
+            out_specs=pl.BlockSpec(
+                (1, copies, 2, unit, depth), lambda step, part: (part[0] ^ step, 0, 0, 0, 0)
+            ),
+        ),
         out_shape=jax.ShapeDtypeStruct((parts, copies, 2, unit, depth), jnp.bfloat16),
         compiler_params=pltpu.CompilerParams(
             dimension_semantics=("arbitrary",), vmem_limit_bytes=56 * 1024 * 1024
@@ -591,7 +674,11 @@
             transcendentals=0,
         ),
         name="weight_grads",
-    )(*acts, *pres, *seconds, *grads)
+    )(part, *acts, *pres, *seconds, *grads)
+
+
+def sync(*values):
+    return lax.optimization_barrier(values)
 
 
 def body(
@@ -607,152 +694,294 @@
     part = lax.axis_index("mp")
     core = member % 2
     rows, depth = tokens.shape
-    heads = rel_table.shape[1]
     head_width = w_out.shape[0]
+    pair_width = 2 * HEAD_LANES
+    pairs = head_width // pair_width
     team_units = w_up.shape[1] // TEAM
     unit = team_units // copies
+    out_rows = head_width // (2 * copies)
     seg_row = seg_ids[0]
+    to_right = [(i, i + 1) for i in range(parts - 1)]
+    to_left = [(i + 1, i) for i in range(parts - 1)]
 
     x_part = tokens.astype(wide)
     unit1, inverse1 = normalize(x_part)
-    normed, rights = chain_gather((unit1 * ln1_gain + ln1_bias).astype(low))
-
-    spot = member * team_units + copy * unit
-    out_rows = head_width // (2 * copies)
-    piece = jnp.concatenate(
-        [
-            jnp.transpose(lax.dynamic_slice_in_dim(w_up, spot, unit, 1)),
-            lax.dynamic_slice_in_dim(w_down, spot, unit, 0),
-            lax.dynamic_slice_in_dim(w_out, (copy * 2 + core) * out_rows, out_rows, 0),
-        ],
-        axis=0,
-    )
-    piece = lax.optimization_barrier((piece, rights[TIE]))[0]
-    weights = lax.all_gather(piece, ("mp", "copy"), axis=0, tiled=False).reshape(
-        parts, copies, piece.shape[0], depth
-    )
-    own_out = weights[:, :, 2 * unit :, :]
-    other_out = flip(own_out, "team", 1)
-    is_first = core == 0
-    w_out_full = jnp.stack(
-        [jnp.where(is_first, own_out, other_out), jnp.where(is_first, other_out, own_out)], axis=2
-    ).reshape(parts, head_width, depth)
-    bias_all = up_bias[None]
-    for bit in bits_of(parts):
-        bias_all = double(bias_all, "mp", bit).reshape(-1, up_bias.shape[0])
-    bias_row = lax.dynamic_slice_in_dim(bias_all, member * team_units, team_units, 1).reshape(1, -1)
-    grad_near, grad_far = team_gather(out_grad)
-
-    w_cat = jnp.transpose(w_qkv, (1, 0, 2)).reshape(depth, -1)
-    projected = jnp.dot(normed, w_cat, preferred_element_type=wide).astype(low)
+    normed = lax.all_gather(
+        (unit1 * ln1_gain + ln1_bias).astype(low), "mp", axis=0, tiled=True
+    )
+
+    up_own = jnp.transpose(
+        lax.dynamic_slice_in_dim(w_up, member * team_units, team_units, 1)
+    ).reshape(copies, unit, depth)
+    down_own = lax.dynamic_slice_in_dim(w_down, member * team_units, team_units, 0).reshape(
+        copies, unit, depth
+    )
+    out_own = lax.dynamic_index_in_dim(
+        w_out.reshape(copies, 2, out_rows, depth), core, 1, keepdims=False
+    )
+    own_slot = jnp.concatenate([up_own, down_own, out_own], axis=1)
+    piece = lax.dynamic_index_in_dim(own_slot, copy, 0, keepdims=False)
+    if not EARLY:
+        piece = after(piece, normed)
+    right1 = lax.ppermute(piece, "mp", to_right)
+    left1 = lax.ppermute(piece, "mp", to_left)
+    grad_across = flip(out_grad, "team", 2)
+    grad_near = with_partner(out_grad)
+    grad_far = with_partner(grad_across)
+    biases = [up_bias] + [flip(up_bias, "mp", k) for k in range(1, parts)]
+    bias_row = jnp.concatenate(
+        [lax.dynamic_slice_in_dim(one, member * team_units, team_units, 0) for one in biases]
+    )[None]
+    w_cat = [
+        jnp.transpose(
+            w_qkv[:, :, pair * pair_width : (pair + 1) * pair_width], (1, 0, 2)
+        ).reshape(depth, -1)
+        for pair in range(pairs)
+    ]
     hot, by_distance = distance_bias(rel_table, bucket_of)
     forward_bias, backward_bias = near_tables(by_distance)
     cut = jnp.sum((seg_row == seg_row[0]).astype(jnp.int32)).reshape(1)
-    attended, logs = attention_forward(cut, projected, forward_bias)
-    own_rows = swap_over_chain(attended.reshape(parts, rows, head_width))
-    branch = jnp.einsum("jtc,jcd->td", own_rows, w_out_full, preferred_element_type=wide)
+    normed, grad_near, grad_far, bias_row, own_slot, w_first, w_last, forward_bias, cut = sync(
+        normed, grad_near, grad_far, bias_row, own_slot, w_cat[0], w_cat[1], forward_bias, cut
+    )
+    w_cat = [w_first, w_last]
+    if EARLY:
+        right1, left1, normed = sync(right1, left1, normed)
+
+    def attend(pair, projected):
+        return attention_forward(cut, projected, forward_bias, 2 * pair)
+
+    def send_rows(att_one):
+        blocks = att_one.reshape(parts, rows, pair_width)
+        return exchange(
+            [
+                lax.dynamic_index_in_dim(blocks, part ^ k, 0, keepdims=False)
+                for k in range(parts)
+            ]
+        )
+
+    def whole_out(mine):
+        other = flip(mine, "team", 1)
+        return jnp.where(
+            core == 0, jnp.stack([mine, other], axis=2), jnp.stack([other, mine], axis=2)
+        )
+
+    projected = [
+        jnp.dot(normed, w_one, preferred_element_type=wide).astype(low) for w_one in w_cat
+    ]
+    attended, logs = [None, None], [None, None]
+    attended[0], logs[0] = attend(0, projected[0])
+    if not EARLY:
+        right1, left1, attended[0] = sync(right1, left1, attended[0])
+    right2 = lax.ppermute(right1, "mp", to_right[1:])
+    left2 = lax.ppermute(left1, "mp", to_left[:-1])
+    beside_slot = spread(jnp.where(part % 2 == 0, left1, right1), "copy", copies)
+    if EARLY:
+        right2, left2, beside_slot, attended[0], projected[1] = sync(
+            right2, left2, beside_slot, attended[0], projected[1]
+        )
+    moved = [send_rows(attended[0]), None]
+    attended[1], logs[1] = attend(1, projected[1])
+    if not EARLY:
+        right2, left2, beside_slot, attended[1] = sync(right2, left2, beside_slot, attended[1])
+    right3 = lax.ppermute(right2, "mp", to_right[2:])
+    left3 = lax.ppermute(left2, "mp", to_left[:-2])
+    across_slot = spread(right2 + left2, "copy", copies)
+    if EARLY:
+        results = sync(right3, left3, across_slot, attended[1], *moved[0])
+        right3, left3, across_slot, attended[1] = results[:4]
+        moved[0] = list(results[4:])
+    corner = jnp.where(
+        (part == 0) | (part == parts - 1), right3 + left3, jnp.where(part == 1, left1, right1)
+    )
+    corner_slot = spread(corner, "copy", copies)
+    moved[1] = send_rows(attended[1])
+    slots = [own_slot, beside_slot, across_slot, corner_slot]
+    w_out_full = jnp.concatenate(
+        [
+            w_out.reshape(1, copies, 2, out_rows, depth),
+            whole_out(jnp.stack([slot[:, 2 * unit :] for slot in slots[1:3]])),
+            whole_out(corner_slot[None, :, 2 * unit :]),
+        ]
+    ).reshape(parts * head_width, depth)
+
+    own_rows = jnp.concatenate(
+        [moved[pair][k] for k in range(parts) for pair in range(pairs)], axis=1
+    )
+    branch = jnp.dot(own_rows, w_out_full, preferred_element_type=wide)
     hidden_in = x_part + branch
     unit2, inverse2 = normalize(hidden_in)
     second = (unit2 * ln2_gain + ln2_bias).astype(low)
-    second_near, second_far = team_gather(second)
-
+    second_across = flip(second, "team", 2)
+    second_near = with_partner(second)
     act_near, pre_near, back_near, feed_near, sums_near = feed_forward(
-        weights, bias_row, second_near, grad_near, unit
-    )
+        slots, bias_row, second_near, grad_near, unit
+    )
+    second_across, back_near = sync(second_across, back_near)
+    beside = flip(back_near[rows:], "team", 1)
+    second_far = with_partner(second_across)
     act_far, pre_far, back_far, feed_far, sums_far = feed_forward(
-        weights, bias_row, second_far, grad_far, unit
-    )
-    beside = flip(back_near[rows:], "team", 1)
-    onward = back_far[:rows].astype(wide) + flip(back_far[rows:], "team", 1).astype(wide)
-    across = flip(onward.astype(low), "team", 2)
+        slots, bias_row, second_far, grad_far, unit
+    )
+    onward = (
+        back_far[:rows].astype(wide) + flip(back_far[rows:], "team", 1).astype(wide)
+    ).astype(low)
+    across = flip(onward, "team", 2)
+    ff_grads = weight_grads(
+        part.reshape(1), (act_near, after(act_far, onward)), (pre_near, pre_far),
+        (second_near, second_far), (grad_near, grad_far), parts, copies,
+    )
+    ff_grads, across, beside = sync(ff_grads, across, beside)
+    ff_piece = lax.psum_scatter(
+        ff_grads.reshape(parts * copies, 2 * unit, depth), ("mp", "copy"),
+        scatter_dimension=0, tiled=False,
+    )
     grad_second = back_near[:rows].astype(wide) + beside.astype(wide) + across.astype(wide)
     grad_part = out_grad.astype(wide)
     grad_hidden = grad_part + normalize_backward(grad_second, ln2_gain, unit2, inverse2)
     grad_branch = grad_hidden.astype(low)
-    grad_stack = jnp.einsum("td,jcd->jtc", grad_branch, w_out_full, preferred_element_type=wide)
-    grad_att = swap_over_chain(grad_stack.astype(low)).reshape(parts * rows, head_width)
-
-    ff_grads = weight_grads(
-        (act_near, act_far), (pre_near, pre_far), (second_near, second_far),
-        (grad_near, grad_far), parts, copies,
-    )
-    ff_piece = lax.psum_scatter(
-        ff_grads.reshape(parts * copies, 2 * unit, depth), ("mp", "copy"),
-        scatter_dimension=0, tiled=False,
-    )
-    ff_all = lax.all_gather(ff_piece, ("team", "copy"), axis=0, tiled=False).reshape(
-        TEAM * copies, 2, unit, depth
-    )
-    grad_up = jnp.transpose(ff_all[:, 0].reshape(TEAM * team_units, depth)).astype(wide)
-    grad_down = ff_all[:, 1].reshape(TEAM * team_units, depth).astype(wide)
-
-    beside = flip(jnp.stack([feed_far[rows:], feed_near[rows:]]), "team", 1)
-    onward = feed_far[:rows].astype(wide) + beside[0].astype(wide)
-    feed_own = (
-        feed_near[:rows].astype(wide) + beside[1].astype(wide)
-        + flip(onward.astype(low), "team", 2).astype(wide)
-    )
-    layer_out = (hidden_in + feed_own + down_bias).astype(low)
-
-    wout_grad = jnp.einsum("jtc,td->jcd", own_rows, grad_branch, preferred_element_type=wide)
-    wout_grad = wout_grad.astype(low).reshape(parts, 2, 2, copies, -1, depth)
-    wout_grad = halve(halve(wout_grad, 1, "team", 1), 1, "team", 2)
+    grad_rows = dot_nt(grad_branch, w_out_full).astype(low)
+    received = [
+        exchange(
+            [
+                grad_rows[
+                    :, k * head_width + pair * pair_width : k * head_width + (pair + 1) * pair_width
+                ]
+                for k in range(parts)
+            ]
+        )
+        for pair in range(pairs)
+    ]
+
+    def in_order(blocks):
+        natural = jnp.zeros((parts, rows, pair_width), low)
+        for k in range(parts):
+            natural = lax.dynamic_update_index_in_dim(natural, blocks[k], part ^ k, 0)
+        return natural.reshape(parts * rows, pair_width)
+
+    def attend_back(pair, grad_att):
+        return attention_backward(
+            cut, projected[pair], grad_att, attended[pair], logs[pair], backward_bias, 2 * pair
+        )
+
+    wout_grad = dot_tn(own_rows, after(grad_branch, grad_rows)).astype(low)
+    wout_grad = wout_grad.reshape(parts, 2, 2, copies, -1, depth)
+    wout_grad = halve(wout_grad, 1, "team", 1)
+    feed_far = after(feed_far, grad_rows)
+    feed_beside = flip(jnp.stack([feed_far[rows:], feed_near[rows:]]), "team", 1)
+    results = sync(wout_grad, feed_beside, *received[0])
+    wout_grad, feed_beside = results[:2]
+    received[0] = results[2:]
+    wout_grad = halve(wout_grad, 1, "team", 2)
+    feed_across = flip(
+        (feed_far[:rows].astype(wide) + feed_beside[0].astype(wide)).astype(low), "team", 2
+    )
+    dqkv, table_sums = [None, None], [None, None]
+    dqkv[0], table_sums[0] = attend_back(0, in_order(received[0]))
+    results = sync(dqkv[0], wout_grad, feed_across, normed, *received[1])
+    dqkv[0], wout_grad, feed_across, late_normed = results[:4]
+    received[1] = results[4:]
+    half = depth // 2
+    normed_keep = lax.dynamic_slice_in_dim(late_normed, core * half, half, 1)
+    normed_send = lax.dynamic_slice_in_dim(late_normed, (1 - core) * half, half, 1)
     for bit in reversed(bits_of(copies)):
         wout_grad = halve(
             wout_grad.reshape((parts, 2, -1) + wout_grad.shape[2:]), 1, "copy", bit
         )
     wout_grad = wout_grad.reshape(parts, -1, depth)
-    for bit in reversed(bits_of(parts)):
-        wout_grad = halve(wout_grad.reshape((2, -1) + wout_grad.shape[1:]), 0, "mp", bit)
-    wout_grad = wout_grad.reshape(-1, depth)
-
-    dqkv, table_sums = attention_backward(
-        cut, projected, grad_att, attended, logs, backward_bias
-    )
-    running = lax.dot_general(
-        dqkv, w_cat, (((1,), (1,)), ((), ())), preferred_element_type=wide
-    ).astype(low)
-    grad_first = chain_scatter(running)
-    grad_first_norm = normalize_backward(grad_first, ln1_gain, unit1, inverse1)
-    grad_tokens = (grad_hidden + grad_first_norm).astype(low)
-
-    qkv_grad = dot_tn(normed, dqkv).astype(low)
-    qkv_grad = qkv_grad.reshape(2, 2, copies, -1, qkv_grad.shape[1])
-    qkv_grad = halve(halve(qkv_grad, 0, "team", 1), 0, "team", 2)
-    for bit in reversed(bits_of(copies)):
-        qkv_grad = halve(qkv_grad.reshape((2, -1) + qkv_grad.shape[1:]), 0, "copy", bit)
-    qkv_grad = qkv_grad.reshape(-1, 3 * head_width)
-    flat = jnp.concatenate([qkv_grad.reshape(-1, head_width), wout_grad.reshape(-1, head_width)])
-    for bit in bits_of(copies):
-        flat = double(flat, "copy", bit)
-    flat = double(double(flat, "team", 2), "team", 1)
-    flat = flat.reshape(TEAM * copies, -1, head_width)
-    qkv_rows = qkv_grad.shape[0] * 3
-    grad_qkv = jnp.transpose(
-        flat[:, :qkv_rows].reshape(depth, 3, head_width), (1, 0, 2)
-    ).astype(wide)
-    grad_wout = flat[:, qkv_rows:].reshape(head_width, depth).astype(wide)
-
-    running_wide = running.astype(wide)
-    unit_all = (normed.astype(wide) - ln1_bias) / ln1_gain
+    dqkv[1], table_sums[1] = attend_back(1, in_order(received[1]))
+    feed_own = (
+        feed_near[:rows].astype(wide) + feed_beside[1].astype(wide) + feed_across.astype(wide)
+    )
+    layer_out = (hidden_in + feed_own + down_bias).astype(low)
     sums = (sums_near + sums_far).reshape(parts, team_units)
-    up_sums = lax.dynamic_update_slice_in_dim(
-        jnp.zeros((parts, TEAM * team_units), wide), sums, member * team_units, 1
-    )
-    table_line = table_gradient(hot, table_sums, heads).reshape(1, -1)
-    table_all = lax.dynamic_update_slice_in_dim(
-        jnp.zeros((parts, table_line.shape[1]), wide), table_line, part, 0
-    )
+    up_sums = jnp.zeros((parts, TEAM * team_units), wide)
+    for k in range(parts):
+        up_sums = lax.dynamic_update_slice(
+            up_sums, sums[k : k + 1], (part ^ k, member * team_units)
+        )
     lines = [
-        jnp.sum(running_wide * unit_all, axis=0), jnp.sum(running_wide, axis=0),
         jnp.sum(grad_second * unit2, axis=0), jnp.sum(grad_second, axis=0),
         jnp.sum(grad_part, axis=0),
     ]
-    small = jnp.concatenate(lines + [up_sums.reshape(-1), table_all.reshape(-1)])
+    early_lines = jnp.concatenate(lines + [up_sums.reshape(-1)])
+    dqkv[1], wout_grad, layer_out, early_lines, normed_keep, normed_send = sync(
+        dqkv[1], wout_grad, layer_out, early_lines, normed_keep, normed_send
+    )
+
+    running, line_sums = input_cotangent(
+        dqkv, w_cat, normed, jnp.stack([ln1_bias, 1.0 / ln1_gain])
+    )
+    grad_first = lax.psum_scatter(running, "mp", scatter_dimension=0, tiled=True).astype(wide)
+
+    late = [after(one, running) for one in dqkv]
+    qkv_send = jnp.concatenate([dot_tn(normed_send, one).astype(low) for one in late], axis=1)
+    qkv_keep = jnp.concatenate([dot_tn(normed_keep, one) for one in late], axis=1)
+    table_line = table_gradient(
+        hot, jnp.concatenate([one[0:2] for one in table_sums]),
+        jnp.concatenate([one[2:4] for one in table_sums]),
+    ).reshape(1, -1)
+    table_all = lax.dynamic_update_slice_in_dim(
+        jnp.zeros((parts, table_line.shape[1]), wide), table_line, part, 0
+    )
+    small = jnp.concatenate(
+        [
+            jnp.sum(line_sums[0:8], axis=0), jnp.sum(line_sums[8:16], axis=0),
+            early_lines, table_all.reshape(-1),
+        ]
+    )
     small = jnp.pad(small, (0, -small.shape[0] % 1024)).reshape(-1, 1024)
-    for axis, size in (("team", TEAM), ("copy", copies), ("mp", parts)):
-        for bit in bits_of(size):
-            small = small + flip(small, axis, bit)
+
+    qkv_got = flip(qkv_send, "team", 1)
+    small_got = flip(small, "team", 1)
+    wout_got = flip(wout_grad[2:], "mp", 2)
+    qkv_grad = (qkv_keep + qkv_got.astype(wide)).astype(low)
+    small = small + small_got
+    wout_grad = (wout_grad[:2].astype(wide) + wout_got.astype(wide)).astype(low)
+    qkv_grad, small, wout_grad, ff_piece = sync(qkv_grad, small, wout_grad, ff_piece)
+
+    qkv_grad = halve(qkv_grad.reshape(2, copies, -1, qkv_grad.shape[1]), 0, "team", 2)
+    small_got = flip(small, "team", 2)
+    wout_got = flip(wout_grad[1:], "mp", 1)
+    ff_all = spread(ff_piece, "copy", copies)
+    small = small + small_got
+    wout_grad = (wout_grad[:1].astype(wide) + wout_got.astype(wide)).astype(low)
+    qkv_grad, small, wout_grad, ff_all = sync(qkv_grad, small, wout_grad, ff_all)
+
+    for bit in reversed(bits_of(copies)):
+        qkv_grad = halve(qkv_grad.reshape((2, -1) + qkv_grad.shape[1:]), 0, "copy", bit)
+    for bit in bits_of(copies):
+        small = small + flip(small, "copy", bit)
+    ff_all = double(ff_all, "team", 2)
+    wout_grad = wout_grad.reshape(-1, depth)
+    qkv_grad = qkv_grad.reshape(-1, 3 * head_width)
+    columns = [
+        jnp.concatenate(
+            [
+                qkv_grad[:, (3 * pair + slot) * pair_width : (3 * pair + slot + 1) * pair_width]
+                for pair in range(pairs)
+            ],
+            axis=1,
+        )
+        for slot in range(3)
+    ] + [wout_grad[:, start : start + head_width] for start in range(0, depth, head_width)]
+    flat, small, ff_all = sync(jnp.concatenate(columns), small, ff_all)
+
+    flat = spread(flat, "copy", copies)
+    small = small + flip(small, "mp", 1)
+    ff_all = double(ff_all, "team", 1)
+    flat, small, ff_all = sync(flat, small, ff_all)
+    flat = double(flat, "team", 2)
+    small = small + flip(small, "mp", 2)
+    grad_up, grad_down = feed_grads_out(
+        ff_all.reshape(TEAM * copies, 2, unit, depth), copies
+    )
+    flat, small, grad_up, grad_down = sync(flat, small, grad_up, grad_down)
+    flat = double(flat, "team", 1)
+    grad_qkv, grad_wout = attention_grads_out(
+        flat.reshape(TEAM * copies, -1, head_width), depth, head_width
+    )
+
     small = small.reshape(-1)
     lines = [small[index * depth : (index + 1) * depth] for index in range(5)]
     start = 5 * depth
@@ -765,6 +994,10 @@
     grad_table = lax.dynamic_index_in_dim(table_all, part, 0, keepdims=False).reshape(
         rel_table.shape
     )
+
+    grad_first = after(grad_first, grad_qkv, grad_wout)
+    grad_first_norm = normalize_backward(grad_first, ln1_gain, unit1, inverse1)
+    grad_tokens = (grad_hidden + grad_first_norm).astype(low)
     return (
         layer_out, grad_tokens, lines[0], lines[1], grad_qkv, grad_table, grad_wout,
         lines[2], lines[3], grad_up, grad_up_bias, grad_down, lines[4],

time: 553 us -> 464 us (0.84)
  waiting for transfers between devices: 237 us -> 141 us
  Pallas kernels: 87 us -> 123 us
  local copies, waits for them, and re-layouts: 58.8 us -> 40.3 us
    ppermute x18 -> x6, waiting for transfers between devices: 165 us -> 0.02 us  [the longest x1 0.01 us: body(): right2 = lax.ppermute(right1, 'mp', to_right[1:])]
    ppermute x30 -> x50, waiting for transfers between devices: 71.6 us -> 131 us  [flip(): return lax.ppermute(value, axis, [(i, i ^ bit) for i in range(size)])]
    pallas_call x5 -> x10, Pallas kernels: 87 us -> 123 us  [the longest x2 38.9 us: attention_backward(): pl.pallas_call(functools.partial(attention_backward_kernel, first_head=fi...]
    ppermute x18 -> x6, starting transfers between devices: 30.3 us -> 9.36 us  [the longest x1 3.64 us: body(): right1 = lax.ppermute(piece, 'mp', to_right)]
    ppermute x30 -> x50, starting transfers between devices: 38.9 us -> 57.6 us  [flip(): return lax.ppermute(value, axis, [(i, i ^ bit) for i in range(size)])]
    select_n x0 -> x11, other arithmetic: none -> 14.8 us  [the longest x9 14.6 us: double(): jnp.where(mine == 0, jnp.stack([value, other]), jnp.stack([other, value]))]
    convert_element_type x9, other arithmetic: 21.7 us -> 11.9 us  [the longest x1 3.18 us: body(): layer_out = (hidden_in + feed_own + down_bias).astype(low)]
    unnamed x100 -> x140, local copies, waits for them, and re-layouts: 22.6 us -> 12.9 us
  transfers between devices with their start and end apart: 51 -> 59, of which waited for: 24 -> 26; matrix products, arithmetic and copies ran while one was open for 19% -> 17% of each run, Pallas kernels for 14% -> 23%
where the time goes in v3:
time: 464 us; the launch traced here: 455 us
  waiting for transfers between devices  141 us (30%)
  Pallas kernels  123 us (27%)
  starting transfers between devices  67 us (14%)
  other arithmetic  52.9 us (11%)
  local copies, waits for them, and re-layouts  40.3 us (9%)
  between operations  15.7 us (3%)
  matrix products  15.5 us (3%)
    ppermute x50, waiting for transfers between devices, flip(): return lax.ppermute(value, axis, [(i, i ^ bit) for i in range(size)])  131 us
    ppermute x50, starting transfers between devices, flip(): return lax.ppermute(value, axis, [(i, i ^ bit) for i in range(size)])  57.6 us
    pallas_call x2, Pallas kernels, attention_backward(): pl.pallas_call(functools.partial(attention_backward_kernel, first_head=fi...  38.9 us
    pallas_call x2, Pallas kernels, feed_forward(): pl.pallas_call(functools.partial(feed_kernel, unit=unit), grid=(FEED_STEP...  26.3 us
    pallas_call x2, Pallas kernels, attention_forward(): pl.pallas_call(functools.partial(attention_forward_kernel, first_head=fir...  23.3 us
    select_n x9, other arithmetic, double(): jnp.where(mine == 0, jnp.stack([value, other]), jnp.stack([other, value]))  14.6 us
    unnamed x140, local copies, waits for them, and re-layouts  12.9 us
    pallas_call x1, Pallas kernels, weight_grads(): pl.pallas_call(weight_grad_kernel, grid_spec=pltpu.PrefetchScalarGridSpec...  12 us
  transfers between devices with their start and end apart: 59, of which 26 were waited for; matrix products, arithmetic and copies ran while one was open for 17% of the time, Pallas kernels for 23%

profile of v3, /device:TPU:0, one launch (start us, length us, event | category | flops | bytes accessed | tf_op | source)
XLA Modules:
  0.0 455.3 jit_solution(18404401531767611212)
XLA Ops:
  11.6 3.0 collective-permute-start.1
  18.0 3.6 collective-permute-start.6
  22.9 2.7 collective-permute-start.3
  27.5 4.9 %collective-permute-done.1 = bf16[384,1024]{1,0:T(8,128)(2,1)} collective-permute-done((bf16[384,1024]{1,0:T(8,128)(2,1)}, bf16[384,1024]{1,0:T(8,128)(2,1)}, u32[]{:S(2)}, u32[]{:S(2)}) %collective-permute-start.1) | collective-permute-done | bytes 786464 | tf_op jit(solution)/shard_map/ppermute | solution.py:374
  34.0 34.7 %collective-permute-done.3 = f32[1024]{0:T(1024)S(1)} collective-permute-done((f32[1024]{0:T(1024)}, f32[1024]{0:T(1024)S(1)}, u32[]{:S(2)}, u32[]{:S(2)}) %collective-permute-start.3) | collective-permute-done | bytes 4128 | tf_op jit(solution)/shard_map/ppermute | solution.py:374
  69.0 4.6 %collective-permute-done.4 = f32[1024]{0:T(1024)S(1)} collective-permute-done((f32[1024]{0:T(1024)}, f32[1024]{0:T(1024)S(1)}, u32[]{:S(2)}, u32[]{:S(2)}) %collective-permute-start.4) | collective-permute-done | bytes 4128 | tf_op jit(solution)/shard_map/ppermute | solution.py:374
  76.1 2.6 copy.59
  80.1 2.4 pad_maximum_fusion.1.grad_ref.grad_a
  82.5 2.7 pad_maximum_fusion.2.grad_ref.grad_b
  85.2 6.8 %all-gather.2.cloned.1.call-done.normed_ref = bf16[1536,1024]{1,0:T(8,128)(2,1)} async-done(((bf16[384,1024]{1,0:T(8,128)(2,1)}), bf16[1536,1024]{1,0:T(8,128)(2,1)}) %all-gather.2.cloned.1.call-update) | async-done | bytes 3145744 | tf_op jit(solution)/shard_map/all_gather | solution.py:709
  96.6 3.7 convolution_convert_fusion.1.qkv_ref
  100.4 11.8 %attention_forward.2 = (bf16[1536,128]{1,0:T(8,128)(2,1)S(1)}, f32[8,1536]{1,0:T(8,128)S(1)}) custom-call(s32[1]{0:T(128)} %bitcast.12.cut_ref, bf16[1536,384]{1,0:T(8,128)(2,1)S(1)} %convolution_convert_fusion.1.qkv_ref, f32[8,512]{1,0:T(8,128)S(1)} %select_maximum_fusion.4.bias_ref), custom_call_target="tpu_custom_call" | custom-call | flops 2415919104 | bytes 1572864 | tf_op jit(solution)/shard_map/attention_forward/pallas_call | solution.py:136
  112.8 1.8 convolution_convert_fusion.qkv_ref
  119.1 1.8 collective-permute-start.12
  121.0 2.7 collective-permute-start.14
  123.7 2.5 collective-permute-start.15
  126.2 11.6 %attention_forward.3 = (bf16[1536,128]{1,0:T(8,128)(2,1)S(1)}, f32[8,1536]{1,0:T(8,128)S(1)}) custom-call(s32[1]{0:T(128)} %bitcast.12.cut_ref, bf16[1536,384]{1,0:T(8,128)(2,1)S(1)} %convolution_convert_fusion.qkv_ref, f32[8,512]{1,0:T(8,128)S(1)} %select_maximum_fusion.4.bias_ref), custom_call_target="tpu_custom_call" | custom-call | flops 2415919104 | bytes 1572864 | tf_op jit(solution)/shard_map/attention_forward/pallas_call | solution.py:136
  140.4 1.9 maximum_select_fusion.4.across_ref
  142.4 3.2 collective-permute-done.16
  147.4 2.3 collective-permute-start.17
  149.6 2.4 collective-permute-start.19
  152.9 6.4 %collective-permute-done.18 = bf16[384,128]{1,0:T(8,128)(2,1)S(1)} collective-permute-done((bf16[384,128]{1,0:T(8,128)(2,1)S(1)}, bf16[384,128]{1,0:T(8,128)(2,1)S(1)}, u32[]{:S(2)}, u32[]{:S(2)}) %collective-permute-start.18) | collective-permute-done | bytes 98336 | tf_op jit(solution)/shard_map/ppermute | solution.py:374
  159.3 3.7 collective-permute-done.21
  171.4 13.1 %feed_forward.2 = (bf16[768,1024]{1,0:T(8,128)(2,1)}, bf16[768,1024]{1,0:T(8,128)(2,1)}, bf16[768,1024]{1,0:T(8,128)(2,1)}, bf16[768,1024]{1,0:T(8,128)(2,1)}, f32[1,1024]{1,0:T(1,128)}) custom-call(bf16[2,320,1024]{2,1,0:T(8,128)(2,1)} %copy-done.19, bf16[2,320,1024]{2,1,0:T(8,128)(2,1)} %maximum_select_fusion.3.beside_ref, ...), custom_call_target="tpu_custom_call" | custom-call | flops 6442450944 | bytes 10485760 | tf_op jit(solution)/shard_map/feed_forward/pallas_call | solution.py:619
  184.5 3.3 collective-permute-done.23
  187.9 2.2 collective-permute-done.25
  191.3 13.2 %feed_forward.3 = (bf16[768,1024]{1,0:T(8,128)(2,1)}, bf16[768,1024]{1,0:T(8,128)(2,1)}, bf16[768,1024]{1,0:T(8,128)(2,1)}, bf16[768,1024]{1,0:T(8,128)(2,1)}, f32[1,1024]{1,0:T(1,128)}) custom-call(bf16[2,320,1024]{2,1,0:T(8,128)(2,1)} %copy-done.19, bf16[2,320,1024]{2,1,0:T(8,128)(2,1)} %maximum_select_fusion.3.beside_ref, ...), custom_call_target="tpu_custom_call" | custom-call | flops 6442450944 | bytes 10485760 | tf_op jit(solution)/shard_map/feed_forward/pallas_call | solution.py:619
  204.5 2.1 slice.207
  209.2 2.3 add_convert_fusion
  213.0 12.0 %weight_grads.1 = bf16[4,2,2,128,1024]{4,3,2,1,0:T(8,128)(2,1)} custom-call(s32[1]{0:T(128)} %bitcast.37.part_ref, bf16[768,1024]{1,0:T(8,128)(2,1)} %get-tuple-element.139.act_a, bf16[768,1024]{1,0:T(8,128)(2,1)} %get-tuple-element.144.act_b, bf16[768,1024]{1,0:T(8,128)(2,1)} %get-tuple-element.145.pre_a, bf16[768,1024]{1,0:T(8,128)(2,1)} %get-tuple-element.146.pre_b, ...), custom_call_target="tpu_custom_call" | custom-call | flops 6442450944 | bytes 16777216 | tf_op jit(solution)/shard_map/weight_grads/pallas_call | solution.py:658
  225.0 6.3 %collective-permute-done.27 = bf16[384,1024]{1,0:T(8,128)(2,1)S(1)} collective-permute-done((bf16[384,1024]{1,0:T(8,128)(2,1)}, bf16[384,1024]{1,0:T(8,128)(2,1)S(1)}, u32[]{:S(2)}, u32[]{:S(2)}) %collective-permute-start.27) | collective-permute-done | bytes 786464 | tf_op jit(solution)/shard_map/ppermute | solution.py:374
  232.2 2.1 fusion.45
  234.3 1.9 convolution_convert_fusion.3
  242.9 2.3 copy.49.weight_a
  245.3 2.4 copy.50.weight_b
  250.2 2.2 collective-permute-start.31
  252.5 2.4 collective-permute-start.33
  256.1 2.1 fusion
  259.2 3.2 collective-permute-done.32
  267.1 19.4 %attention_backward.2 = (bf16[1536,384]{1,0:T(8,128)(2,1)}, f32[8,512]{1,0:T(8,128)}) custom-call(s32[1]{0:T(128)} %bitcast.12.cut_ref, bf16[1536,384]{1,0:T(8,128)(2,1)} %copy-done.5, bf16[1536,128]{1,0:T(8,128)(2,1)} %bitcast.192, bf16[1536,128]{1,0:T(8,128)(2,1)} %copy-done.2, f32[8,1536]{1,0:T(8,128)} %copy-done.6, f32[8,512]{1,0:T(8,128)} %select_maximum_fusion.3.bias_ref), custom_call_target="tpu_custom_call" | custom-call | flops 6039797760 | bytes 3145728 | tf_op jit(solution)/shard_map/attention_backward/pallas_call | solution.py:286
  287.3 7.2 %collective-permute-done.34 = bf16[4,2,32,1024]{3,2,0,1:T(8,128)(2,1)S(1)} collective-permute-done((bf16[4,2,32,1024]{3,2,0,1:T(8,128)(2,1)S(1)}, bf16[4,2,32,1024]{3,2,0,1:T(8,128)(2,1)S(1)}, u32[]{:S(2)}, u32[]{:S(2)}) %collective-permute-start.34) | collective-permute-done | bytes 524320 | tf_op jit(solution)/shard_map/ppermute | solution.py:374
  297.3 19.5 %attention_backward.3 = (bf16[1536,384]{1,0:T(8,128)(2,1)}, f32[8,512]{1,0:T(8,128)}) custom-call(s32[1]{0:T(128)} %bitcast.12.cut_ref, bf16[1536,384]{1,0:T(8,128)(2,1)} %copy-done.4, bf16[1536,128]{1,0:T(8,128)(2,1)} %bitcast.191, bf16[1536,128]{1,0:T(8,128)(2,1)} %copy-done.3, f32[8,1536]{1,0:T(8,128)} %copy-done.7, f32[8,512]{1,0:T(8,128)} %select_maximum_fusion.3.bias_ref), custom_call_target="tpu_custom_call" | custom-call | flops 6039797760 | bytes 3145728 | tf_op jit(solution)/shard_map/attention_backward/pallas_call | solution.py:286
  318.4 3.2 fusion.18
  323.2 8.9 %input_cotangent.1 = (bf16[1536,1024]{1,0:T(8,128)(2,1)}, f32[16,1024]{1,0:T(8,128)}) custom-call(bf16[1536,384]{1,0:T(8,128)(2,1)} %get-tuple-element.177.grad_a, bf16[1536,384]{1,0:T(8,128)(2,1)} %get-tuple-element.178.grad_b, bf16[1024,384]{1,0:T(8,128)(2,1)} %copy.49.weight_a, bf16[1024,384]{1,0:T(8,128)(2,1)} %copy.50.weight_b, ...), custom_call_target="tpu_custom_call" | custom-call | flops 2415919104 | bytes 10223616 | tf_op jit(solution)/shard_map/input_cotangent/pallas_call | solution.py:544
  332.0 8.7 %collective-permute-start.42 = (bf16[2,32,1024]{2,1,0:T(8,128)(2,1)S(1)}, bf16[2,32,1024]{2,1,0:T(8,128)(2,1)S(1)}, u32[]{:S(2)}, u32[]{:S(2)}) collective-permute-start(bf16[2,32,1024]{2,1,0:T(8,128)(2,1)S(1)} %slice.236), channel_id=1, source_target_pairs={{0,2},{1,3},{2,0},{3,1},{4,6},{5,7},{6,4},{7,5},{8,10},{9,11},{10,... | collective-permute-start | bytes 393224 | tf_op jit(solution)/shard_map/ppermute | solution.py:374
  341.7 2.7 convolution_convert_fusion.5
  348.3 7.0 %collective-permute-done.42 = bf16[2,32,1024]{2,1,0:T(8,128)(2,1)S(1)} collective-permute-done((bf16[2,32,1024]{2,1,0:T(8,128)(2,1)S(1)}, bf16[2,32,1024]{2,1,0:T(8,128)(2,1)S(1)}, u32[]{:S(2)}, u32[]{:S(2)}) %collective-permute-start.42) | collective-permute-done | bytes 131104 | tf_op jit(solution)/shard_map/ppermute | solution.py:374
  355.6 3.6 reduce-scatter.5.cloned.1.call-done
  365.6 7.1 %collective-permute-done.44 = f32[10,1024]{1,0:T(8,128)S(1)} collective-permute-done((f32[10,1024]{1,0:T(8,128)S(1)}, f32[10,1024]{1,0:T(8,128)S(1)}, u32[]{:S(2)}, u32[]{:S(2)}) %collective-permute-start.44) | collective-permute-done | bytes 40992 | tf_op jit(solution)/shard_map/ppermute | solution.py:374
  373.9 1.6 collective-permute-done.46
  377.0 1.7 collective-permute-start.47
  379.7 3.8 collective-permute-done.48
  383.7 18.2 %collective-permute-done.49 = bf16[2,256,1024]{2,1,0:T(8,128)(2,1)S(1)} collective-permute-done((bf16[2,256,1024]{2,1,0:T(8,128)(2,1)S(1)}, bf16[2,256,1024]{2,1,0:T(8,128)(2,1)S(1)}, u32[]{:S(2)}, u32[]{:S(2)}) %collective-permute-start.49) | collective-permute-done | bytes 1048608 | tf_op jit(solution)/shard_map/ppermute | solution.py:374
  401.9 1.9 maximum_select_fusion.1
  403.8 1.7 collective-permute-start.50
  405.6 2.1 collective-permute-start.51
  407.6 5.2 %collective-permute-done.51 = f32[10,1024]{1,0:T(8,128)S(1)} collective-permute-done((f32[10,1024]{1,0:T(8,128)S(1)}, f32[10,1024]{1,0:T(8,128)S(1)}, u32[]{:S(2)}, u32[]{:S(2)}) %collective-permute-start.51) | collective-permute-done | bytes 40992 | tf_op jit(solution)/shard_map/ppermute | solution.py:374
  413.0 2.4 maximum_select_fusion
  416.9 7.5 %feed_grads_out.1 = (f32[1024,1024]{1,0:T(8,128)}, f32[1024,1024]{1,0:T(8,128)}) custom-call(bf16[8,2,128,1024]{3,2,1,0:T(8,128)(2,1)} %bitcast.167), custom_call_target="tpu_custom_call" | custom-call | bytes 12582912 | tf_op jit(solution)/shard_map/feed_grads_out/pallas_call | solution.py:423
  424.3 1.7 collective-permute-done.54
  426.0 3.4 collective-permute-done.53
  434.1 4.0 maximum_select_fusion.2
  438.1 6.0 %attention_grads_out.1 = (f32[3,1024,256]{2,1,0:T(8,128)}, f32[256,1024]{1,0:T(8,128)}) custom-call(bf16[8,512,256]{2,1,0:T(8,128)(2,1)} %bitcast.168), custom_call_target="tpu_custom_call" | custom-call | bytes 6291456 | tf_op jit(solution)/shard_map/attention_grads_out/pallas_call | solution.py:463
  445.5 2.9 fusion.12
  (363 shorter events, 91.4 us)
Async XLA Ops:
  7.2 84.7 %all-gather.2.cloned.1.call-start = ((), (), s32[]{:S(2)}) async-start(), calls=%async_computation.2 | async-start | bytes 3932160 | tf_op jit(solution)/shard_map/all_gather | solution.py:709
  11.5 347.7 %reduce-scatter.5.cloned.1.call-start = ((), (), s32[]{:S(2)}) async-start(), calls=%async_computation.4 | async-start | bytes 4718592 | tf_op jit(solution)/shard_map/reduce_scatter | solution.py:835
  11.6 20.9 %collective-permute-start.1 = (bf16[384,1024]{1,0:T(8,128)(2,1)}, bf16[384,1024]{1,0:T(8,128)(2,1)}, u32[]{:S(2)}, u32[]{:S(2)}) collective-permute-start(bf16[384,1024]{1,0:T(8,128)(2,1)} %param.29), channel_id=1, source_target_pairs={{0,8},{4,12},{8,0},{12,4},{1,9},{5,13},{9,1},{13,5},{2,10},{6,14},... | collective-permute-start | bytes 2359304 | tf_op jit(solution)/shard_map/ppermute | solution.py:374
  14.6 65.5 %collective-permute-start = (bf16[384,1024]{1,0:T(8,128)(2,1)}, bf16[384,1024]{1,0:T(8,128)(2,1)}, u32[]{:S(2)}, u32[]{:S(2)}) collective-permute-start(bf16[384,1024]{1,0:T(8,128)(2,1)} %param.29), channel_id=1, source_target_pairs={{0,4},{4,0},{8,12},{12,8},{1,5},{5,1},{9,13},{13,9},{2,6},{6,2},{1... | collective-permute-start | bytes 2359304 | tf_op jit(solution)/shard_map/ppermute | solution.py:374
  18.0 74.0 %collective-permute-start.6 = (bf16[320,1024]{1,0:T(8,128)(2,1)}, bf16[320,1024]{1,0:T(8,128)(2,1)S(1)}, u32[]{:S(2)}, u32[]{:S(2)}) collective-permute-start(bf16[320,1024]{1,0:T(8,128)(2,1)} %dynamic-slice_bitcast_fusion), channel_id=1, source_target_pairs={{0,1},{1,2},{2,3},{4,5},{5,6},{6,7},{8,9},{9,10},{10,11},{12,13},{... | collective-permute-start | bytes 1966088 | tf_op jit(solution)/shard_map/ppermute | solution.py:726
  21.6 70.3 %collective-permute-start.7 = (bf16[320,1024]{1,0:T(8,128)(2,1)}, bf16[320,1024]{1,0:T(8,128)(2,1)}, u32[]{:S(2)}, u32[]{:S(2)}) collective-permute-start(bf16[320,1024]{1,0:T(8,128)(2,1)} %dynamic-slice_bitcast_fusion), channel_id=1, source_target_pairs={{1,0},{2,1},{3,2},{5,4},{6,5},{7,6},{9,8},{10,9},{11,10},{13,12},{... | collective-permute-start | bytes 1966088 | tf_op jit(solution)/shard_map/ppermute | solution.py:727
  22.9 45.8 %collective-permute-start.3 = (f32[1024]{0:T(1024)}, f32[1024]{0:T(1024)S(1)}, u32[]{:S(2)}, u32[]{:S(2)}) collective-permute-start(f32[1024]{0:T(1024)} %param.26), channel_id=1, source_target_pairs={{0,1},{1,0},{2,3},{3,2},{4,5},{5,4},{6,7},{7,6},{8,9},{9,8},{10,11... | collective-permute-start | bytes 12296 | tf_op jit(solution)/shard_map/ppermute | solution.py:374
  32.4 50.1 %collective-permute-start.2 = (bf16[384,1024]{1,0:T(8,128)(2,1)}, bf16[384,1024]{1,0:T(8,128)(2,1)}, u32[]{:S(2)}, u32[]{:S(2)}) collective-permute-start(bf16[384,1024]{1,0:T(8,128)(2,1)} %collective-permute-done.1), channel_id=1, source_target_pairs={{0,4},{4,0},{8,12},{12,8},{1,5},{5,1},{9,13},{13,9},{2,6},{6,2},{1... | collective-permute-start | bytes 2359304 | tf_op jit(solution)/shard_map/ppermute | solution.py:374
  68.7 4.9 %collective-permute-start.4 = (f32[1024]{0:T(1024)}, f32[1024]{0:T(1024)S(1)}, u32[]{:S(2)}, u32[]{:S(2)}) collective-permute-start(f32[1024]{0:T(1024)} %param.26), channel_id=1, source_target_pairs={{0,2},{1,3},{2,0},{3,1},{4,6},{5,7},{6,4},{7,5},{8,10},{9,11},{10,... | collective-permute-start | bytes 12296 | tf_op jit(solution)/shard_map/ppermute | solution.py:374
  73.6 5.8 %collective-permute-start.5 = (f32[1024]{0:T(1024)}, f32[1024]{0:T(1024)S(1)}, u32[]{:S(2)}, u32[]{:S(2)}) collective-permute-start(f32[1024]{0:T(1024)} %param.26), channel_id=1, source_target_pairs={{0,3},{1,2},{2,1},{3,0},{4,7},{5,6},{6,5},{7,4},{8,11},{9,10},{10,... | collective-permute-start | bytes 12296 | tf_op jit(solution)/shard_map/ppermute | solution.py:374
  76.1 20.6 %copy-start.15 = (bf16[3,1024,128]{1,2,0:T(8,128)(2,1)}, bf16[3,1024,128]{1,2,0:T(8,128)(2,1)S(1)}, u32[]{:S(2)}) copy-start(bf16[3,1024,128]{1,2,0:T(8,128)(2,1)S(1)} %copy.58) | copy-start | bytes 2359300
  91.9 24.2 %collective-permute-start.8 = (bf16[320,1024]{1,0:T(8,128)(2,1)S(1)}, bf16[320,1024]{1,0:T(8,128)(2,1)S(1)}, u32[]{:S(2)}, u32[]{:S(2)}) collective-permute-start(bf16[320,1024]{1,0:T(8,128)(2,1)S(1)} %collective-permute-done.6), channel_id=1, source_target_pairs={{1,2},{2,3},{5,6},{6,7},{9,10},{10,11},{13,14},{14,15},{17,18},{18... | collective-permute-start | bytes 1966088 | tf_op jit(solution)/shard_map/ppermute | solution.py:776
  92.6 23.5 %collective-permute-start.9 = (bf16[320,1024]{1,0:T(8,128)(2,1)}, bf16[320,1024]{1,0:T(8,128)(2,1)S(1)}, u32[]{:S(2)}, u32[]{:S(2)}) collective-permute-start(bf16[320,1024]{1,0:T(8,128)(2,1)} %collective-permute-done.7), channel_id=1, source_target_pairs={{1,0},{2,1},{5,4},{6,5},{9,8},{10,9},{13,12},{14,13},{17,16},{18,1... | collective-permute-start | bytes 1966088 | tf_op jit(solution)/shard_map/ppermute | solution.py:777
  95.1 19.5 %collective-permute-start.10 = (bf16[1,320,1024]{2,1,0:T(8,128)(2,1)S(1)}, bf16[1,320,1024]{2,1,0:T(8,128)(2,1)S(1)}, u32[]{:S(2)}, u32[]{:S(2)}) collective-permute-start(bf16[1,320,1024]{2,1,0:T(8,128)(2,1)S(1)} %select_bitcast_fusion.1), channel_id=1, source_target_pairs={{0,16},{16,0},{1,17},{17,1},{2,18},{18,2},{3,19},{19,3},{4,20},{20... | collective-permute-start | bytes 1966088 | tf_op jit(solution)/shard_map/ppermute | solution.py:374
  117.9 21.0 %collective-permute-start.13 = (bf16[1,320,1024]{2,1,0:T(8,128)(2,1)}, bf16[1,320,1024]{2,1,0:T(8,128)(2,1)}, u32[]{:S(2)}, u32[]{:S(2)}) collective-permute-start(bf16[1,320,1024]{2,1,0:T(8,128)(2,1)} %add_bitcast_fusion), channel_id=1, source_target_pairs={{0,16},{16,0},{1,17},{17,1},{2,18},{18,2},{3,19},{19,3},{4,20},{20... | collective-permute-start | bytes 1966088 | tf_op jit(solution)/shard_map/ppermute | solution.py:374
  118.4 27.1 %collective-permute-start.11 = (bf16[320,1024]{1,0:T(8,128)(2,1)}, bf16[320,1024]{1,0:T(8,128)(2,1)S(1)}, u32[]{:S(2)}, u32[]{:S(2)}) collective-permute-start(bf16[320,1024]{1,0:T(8,128)(2,1)} %copy-done.32), channel_id=1, source_target_pairs={{2,3},{6,7},{10,11},{14,15},{18,19},{22,23},{26,27},{30,31}} | collective-permute-start | bytes 1966088 | tf_op jit(solution)/shard_map/ppermute | solution.py:787
  119.1 26.4 %collective-permute-start.12 = (bf16[320,1024]{1,0:T(8,128)(2,1)}, bf16[320,1024]{1,0:T(8,128)(2,1)S(1)}, u32[]{:S(2)}, u32[]{:S(2)}) collective-permute-start(bf16[320,1024]{1,0:T(8,128)(2,1)} %copy-done.33), channel_id=1, source_target_pairs={{1,0},{5,4},{9,8},{13,12},{17,16},{21,20},{25,24},{29,28}} | collective-permute-start | bytes 1966088 | tf_op jit(solution)/shard_map/ppermute | solution.py:788
  121.0 21.4 %collective-permute-start.14 = (bf16[384,128]{1,0:T(8,128)(2,1)S(1)}, bf16[384,128]{1,0:T(8,128)(2,1)S(1)}, u32[]{:S(2)}, u32[]{:S(2)}) collective-permute-start(bf16[384,128]{1,0:T(8,128)(2,1)S(1)} %get-tuple-element.271), channel_id=1, source_target_pairs={{0,1},{1,0},{2,3},{3,2},{4,5},{5,4},{6,7},{7,6},{8,9},{9,8},{10,11... | collective-permute-start | bytes 294920 | tf_op jit(solution)/shard_map/ppermute | solution.py:374
  123.7 18.6 %collective-permute-start.15 = (bf16[384,128]{1,0:T(8,128)(2,1)S(1)}, bf16[384,128]{1,0:T(8,128)(2,1)S(1)}, u32[]{:S(2)}, u32[]{:S(2)}) collective-permute-start(bf16[384,128]{1,0:T(8,128)(2,1)S(1)} %get-tuple-element.270), channel_id=1, source_target_pairs={{0,2},{1,3},{2,0},{3,1},{4,6},{5,7},{6,4},{7,5},{8,10},{9,11},{10,... | collective-permute-start | bytes 294920 | tf_op jit(solution)/shard_map/ppermute | solution.py:374
  138.9 6.6 %collective-permute-start.16 = (bf16[384,128]{1,0:T(8,128)(2,1)S(1)}, bf16[384,128]{1,0:T(8,128)(2,1)S(1)}, u32[]{:S(2)}, u32[]{:S(2)}) collective-permute-start(bf16[384,128]{1,0:T(8,128)(2,1)S(1)} %get-tuple-element.269), channel_id=1, source_target_pairs={{0,3},{1,2},{2,1},{3,0},{4,7},{5,6},{6,5},{7,4},{8,11},{9,10},{10,... | collective-permute-start | bytes 294920 | tf_op jit(solution)/shard_map/ppermute | solution.py:374
  145.6 17.9 %collective-permute-start.20 = (bf16[2,2,64,1024]{3,2,1,0:T(8,128)(2,1)S(1)}, bf16[2,2,64,1024]{3,2,1,0:T(8,128)(2,1)S(1)}, u32[]{:S(2)}, u32[]{:S(2)}) collective-permute-start(bf16[2,2,64,1024]{3,2,1,0:T(8,128)(2,1)S(1)} %get-tuple-element.265), channel_id=1, source_target_pairs={{0,4},{4,0},{8,12},{12,8},{1,5},{5,1},{9,13},{13,9},{2,6},{6,2},{1... | collective-permute-start | bytes 1572872 | tf_op jit(solution)/shard_map/ppermute | solution.py:374
  145.8 17.2 %collective-permute-start.21 = (bf16[1,320,1024]{2,1,0:T(8,128)(2,1)S(1)}, bf16[1,320,1024]{2,1,0:T(8,128)(2,1)S(1)}, u32[]{:S(2)}, u32[]{:S(2)}) collective-permute-start(bf16[1,320,1024]{2,1,0:T(8,128)(2,1)S(1)} %select_bitcast_fusion), channel_id=1, source_target_pairs={{0,16},{16,0},{1,17},{17,1},{2,18},{18,2},{3,19},{19,3},{4,20},{20... | collective-permute-start | bytes 1966088 | tf_op jit(solution)/shard_map/ppermute | solution.py:374
  147.4 5.4 %collective-permute-start.17 = (bf16[384,128]{1,0:T(8,128)(2,1)S(1)}, bf16[384,128]{1,0:T(8,128)(2,1)S(1)}, u32[]{:S(2)}, u32[]{:S(2)}) collective-permute-start(bf16[384,128]{1,0:T(8,128)(2,1)S(1)} %get-tuple-element.268), channel_id=1, source_target_pairs={{0,1},{1,0},{2,3},{3,2},{4,5},{5,4},{6,7},{7,6},{8,9},{9,8},{10,11... | collective-permute-start | bytes 294920 | tf_op jit(solution)/shard_map/ppermute | solution.py:374
  149.6 9.6 %collective-permute-start.18 = (bf16[384,128]{1,0:T(8,128)(2,1)S(1)}, bf16[384,128]{1,0:T(8,128)(2,1)S(1)}, u32[]{:S(2)}, u32[]{:S(2)}) collective-permute-start(bf16[384,128]{1,0:T(8,128)(2,1)S(1)} %get-tuple-element.267), channel_id=1, source_target_pairs={{0,2},{1,3},{2,0},{3,1},{4,6},{5,7},{6,4},{7,5},{8,10},{9,11},{10,... | collective-permute-start | bytes 294920 | tf_op jit(solution)/shard_map/ppermute | solution.py:374
  149.6 13.8 %collective-permute-start.19 = (bf16[384,128]{1,0:T(8,128)(2,1)S(1)}, bf16[384,128]{1,0:T(8,128)(2,1)S(1)}, u32[]{:S(2)}, u32[]{:S(2)}) collective-permute-start(bf16[384,128]{1,0:T(8,128)(2,1)S(1)} %get-tuple-element.266), channel_id=1, source_target_pairs={{0,3},{1,2},{2,1},{3,0},{4,7},{5,6},{6,5},{7,4},{8,11},{9,10},{10,... | collective-permute-start | bytes 294920 | tf_op jit(solution)/shard_map/ppermute | solution.py:374
  163.3 1.6 collective-permute-start.22
  167.8 2.4 collective-permute-start.24
  168.2 19.6 %collective-permute-start.23 = (bf16[384,1024]{1,0:T(8,128)(2,1)S(1)}, bf16[384,1024]{1,0:T(8,128)(2,1)S(1)}, u32[]{:S(2)}, u32[]{:S(2)}) collective-permute-start(bf16[384,1024]{1,0:T(8,128)(2,1)S(1)} %add_convert_fusion.1), channel_id=1, source_target_pairs={{0,8},{4,12},{8,0},{12,4},{1,9},{5,13},{9,1},{13,5},{2,10},{6,14},... | collective-permute-start | bytes 2359304 | tf_op jit(solution)/shard_map/ppermute | solution.py:374
  187.8 2.3 collective-permute-start.25
  206.6 2.6 collective-permute-start.26
  208.0 17.0 %collective-permute-start.28 = (bf16[384,1024]{1,0:T(8,128)(2,1)S(1)}, bf16[384,1024]{1,0:T(8,128)(2,1)S(1)}, u32[]{:S(2)}, u32[]{:S(2)}) collective-permute-start(bf16[384,1024]{1,0:T(8,128)(2,1)S(1)} %slice.208), channel_id=1, source_target_pairs={{0,4},{4,0},{8,12},{12,8},{1,5},{5,1},{9,13},{13,9},{2,6},{6,2},{1... | collective-permute-start | bytes 2359304 | tf_op jit(solution)/shard_map/ppermute | solution.py:374
  211.5 19.8 %collective-permute-start.27 = (bf16[384,1024]{1,0:T(8,128)(2,1)}, bf16[384,1024]{1,0:T(8,128)(2,1)S(1)}, u32[]{:S(2)}, u32[]{:S(2)}) collective-permute-start(bf16[384,1024]{1,0:T(8,128)(2,1)} %add_convert_fusion), channel_id=1, source_target_pairs={{0,8},{4,12},{8,0},{12,4},{1,9},{5,13},{9,1},{13,5},{2,10},{6,14},... | collective-permute-start | bytes 2359304 | tf_op jit(solution)/shard_map/ppermute | solution.py:374
  237.6 24.8 %collective-permute-start.30 = (bf16[2,384,1024]{2,1,0:T(8,128)(2,1)}, bf16[2,384,1024]{2,1,0:T(8,128)(2,1)}, u32[]{:S(2)}, u32[]{:S(2)}) collective-permute-start(bf16[2,384,1024]{2,1,0:T(8,128)(2,1)} %pad_maximum_fusion.4), channel_id=1, source_target_pairs={{0,4},{4,0},{8,12},{12,8},{1,5},{5,1},{9,13},{13,9},{2,6},{6,2},{1... | collective-permute-start | bytes 4718600 | tf_op jit(solution)/shard_map/ppermute | solution.py:374
  241.1 13.9 %collective-permute-start.29 = (bf16[4,2,2,32,1024]{4,3,0,2,1:T(8,128)(2,1)}, bf16[4,2,2,32,1024]{4,3,0,2,1:T(8,128)(2,1)}, u32[]{:S(2)}, u32[]{:S(2)}) collective-permute-start(bf16[4,2,2,32,1024]{4,3,0,2,1:T(8,128)(2,1)} %bitcast.162), channel_id=1, source_target_pairs={{0,4},{4,0},{8,12},{12,8},{1,5},{5,1},{9,13},{13,9},{2,6},{6,2},{1... | collective-permute-start | bytes 3145736 | tf_op jit(solution)/shard_map/ppermute | solution.py:374
  250.2 8.0 %collective-permute-start.31 = (bf16[384,128]{1,0:T(8,128)(2,1)S(1)}, bf16[384,128]{1,0:T(8,128)(2,1)S(1)}, u32[]{:S(2)}, u32[]{:S(2)}) collective-permute-start(bf16[384,128]{1,0:T(8,128)(2,1)S(1)} %get-tuple-element.262), channel_id=1, source_target_pairs={{0,1},{1,0},{2,3},{3,2},{4,5},{5,4},{6,7},{7,6},{8,9},{9,8},{10,11... | collective-permute-start | bytes 294920 | tf_op jit(solution)/shard_map/ppermute | solution.py:374
  252.5 9.9 %collective-permute-start.32 = (bf16[384,128]{1,0:T(8,128)(2,1)S(1)}, bf16[384,128]{1,0:T(8,128)(2,1)S(1)}, u32[]{:S(2)}, u32[]{:S(2)}) collective-permute-start(bf16[384,128]{1,0:T(8,128)(2,1)S(1)} %get-tuple-element.261), channel_id=1, source_target_pairs={{0,2},{1,3},{2,0},{3,1},{4,6},{5,7},{6,4},{7,5},{8,10},{9,11},{10,... | collective-permute-start | bytes 294920 | tf_op jit(solution)/shard_map/ppermute | solution.py:374
  252.5 9.9 %collective-permute-start.33 = (bf16[384,128]{1,0:T(8,128)(2,1)S(1)}, bf16[384,128]{1,0:T(8,128)(2,1)S(1)}, u32[]{:S(2)}, u32[]{:S(2)}) collective-permute-start(bf16[384,128]{1,0:T(8,128)(2,1)S(1)} %get-tuple-element.260), channel_id=1, source_target_pairs={{0,3},{1,2},{2,1},{3,0},{4,7},{5,6},{6,5},{7,4},{8,11},{9,10},{10,... | collective-permute-start | bytes 294920 | tf_op jit(solution)/shard_map/ppermute | solution.py:374
  254.9 175.6 %reduce-scatter.3.cloned.1.call-start = ((), (), s32[]{:S(2)}) async-start(), calls=%async_computation.3 | async-start | bytes 3932160 | tf_op jit(solution)/shard_map/reduce_scatter | solution.py:915
  255.0 39.7 %collective-permute-start.36 = (bf16[384,128]{1,0:T(8,128)(2,1)S(1)}, bf16[384,128]{1,0:T(8,128)(2,1)S(1)}, u32[]{:S(2)}, u32[]{:S(2)}) collective-permute-start(bf16[384,128]{1,0:T(8,128)(2,1)S(1)} %get-tuple-element.258), channel_id=1, source_target_pairs={{0,1},{1,0},{2,3},{3,2},{4,5},{5,4},{6,7},{7,6},{8,9},{9,8},{10,11... | collective-permute-start | bytes 294920 | tf_op jit(solution)/shard_map/ppermute | solution.py:374
  258.2 36.5 %collective-permute-start.37 = (bf16[384,128]{1,0:T(8,128)(2,1)S(1)}, bf16[384,128]{1,0:T(8,128)(2,1)S(1)}, u32[]{:S(2)}, u32[]{:S(2)}) collective-permute-start(bf16[384,128]{1,0:T(8,128)(2,1)S(1)} %get-tuple-element.257), channel_id=1, source_target_pairs={{0,2},{1,3},{2,0},{3,1},{4,6},{5,7},{6,4},{7,5},{8,10},{9,11},{10,... | collective-permute-start | bytes 294920 | tf_op jit(solution)/shard_map/ppermute | solution.py:374
  262.4 32.4 %collective-permute-start.38 = (bf16[384,128]{1,0:T(8,128)(2,1)S(1)}, bf16[384,128]{1,0:T(8,128)(2,1)S(1)}, u32[]{:S(2)}, u32[]{:S(2)}) collective-permute-start(bf16[384,128]{1,0:T(8,128)(2,1)S(1)} %get-tuple-element.256), channel_id=1, source_target_pairs={{0,3},{1,2},{2,1},{3,0},{4,7},{5,6},{6,5},{7,4},{8,11},{9,10},{10,... | collective-permute-start | bytes 294920 | tf_op jit(solution)/shard_map/ppermute | solution.py:374
  263.9 30.8 %collective-permute-start.35 = (bf16[384,1024]{1,0:T(8,128)(2,1)S(1)}, bf16[384,1024]{1,0:T(8,128)(2,1)S(1)}, u32[]{:S(2)}, u32[]{:S(2)}) collective-permute-start(bf16[384,1024]{1,0:T(8,128)(2,1)S(1)} %fusion.19), channel_id=1, source_target_pairs={{0,8},{4,12},{8,0},{12,4},{1,9},{5,13},{9,1},{13,5},{2,10},{6,14},... | collective-permute-start | bytes 2359304 | tf_op jit(solution)/shard_map/ppermute | solution.py:374
  265.3 29.2 %collective-permute-start.34 = (bf16[4,2,32,1024]{3,2,0,1:T(8,128)(2,1)S(1)}, bf16[4,2,32,1024]{3,2,0,1:T(8,128)(2,1)S(1)}, u32[]{:S(2)}, u32[]{:S(2)}) collective-permute-start(bf16[4,2,32,1024]{3,2,0,1:T(8,128)(2,1)S(1)} %dynamic-slice_bitcast_fusion.1), channel_id=1, source_target_pairs={{0,8},{4,12},{8,0},{12,4},{1,9},{5,13},{9,1},{13,5},{2,10},{6,14},... | collective-permute-start | bytes 1572872 | tf_op jit(solution)/shard_map/ppermute | solution.py:374
  294.7 22.0 %copy-start.31 = (bf16[384,1024]{1,0:T(8,128)(2,1)}, bf16[384,1024]{1,0:T(8,128)(2,1)S(1)}, u32[]{:S(2)}) copy-start(bf16[384,1024]{1,0:T(8,128)(2,1)S(1)} %collective-permute-done.35) | copy-start | bytes 2359300
  294.8 28.3 %collective-permute-start.39 = (bf16[4,1,32,1024]{3,2,0,1:T(8,128)(2,1)S(1)}, bf16[4,1,32,1024]{3,2,0,1:T(8,128)(2,1)S(1)}, u32[]{:S(2)}, u32[]{:S(2)}) collective-permute-start(bf16[4,1,32,1024]{3,2,0,1:T(8,128)(2,1)S(1)} %constant_dynamic-slice_fusion.7), channel_id=1, source_target_pairs={{0,16},{16,0},{1,17},{17,1},{2,18},{18,2},{3,19},{19,3},{4,20},{20... | collective-permute-start | bytes 786440 | tf_op jit(solution)/shard_map/ppermute | solution.py:374
  297.3 20.7 %copy-start.59 = (s32[128]{0:T(128)S(1)}, s32[128]{0:T(128)}, u32[]{:S(2)}) copy-start(s32[128]{0:T(128)} %param.17) | copy-start | bytes 1540
  297.3 21.1 %copy-start.56 = (f32[1024]{0:T(1024)S(1)}, f32[1024]{0:T(1024)}, u32[]{:S(2)}) copy-start(f32[1024]{0:T(1024)} %param.28) | copy-start | bytes 12292
  332.0 23.3 %collective-permute-start.42 = (bf16[2,32,1024]{2,1,0:T(8,128)(2,1)S(1)}, bf16[2,32,1024]{2,1,0:T(8,128)(2,1)S(1)}, u32[]{:S(2)}, u32[]{:S(2)}) collective-permute-start(bf16[2,32,1024]{2,1,0:T(8,128)(2,1)S(1)} %slice.236), channel_id=1, source_target_pairs={{0,2},{1,3},{2,0},{3,1},{4,6},{5,7},{6,4},{7,5},{8,10},{9,11},{10,... | collective-permute-start | bytes 393224 | tf_op jit(solution)/shard_map/ppermute | solution.py:374
  341.6 6.6 %collective-permute-start.41 = (f32[10,1024]{1,0:T(8,128)S(1)}, f32[10,1024]{1,0:T(8,128)S(1)}, u32[]{:S(2)}, u32[]{:S(2)}) collective-permute-start(f32[10,1024]{1,0:T(8,128)S(1)} %reshape.429), channel_id=1, source_target_pairs={{0,4},{4,0},{8,12},{12,8},{1,5},{5,1},{9,13},{13,9},{2,6},{6,2},{1... | collective-permute-start | bytes 122888 | tf_op jit(solution)/shard_map/ppermute | solution.py:374
  345.3 10.0 %collective-permute-start.40 = (bf16[512,768]{0,1:T(8,128)(2,1)S(1)}, bf16[512,768]{0,1:T(8,128)(2,1)S(1)}, u32[]{:S(2)}, u32[]{:S(2)}) collective-permute-start(bf16[512,768]{0,1:T(8,128)(2,1)S(1)} %pad_maximum_fusion.6), channel_id=1, source_target_pairs={{0,4},{4,0},{8,12},{12,8},{1,5},{5,1},{9,13},{13,9},{2,6},{6,2},{1... | collective-permute-start | bytes 2359304 | tf_op jit(solution)/shard_map/ppermute | solution.py:374
  360.4 12.3 %collective-permute-start.43 = (bf16[2,128,768]{2,1,0:T(8,128)(2,1)S(1)}, bf16[2,128,768]{2,1,0:T(8,128)(2,1)}, u32[]{:S(2)}, u32[]{:S(2)}) collective-permute-start(bf16[2,128,768]{2,1,0:T(8,128)(2,1)S(1)} %bitcast.190), channel_id=1, source_target_pairs={{0,8},{4,12},{8,0},{12,4},{1,9},{5,13},{9,1},{13,5},{2,10},{6,14},... | collective-permute-start | bytes 1179656 | tf_op jit(solution)/shard_map/ppermute | solution.py:374
  362.0 10.8 %collective-permute-start.45 = (bf16[1,32,1024]{2,1,0:T(8,128)(2,1)S(1)}, bf16[1,32,1024]{2,1,0:T(8,128)(2,1)S(1)}, u32[]{:S(2)}, u32[]{:S(2)}) collective-permute-start(bf16[1,32,1024]{2,1,0:T(8,128)(2,1)S(1)} %slice.238), channel_id=1, source_target_pairs={{0,1},{1,0},{2,3},{3,2},{4,5},{5,4},{6,7},{7,6},{8,9},{9,8},{10,11... | collective-permute-start | bytes 196616 | tf_op jit(solution)/shard_map/ppermute | solution.py:374
  362.9 12.6 %collective-permute-start.46 = (bf16[1,256,1024]{2,1,0:T(8,128)(2,1)S(1)}, bf16[1,256,1024]{2,1,0:T(8,128)(2,1)}, u32[]{:S(2)}, u32[]{:S(2)}) collective-permute-start(bf16[1,256,1024]{2,1,0:T(8,128)(2,1)S(1)} %copy-done.34), channel_id=1, source_target_pairs={{0,16},{16,0},{1,17},{17,1},{2,18},{18,2},{3,19},{19,3},{4,20},{20... | collective-permute-start | bytes 1572872 | tf_op jit(solution)/shard_map/ppermute | solution.py:374
  364.1 8.6 %collective-permute-start.44 = (f32[10,1024]{1,0:T(8,128)S(1)}, f32[10,1024]{1,0:T(8,128)S(1)}, u32[]{:S(2)}, u32[]{:S(2)}) collective-permute-start(f32[10,1024]{1,0:T(8,128)S(1)} %add.302), channel_id=1, source_target_pairs={{0,8},{4,12},{8,0},{12,4},{1,9},{5,13},{9,1},{13,5},{2,10},{6,14},... | collective-permute-start | bytes 122888 | tf_op jit(solution)/shard_map/ppermute | solution.py:374
  377.0 24.9 %copy-start.11 = (bf16[2,256,1024]{2,1,0:T(8,128)(2,1)}, bf16[2,256,1024]{2,1,0:T(8,128)(2,1)S(1)}, u32[]{:S(2)}) copy-start(bf16[2,256,1024]{2,1,0:T(8,128)(2,1)S(1)} %maximum_select_fusion.7) | copy-start | bytes 3145732
  377.0 6.5 %collective-permute-start.47 = (bf16[1,128,768]{2,1,0:T(8,128)(2,1)S(1)}, bf16[1,128,768]{2,1,0:T(8,128)(2,1)S(1)}, u32[]{:S(2)}, u32[]{:S(2)}) collective-permute-start(bf16[1,128,768]{2,1,0:T(8,128)(2,1)S(1)} %constant_dynamic-slice_fusion.2), channel_id=1, source_target_pairs={{0,16},{16,0},{1,17},{17,1},{2,18},{18,2},{3,19},{19,3},{4,20},{20... | collective-permute-start | bytes 589832 | tf_op jit(solution)/shard_map/ppermute | solution.py:374
  378.8 4.7 %collective-permute-start.48 = (f32[10,1024]{1,0:T(8,128)S(1)}, f32[10,1024]{1,0:T(8,128)S(1)}, u32[]{:S(2)}, u32[]{:S(2)}) collective-permute-start(f32[10,1024]{1,0:T(8,128)S(1)} %add.305), channel_id=1, source_target_pairs={{0,16},{16,0},{1,17},{17,1},{2,18},{18,2},{3,19},{19,3},{4,20},{20... | collective-permute-start | bytes 122888 | tf_op jit(solution)/shard_map/ppermute | solution.py:374
  379.1 22.8 %collective-permute-start.49 = (bf16[2,256,1024]{2,1,0:T(8,128)(2,1)S(1)}, bf16[2,256,1024]{2,1,0:T(8,128)(2,1)S(1)}, u32[]{:S(2)}, u32[]{:S(2)}) collective-permute-start(bf16[2,256,1024]{2,1,0:T(8,128)(2,1)S(1)} %maximum_select_fusion.7), channel_id=1, source_target_pairs={{0,8},{4,12},{8,0},{12,4},{1,9},{5,13},{9,1},{13,5},{2,10},{6,14},... | collective-permute-start | bytes 3145736 | tf_op jit(solution)/shard_map/ppermute | solution.py:374
  403.8 9.2 %collective-permute-start.52 = (bf16[2,2,256,1024]{3,2,1,0:T(8,128)(2,1)S(1)}, bf16[2,2,256,1024]{3,2,1,0:T(8,128)(2,1)S(1)}, u32[]{:S(2)}, u32[]{:S(2)}) collective-permute-start(bf16[2,2,256,1024]{3,2,1,0:T(8,128)(2,1)S(1)} %maximum_select_fusion.1), channel_id=1, source_target_pairs={{0,4},{4,0},{8,12},{12,8},{1,5},{5,1},{9,13},{13,9},{2,6},{6,2},{1... | collective-permute-start | bytes 6291464 | tf_op jit(solution)/shard_map/ppermute | solution.py:374
  403.8 9.0 %collective-permute-start.50 = (bf16[1,512,256]{2,1,0:T(8,128)(2,1)S(1)}, bf16[1,512,256]{2,1,0:T(8,128)(2,1)S(1)}, u32[]{:S(2)}, u32[]{:S(2)}) collective-permute-start(bf16[1,512,256]{2,1,0:T(8,128)(2,1)S(1)} %bitcast.188), channel_id=1, source_target_pairs={{0,16},{16,0},{1,17},{17,1},{2,18},{18,2},{3,19},{19,3},{4,20},{20... | collective-permute-start | bytes 786440 | tf_op jit(solution)/shard_map/ppermute | solution.py:374
  405.6 7.3 %collective-permute-start.51 = (f32[10,1024]{1,0:T(8,128)S(1)}, f32[10,1024]{1,0:T(8,128)S(1)}, u32[]{:S(2)}, u32[]{:S(2)}) collective-permute-start(f32[10,1024]{1,0:T(8,128)S(1)} %add.308), channel_id=1, source_target_pairs={{0,1},{1,0},{2,3},{3,2},{4,5},{5,4},{6,7},{7,6},{8,9},{9,8},{10,11... | collective-permute-start | bytes 122888 | tf_op jit(solution)/shard_map/ppermute | solution.py:374
  415.4 14.1 %collective-permute-start.53 = (bf16[2,512,256]{2,1,0:T(8,128)(2,1)S(1)}, bf16[2,512,256]{2,1,0:T(8,128)(2,1)S(1)}, u32[]{:S(2)}, u32[]{:S(2)}) collective-permute-start(bf16[2,512,256]{2,1,0:T(8,128)(2,1)S(1)} %maximum_select_fusion.10), channel_id=1, source_target_pairs={{0,8},{4,12},{8,0},{12,4},{1,9},{5,13},{9,1},{13,5},{2,10},{6,14},... | collective-permute-start | bytes 1572872 | tf_op jit(solution)/shard_map/ppermute | solution.py:374
  416.8 9.2 %collective-permute-start.54 = (f32[10,1024]{1,0:T(8,128)S(1)}, f32[10,1024]{1,0:T(8,128)S(1)}, u32[]{:S(2)}, u32[]{:S(2)}) collective-permute-start(f32[10,1024]{1,0:T(8,128)S(1)} %add.309), channel_id=1, source_target_pairs={{0,2},{1,3},{2,0},{3,1},{4,6},{5,7},{6,4},{7,5},{8,10},{9,11},{10,... | collective-permute-start | bytes 122888 | tf_op jit(solution)/shard_map/ppermute | solution.py:374
  430.6 3.6 collective-permute-start.55
  (57 other events, 275.9 us)
Sparse Core Ops, SparseCore 0:
  11.6 80.2 all-gather.1
  255.0 104.1 reduce-scatter.4
  365.3 61.4 reduce-scatter.2
